TPU v7x, 256 devices: a whole 4x4x8 slice. The times are simulated.
256 devices in a mesh: row: 16 (over x_hi, y, core), col: 16 (over z, x_lo).
Axes of the slice: x: 4 (x_hi: 2, x_lo: 2; x = x_hi * 2 + x_lo), y: 4, z: 8, core: 2. Of those that a mesh axis runs over, the one named last changes fastest.
Arguments:
- matrix: float32 [32768, 4096], P('row', 'col')
- signs: int32 [32768], P('row'), may hold values from -1 to 1, as said below
- picked: int32 [16384], P('row'), may hold values from 0 to 2047, as said below
Outputs:
- gram: float32 [4096, 4096], P('row', 'col')
Inputs may be any that keep to these rules, and one draw needn't show every extreme that they name: `signs`: each entry is -1 or 1. `picked`: stratified sampling with replacement, independently in each row block: entry k of a row block's list (k counted from the block's first entry) lies in rows s * (128) to (s + 1) * 128 - 1 with s = k // 64, uniformly there; entry 0 of the whole array is 0 and its last entry is 2047.
All inputs are finite; a program needn't handle non-finite values.
Results may differ from a plain program's by a relative error of at most 0.000059.
Values sent between devices are 32-bit elements; how exact they have to be, the bound alone decides.
No kernel may reach another device: no remote copies, remote signals or barrier semaphores. Data moves between devices by JAX's collectives and lax.ppermute only.
A program may use at most 64 MiB of HBM per device.

v0:
```python
import jax
import jax.numpy as jnp
from jax import lax
from jax.sharding import PartitionSpec as P


def swapped(block, axis, stride):
    count = lax.axis_size(axis)
    route = []
    for low in range(count):
        high = low | 1 << stride
        if high != low and high < count:
            route += [(low, high), (high, low)]
    return lax.ppermute(block, axis, route)


def parity_sign(values, width):
    count = jnp.zeros(values.shape, jnp.int32)
    for bit in range(max(width.bit_length(), 1)):
        count = count + jnp.bitwise_and(jnp.right_shift(values, bit), 1)
    return (1 - 2 * (count % 2)).astype(jnp.float32)


def sylvester(size):
    idx = jnp.arange(size, dtype=jnp.int32)
    return parity_sign(jnp.bitwise_and(idx[:, None], idx[None, :]), size)


def shards(matrix, signs, picked):
    hp = lax.Precision.HIGHEST
    rows_here, cols_here = matrix.shape
    samp_here = picked.shape[0]
    row_count = lax.axis_size("row")
    inner = min(rows_here, 128)
    outer = rows_here // inner
    signed = matrix * signs.astype(jnp.float32)[:, None]
    blocks = signed.reshape(outer, inner, cols_here)
    blocks = jnp.einsum("tb,abc->atc", sylvester(inner), blocks, precision=hp)
    blocks = jnp.einsum("sa,atc->stc", sylvester(outer), blocks, precision=hp)
    local_mix = blocks.reshape(rows_here, cols_here)
    scale = 1.0 / (samp_here * row_count) ** 0.5
    mixed = local_mix
    mine = lax.axis_index("row")
    for bit in range(row_count.bit_length() - 1):
        partner = swapped(mixed, "row", bit)
        upper = jnp.bitwise_and(jnp.right_shift(mine, bit), 1)
        mixed = jnp.where(upper == 0, mixed + partner, partner - mixed)
    sketch = jnp.take(mixed, picked, axis=0) * scale
    full_sketch = lax.all_gather(sketch, "col", axis=1, tiled=True)
    return lax.psum_scatter(
        lax.dot_general(
            full_sketch,
            sketch,
            (((0,), (0,)), ((), ())),
            precision=hp,
            preferred_element_type=jnp.float32,
        ),
        "row",
        scatter_dimension=0,
        tiled=True,
    )


def solution(mesh):
    in_specs = (P("row", "col"), P("row"), P("row"))
    out_specs = P("row", "col")
    return jax.shard_map(shards, mesh=mesh, in_specs=in_specs, out_specs=out_specs, check_vma=False)
```

profile of v0, /device:TPU:6, one launch (start us, length us, event | category | flops | bytes accessed | tf_op | source)
XLA Modules:
  0.0 667.7 jit_solution(11536179864067072099)
XLA Ops:
  6.5 0.0 all-gather.2.cloned.1.call-start
  6.5 0.7 convert_element_type.10
  7.2 1.9 broadcast_multiply_fusion
  9.2 3.6 fusion.7
  12.8 2.1 copy.5
  14.8 3.5 fusion
  18.3 1.2 copy.4
  19.5 0.0 copy-start.3
  19.5 0.1 collective-permute-start
  19.6 1.2 copy-done.3
  20.8 3.1 collective-permute-done
  23.9 2.5 subtract_select_fusion.3
  26.4 0.0 copy-start.2
  26.4 1.7 collective-permute-start.1
  28.1 0.0 copy-done.2
  28.1 46.2 %collective-permute-done.1 = f32[2048,256]{1,0:T(8,128)} collective-permute-done((f32[2048,256]{1,0:T(8,128)S(1)}, f32[2048,256]{1,0:T(8,128)}, u32[]{:S(2)}, u32[]{:S(2)}) %collective-permute-start.1) | collective-permute-done | bytes 2097184 | tf_op jit(solution)/shard_map/ppermute | solution.py:14
  74.3 2.5 subtract_select_fusion.2
  76.8 0.0 copy-start.1
  76.8 3.3 collective-permute-start.2
  80.1 0.0 copy-done.1
  80.1 0.0 copy-start.4
  80.1 45.3 %collective-permute-done.2 = f32[2048,256]{1,0:T(8,128)} collective-permute-done((f32[2048,256]{1,0:T(8,128)S(1)}, f32[2048,256]{1,0:T(8,128)}, u32[]{:S(2)}, u32[]{:S(2)}) %collective-permute-start.2) | collective-permute-done | bytes 2097184 | tf_op jit(solution)/shard_map/ppermute | solution.py:14
  125.3 2.5 subtract_select_fusion.1
  127.8 0.0 copy-start
  127.8 1.5 collective-permute-start.3
  129.3 0.0 copy-done.4
  129.3 0.0 copy-done
  129.3 46.1 %collective-permute-done.3 = f32[2048,256]{1,0:T(8,128)} collective-permute-done((f32[2048,256]{1,0:T(8,128)S(1)}, f32[2048,256]{1,0:T(8,128)}, u32[]{:S(2)}, u32[]{:S(2)}) %collective-permute-start.3) | collective-permute-done | bytes 2097184 | tf_op jit(solution)/shard_map/ppermute | solution.py:14
  175.4 2.5 subtract_select_fusion
  177.9 3.5 gather_fusion
  181.4 1.2 select_multiply_fusion
  182.6 0.0 all-gather.2.cloned.1.call-update
  182.6 0.2 reduce-scatter.2.cloned.1.call-start
  182.8 353.2 %all-gather.2.cloned.1.call-done = f32[1024,4096]{1,0:T(8,128)} async-done(((f32[1024,256]{1,0:T(8,128)}), f32[1024,4096]{1,0:T(8,128)}) %all-gather.2.cloned.1.call-update) | async-done | bytes 16777232 | tf_op jit(solution)/shard_map/all_gather | solution.py:49
  536.0 30.2 %fusion.48 = f32[4096,256]{1,0:T(8,128)} fusion(f32[1024,4096]{1,0:T(8,128)} %all-gather.2.cloned.1.call-done, f32[1024,256]{1,0:T(8,128)} %select_multiply_fusion), kind=kOutput, calls=%fused_computation.61 | convolution fusion | flops 12884901888 | bytes 22020096 | tf_op jit(solution)/shard_map/dot_general | solution.py:51
  566.3 0.0 reduce-scatter.2.cloned.1.call-update
  566.3 94.6 %reduce-scatter.2.cloned.1.call-done = f32[256,256]{1,0:T(8,128)} async-done(((f32[4096,256]{1,0:T(8,128)}), f32[256,256]{1,0:T(8,128)}) %reduce-scatter.2.cloned.1.call-update) | async-done | bytes 262160 | tf_op jit(solution)/shard_map/reduce_scatter | solution.py:50
  (2 shorter events, 0.0 us)
Async XLA Ops:
  6.5 529.5 %all-gather.2.cloned.1.call-start = ((), (), s32[]{:S(2)}) async-start(), calls=%async_computation.1 | async-start | bytes 17825792 | tf_op jit(solution)/shard_map/all_gather | solution.py:49
  19.5 1.3 copy-start.3
  19.5 4.4 collective-permute-start
  26.4 1.7 copy-start.2
  26.4 47.9 %collective-permute-start.1 = (f32[2048,256]{1,0:T(8,128)S(1)}, f32[2048,256]{1,0:T(8,128)}, u32[]{:S(2)}, u32[]{:S(2)}) collective-permute-start(f32[2048,256]{1,0:T(8,128)S(1)} %subtract_select_fusion.3), channel_id=1, source_target_pairs={{0,32},{32,0},{16,48},{48,16},{64,96},{96,64},{80,112},{112,80},{1... | collective-permute-start | bytes 6291464 | tf_op jit(solution)/shard_map/ppermute | solution.py:14
  76.8 3.3 copy-start.1
  76.8 48.5 %collective-permute-start.2 = (f32[2048,256]{1,0:T(8,128)S(1)}, f32[2048,256]{1,0:T(8,128)}, u32[]{:S(2)}, u32[]{:S(2)}) collective-permute-start(f32[2048,256]{1,0:T(8,128)S(1)} %subtract_select_fusion.2), channel_id=1, source_target_pairs={{0,64},{64,0},{16,80},{80,16},{32,96},{96,32},{48,112},{112,48},{1... | collective-permute-start | bytes 6291464 | tf_op jit(solution)/shard_map/ppermute | solution.py:14
  80.1 49.3 %copy-start.4 = (s32[1024]{0:T(1024)S(1)}, s32[1024]{0:T(1024)}, u32[]{:S(2)}) copy-start(s32[1024]{0:T(1024)} %param.5) | copy-start | bytes 12292
  127.8 1.5 copy-start
  127.8 47.6 %collective-permute-start.3 = (f32[2048,256]{1,0:T(8,128)S(1)}, f32[2048,256]{1,0:T(8,128)}, u32[]{:S(2)}, u32[]{:S(2)}) collective-permute-start(f32[2048,256]{1,0:T(8,128)S(1)} %subtract_select_fusion.1), channel_id=1, source_target_pairs={{0,128},{128,0},{16,144},{144,16},{32,160},{160,32},{48,176},{176,... | collective-permute-start | bytes 6291464 | tf_op jit(solution)/shard_map/ppermute | solution.py:14
  182.6 478.3 %reduce-scatter.2.cloned.1.call-start = ((), (), s32[]{:S(2)}) async-start(), calls=%async_computation.2 | async-start | bytes 4456448 | tf_op jit(solution)/shard_map/reduce_scatter | solution.py:50
Sparse Core Ops, SparseCore 0:
  182.7 353.2 all-gather.1
  566.4 94.4 reduce-scatter.1
where the time goes:
time: 669 us; the launch traced here: 668 us
  waiting for transfers between devices  588 us (88%)
  matrix products  37.3 us (6%)
  other arithmetic  13.8 us (2%)
  between operations  13.5 us (2%)
  local copies, waits for them, and re-layouts  7.95 us (1%)
  starting transfers between devices  6.76 us (1%)
    all_gather x1, waiting for transfers between devices, shards(): full_sketch = lax.all_gather(sketch, 'col', axis=1, tiled=True)  353 us
    ppermute x4, waiting for transfers between devices, swapped(): return lax.ppermute(block, axis, route)  141 us
    reduce_scatter x1, waiting for transfers between devices, shards(): lax.psum_scatter(lax.dot_general(full_sketch, sketch, (((0,), (0,)), ((),...  94.6 us
    dot_general x1, matrix products, shards(): lax.dot_general(full_sketch, sketch, (((0,), (0,)), ((), ())), precision=...  30.2 us
  transfers between devices with their start and end apart: 6, of which 6 were waited for; matrix products, arithmetic and copies ran while one was open for 0% of the time, Pallas kernels for 0%

commit v1 on v0

v1 whole, which is shorter than its diff:
```python
import itertools

import jax
import jax.numpy as jnp
import numpy as np
from jax import lax
from jax.experimental import pallas as pl
from jax.experimental.pallas import tpu as pltpu
from jax.sharding import Mesh
from jax.sharding import PartitionSpec as P

NAMES = ("xh", "y", "core", "z", "xl")
SIZES = (2, 4, 2, 8, 2)
ROW = ("xh", "y", "core")
COL = ("z", "xl")
CHIPS = ("xh", "y")
SLICES = 16
SPAN = 128
F32 = jnp.float32
BF16 = jnp.bfloat16


def permute(block, route):
    pairs = []
    for here in itertools.product(*[range(s) for s in SIZES]):
        there = route(*here)
        if there is None:
            continue
        there = tuple(v % s for v, s in zip(there, SIZES))
        pairs.append((int(np.ravel_multi_index(here, SIZES)), int(np.ravel_multi_index(there, SIZES))))
    return lax.ppermute(block, NAMES, pairs)


def hadamard(vals):
    step = 1
    vals = list(vals)
    while step < len(vals):
        for i in range(len(vals)):
            if not i & step:
                a, b = vals[i], vals[i | step]
                vals[i], vals[i | step] = a + b, a - b
        step *= 2
    return vals


def mix_kernel(signs_ref, picked_ref, x_ref, o_ref, sign_ref):
    sign_ref[...] = signs_ref[...].astype(F32).T

    def chunk(i, carry):
        rows = pl.ds(pl.multiple_of(i * 8, 8), 8)
        sign = sign_ref[rows, :]
        vals = hadamard([x_ref[a, rows, :] * sign[:, a : a + 1] for a in range(SLICES)])
        for s in range(SLICES):
            o_ref[s, rows, :] = vals[s]
        return carry

    lax.fori_loop(0, SPAN // 8, chunk, 0)
    for s in range(SLICES):
        row = picked_ref[s // 2 : s // 2 + 1, :].astype(F32)
        o_ref[s, SPAN:, :] = jnp.broadcast_to(row, (8, 128))


def mix_slices(matrix, signs, picked):
    rows, cols = matrix.shape
    return pl.pallas_call(
        mix_kernel,
        out_shape=jax.ShapeDtypeStruct((SLICES, SPAN + 8, cols), F32),
        grid=(cols // 128,),
        in_specs=[
            pl.BlockSpec((SLICES, SPAN), lambda j: (0, 0)),
            pl.BlockSpec((8, 128), lambda j: (0, 0)),
            pl.BlockSpec((SLICES, SPAN, 128), lambda j: (0, 0, j)),
        ],
        out_specs=pl.BlockSpec((SLICES, SPAN + 8, 128), lambda j: (0, 0, j)),
        scratch_shapes=[pltpu.VMEM((SPAN, SLICES), F32)],
        name="mix_slices",
    )(signs.reshape(SLICES, SPAN), picked.reshape(8, 128), matrix.reshape(SLICES, SPAN, cols))


def sample_kernel(scale, half_ref, y_ref, o_ref, mixed_ref, where_ref):
    picks = jnp.concatenate([y_ref[q, SPAN : SPAN + 1, :128] for q in range(SLICES)], axis=0)
    where_ref[...] = picks.T.astype(jnp.int32)

    def chunk(i, carry):
        rows = pl.ds(pl.multiple_of(i * 8, 8), 8)
        vals = hadamard([y_ref[p, rows, :] for p in range(SLICES)])
        for q in range(SLICES):
            mixed_ref[q, rows, :] = vals[q] * scale
        return carry

    lax.fori_loop(0, SPAN // 8, chunk, 0)
    mine = pl.ds(pl.multiple_of(half_ref[0] * 64, 64), 64)
    lane = lax.broadcasted_iota(jnp.int32, (64, SPAN), 1)
    for q in range(SLICES):
        both = where_ref[mine, q : q + 1] & lane
        both = both ^ (both >> 4)
        both = both ^ (both >> 2)
        both = both ^ (both >> 1)
        signs = (1 - 2 * (both & 1)).astype(F32).astype(BF16)
        vals = mixed_ref[q]
        high = vals.astype(BF16)
        rest = vals - high.astype(F32)
        mid = rest.astype(BF16)
        low = (rest - mid.astype(F32)).astype(BF16)
        out = jnp.dot(signs, low, preferred_element_type=F32)
        out += jnp.dot(signs, mid, preferred_element_type=F32)
        out += jnp.dot(signs, high, preferred_element_type=F32)
        o_ref[q * 64 : (q + 1) * 64, :] = out


def sample(slices, scale):
    cols = slices.shape[2]
    half = lax.axis_index("core").reshape(1)
    return pl.pallas_call(
        lambda *refs: sample_kernel(scale, *refs),
        out_shape=jax.ShapeDtypeStruct((SLICES * 64, cols), F32),
        in_specs=[pl.BlockSpec(memory_space=pltpu.SMEM), pl.BlockSpec(memory_space=pltpu.VMEM)],
        out_specs=pl.BlockSpec(memory_space=pltpu.VMEM),
        scratch_shapes=[pltpu.VMEM((SLICES, SPAN, cols), F32), pltpu.VMEM((SPAN, SLICES), jnp.int32)],
        name="sample",
    )(half, slices)


def pairs_of(z):
    low = z < 4
    return [
        ((1, 0), (0, 0)),
        ((1, 0), (0, 1)),
        ((1, 0), (-1, 0)),
        ((2, 0), (0, 1)) if low else ((2, 1), (0, 0)),
        ((1, 0), (-2, 0)),
        ((2, 0), (-1, 1)) if low else ((2, 1), (-1, 0)),
        ((2, 0), (-2, 0)) if low else ((2, 1), (-2, 0)),
    ]


def home(xh, y, core, z, xl):
    chip = xh * 4 + y
    if chip == 7:
        row, col, mirror = (z, xl ^ core), (z, xl), False
    else:
        (rz, rx), (cz, cx) = pairs_of(z)[chip]
        row, col, mirror = ((z + rz) % 8, xl ^ rx), ((z + cz) % 8, xl ^ cx), core == 1
        if mirror:
            row, col = col, row
    return (row[0] // 4, row[0] % 4, row[1], col[0], col[1]), mirror


def mirrored():
    table = np.zeros(SIZES, np.int32)
    for here in itertools.product(*[range(s) for s in SIZES]):
        there, mirror = home(*here)
        table[there] = mirror
    return table.reshape(-1)


def block(a, b):
    return lax.dot_general(
        a, b, (((0,), (0,)), ((), ())), precision=lax.Precision.HIGH, preferred_element_type=F32
    )


def other_core(v):
    return permute(v, lambda xh, y, c, z, x: (xh, y, c + 1, z, x))


def reduce_chips(slots):
    got = lax.all_to_all(jnp.stack(slots), CHIPS, 0, 0, tiled=True)
    return jnp.sum(got, axis=0)


def shards(matrix, signs, picked):
    core = lax.axis_index("core")
    z = lax.axis_index("z")
    chip = lax.axis_index("xh") * 4 + lax.axis_index("y")
    samples = picked.shape[0] * 16
    slices = mix_slices(matrix, signs, picked)
    slices = lax.all_to_all(slices, ROW, 0, 0, tiled=True)
    own = sample(slices, 1.0 / samples**0.5)

    beside = permute(own, lambda xh, y, c, z, x: (xh, y, c, z, x + 1))
    up = permute(own, lambda xh, y, c, z, x: (xh, y, c, z - 1, x))
    down = permute(own, lambda xh, y, c, z, x: (xh, y, c, z + 1, x))
    up2 = permute(up, lambda xh, y, c, z, x: (xh, y, c, z - 1, x if (z - 1) % 8 < 4 else x + 1))
    down2 = permute(down, lambda xh, y, c, z, x: (xh, y, c, z + 1, x))
    down_beside = permute(down, lambda xh, y, c, z, x: (xh, y, c, z, x + 1) if z < 4 else None)

    def halves(v):
        v = v.reshape(2, 128, 256)
        return jnp.where(core == 0, v[0], v[1]), jnp.where(core == 0, v[1], v[0])

    diag, near = block(own, own), block(beside, own)
    first = [halves(block(up, v)) for v in (own, beside, down)]
    keep = jnp.concatenate([jnp.where(core == 0, diag, near)] + [v[0] for v in first])
    send = jnp.concatenate([jnp.where(core == 0, near, diag)] + [v[1] for v in first])
    early = (keep + other_core(send)).reshape(5, 128, 256)
    none = jnp.zeros((128, 256), F32)
    early_sum = reduce_chips([early[2], early[3], early[4], none, none, none, none, early[1]])

    low = z < 4
    second = [
        halves(block(up2, jnp.where(low, beside, own))),
        halves(block(up, down2)),
        halves(block(up2, jnp.where(low, down_beside, down))),
        halves(block(up2, down2)),
    ]
    keep = jnp.concatenate([v[0] for v in second])
    send = jnp.concatenate([v[1] for v in second])
    late = (keep + other_core(send)).reshape(4, 128, 256)
    late_sum = reduce_chips([none, none, none, late[0], late[1], late[2], late[3], early[0]])

    half = jnp.where(chip < 3, early_sum, late_sum)
    other = jnp.where(chip == 7, early_sum, other_core(half))
    swap = (core == 1) & (chip < 7)
    whole = jnp.concatenate([jnp.where(swap, other, half), jnp.where(swap, half, other)])
    whole = permute(whole, lambda *here: home(*here)[0])
    here = lax.axis_index(NAMES)
    return jnp.where(jnp.asarray(mirrored())[here] == 1, whole.T, whole)


def solution(mesh):
    mesh = Mesh(mesh.devices.reshape(SIZES), NAMES)
    return jax.shard_map(
        shards, mesh=mesh, in_specs=(P(ROW, COL), P(ROW), P(ROW)), out_specs=P(ROW, COL), check_vma=False
    )
```

time: 669 us -> 192 us (0.29)
  waiting for transfers between devices: 588 us -> 101 us
  blocking collectives: 0 us -> 23.4 us
  starting transfers between devices: 6.76 us -> 27.1 us
  matrix products: 37.3 us -> 17.2 us
  between operations: 13.5 us -> 0.95 us
  Pallas kernels: 0 us -> 9.8 us
  other arithmetic: 13.8 us -> 4.62 us
    all_gather x1 -> x0, waiting for transfers between devices: 353 us -> none  [shards(): full_sketch = lax.all_gather(sketch, 'col', axis=1, tiled=True)]
    reduce_scatter x1 -> x0, waiting for transfers between devices: 94.6 us -> none  [shards(): lax.psum_scatter(lax.dot_general(full_sketch, sketch, (((0,), (0,)), ((),...]
    ppermute x4 -> x10, waiting for transfers between devices: 141 us -> 58.8 us  [permute(): return lax.ppermute(block, NAMES, pairs)]
    all_to_all x0 -> x2, waiting for transfers between devices: none -> 42.3 us  [the longest x1 29.2 us: shards(): slices = lax.all_to_all(slices, ROW, 0, 0, tiled=True)]
    all_to_all x0 -> x1, blocking collectives: none -> 23.4 us  [reduce_chips(): got = lax.all_to_all(jnp.stack(slots), CHIPS, 0, 0, tiled=True)]
    dot_general x3 -> x9, matrix products: 37.3 us -> 17.2 us  [block(): lax.dot_general(a, b, (((0,), (0,)), ((), ())), precision=lax.Precision.H...]
    all_to_all x0 -> x2, starting transfers between devices: none -> 13.8 us  [the longest x1 7.45 us: shards(): slices = lax.all_to_all(slices, ROW, 0, 0, tiled=True)]
    pallas_call x0 -> x2, Pallas kernels: none -> 9.8 us  [the longest x1 5.84 us: mix_slices(): pl.pallas_call(mix_kernel, out_shape=jax.ShapeDtypeStruct((SLICES, SPAN +...]
  transfers between devices with their start and end apart: 6 -> 12, of which waited for: 6 -> 10; matrix products, arithmetic and copies ran while one was open for 0% -> 6% of each run, Pallas kernels for 0% -> 0%
where the time goes in v1:
time: 192 us; the launch traced here: 191 us
  waiting for transfers between devices  101 us (53%)
  starting transfers between devices  27.1 us (14%)
  blocking collectives  23.4 us (12%)
  matrix products  17.2 us (9%)
  Pallas kernels  9.8 us (5%)
  local copies, waits for them, and re-layouts  6.87 us (4%)
  other arithmetic  4.62 us (2%)
    ppermute x10, waiting for transfers between devices, permute(): return lax.ppermute(block, NAMES, pairs)  58.8 us
    all_to_all x1, waiting for transfers between devices, shards(): slices = lax.all_to_all(slices, ROW, 0, 0, tiled=True)  29.2 us
    all_to_all x1, blocking collectives, reduce_chips(): got = lax.all_to_all(jnp.stack(slots), CHIPS, 0, 0, tiled=True)  23.4 us
    dot_general x9, matrix products, block(): lax.dot_general(a, b, (((0,), (0,)), ((), ())), precision=lax.Precision.H...  17.2 us
    ppermute x10, starting transfers between devices, permute(): return lax.ppermute(block, NAMES, pairs)  13.2 us
    all_to_all x1, waiting for transfers between devices, reduce_chips(): got = lax.all_to_all(jnp.stack(slots), CHIPS, 0, 0, tiled=True)  13.1 us
    all_to_all x1, starting transfers between devices, shards(): slices = lax.all_to_all(slices, ROW, 0, 0, tiled=True)  7.45 us
    all_to_all x1, starting transfers between devices, reduce_chips(): got = lax.all_to_all(jnp.stack(slots), CHIPS, 0, 0, tiled=True)  6.39 us
  transfers between devices with their start and end apart: 12, of which 10 were waited for; matrix products, arithmetic and copies ran while one was open for 6% of the time, Pallas kernels for 0%

profile of v1, /device:TPU:6, one launch (start us, length us, event | category | flops | bytes accessed | tf_op | source)
XLA Modules:
  0.0 191.0 jit_solution(347787416383717716)
XLA Ops:
  0.0 5.8 %mix_slices.1 = f32[16,136,256]{2,1,0:T(8,128)} custom-call(s32[16,128]{1,0:T(8,128)} %bitcast.60, s32[8,128]{1,0:T(8,128)} %bitcast.61, f32[16,128,256]{2,1,0:T(8,128)} %bitcast.59), custom_call_target="tpu_custom_call" | custom-call | tf_op jit(solution)/shard_map/mix_slices/pallas_call | solution.py:65
  5.8 7.5 %all-to-all-start = ((f32[16,136,256]{2,1,0:T(8,128)}), f32[16,136,256]{2,1,0:T(8,128)S(1)}, u32[]{:S(2)}, u32[]{:S(2)}) async-start(f32[16,136,256]{2,1,0:T(8,128)} %mix_slices.1), calls=%async_computation | async-start | bytes 4456448 | tf_op jit(solution)/shard_map/all_to_all | solution.py:178
  13.3 29.2 %all-to-all-done.refs_1_ = f32[16,136,256]{2,1,0:T(8,128)S(1)} async-done(((f32[16,136,256]{2,1,0:T(8,128)}), f32[16,136,256]{2,1,0:T(8,128)S(1)}, u32[]{:S(2)}, u32[]{:S(2)}) %all-to-all-start) | async-done | bytes 2228256 | tf_op jit(solution)/shard_map/all_to_all | solution.py:178
  42.5 1.4 copy-done.1
  43.9 4.0 %sample.1 = f32[1024,256]{1,0:T(8,128)} custom-call(s32[1]{0:T(128)} %bitcast.1.refs_0_, f32[16,136,256]{2,1,0:T(8,128)} %copy-done.1), custom_call_target="tpu_custom_call" | custom-call | tf_op jit(solution)/shard_map/sample/pallas_call | solution.py:114
  47.8 5.9 %collective-permute-start.1 = (f32[1024,256]{1,0:T(8,128)}, f32[1024,256]{1,0:T(8,128)S(1)}, u32[]{:S(2)}, u32[]{:S(2)}) collective-permute-start(f32[1024,256]{1,0:T(8,128)} %sample.1), channel_id=1, source_target_pairs={{0,14},{1,15},{2,0},{3,1},{4,2},{5,3},{6,4},{7,5},{8,6},{9,7},{10,... | collective-permute-start | bytes 3145736 | tf_op jit(solution)/shard_map/ppermute | solution.py:31
  53.7 0.2 collective-permute-start
  53.9 2.5 %fusion.15 = f32[256,256]{1,0:T(8,128)S(1)} fusion(f32[1024,256]{1,0:T(8,128)} %sample.1), kind=kOutput, calls=%fused_computation.53 | convolution fusion | flops 402653184 | bytes 1310720 | tf_op jit(solution)/shard_map/dot_general | solution.py:158
  56.4 19.8 %collective-permute-done.1 = f32[1024,256]{1,0:T(8,128)S(1)} collective-permute-done((f32[1024,256]{1,0:T(8,128)}, f32[1024,256]{1,0:T(8,128)S(1)}, u32[]{:S(2)}, u32[]{:S(2)}) %collective-permute-start.1) | collective-permute-done | bytes 1048608 | tf_op jit(solution)/shard_map/ppermute | solution.py:31
  76.2 3.4 %collective-permute-done.2 = f32[1024,256]{1,0:T(8,128)} collective-permute-done((f32[1024,256]{1,0:T(8,128)}, f32[1024,256]{1,0:T(8,128)}, u32[]{:S(2)}, u32[]{:S(2)}) %collective-permute-start.2) | collective-permute-done | bytes 1048608 | tf_op jit(solution)/shard_map/ppermute | solution.py:31
  79.6 2.2 %fusion.18 = f32[256,256]{1,0:T(8,128)S(1)} fusion(f32[1024,256]{1,0:T(8,128)S(1)} %collective-permute-done.1, f32[1024,256]{1,0:T(8,128)} %collective-permute-done.2), kind=kOutput, calls=%fused_computation.56 | convolution fusion | flops 402653184 | bytes 2359296 | tf_op jit(solution)/shard_map/dot_general | solution.py:158
  81.9 1.0 fusion.17
  82.9 0.7 slice_select_fusion.11
  83.6 1.0 fusion.16
  84.6 0.7 slice_select_fusion.13
  85.3 1.0 broadcast_select_fusion.1
  86.3 0.9 pad_maximum_fusion
  87.2 2.0 %collective-permute-start.5 = (f32[1024,256]{1,0:T(8,128)}, f32[1024,256]{1,0:T(8,128)}, u32[]{:S(2)}, u32[]{:S(2)}) collective-permute-start(f32[1024,256]{1,0:T(8,128)} %collective-permute-done.2), channel_id=1, source_target_pairs={{0,2},{1,3},{2,4},{3,5},{4,6},{5,7},{6,8},{7,9},{8,10},{9,11},{10,... | collective-permute-start | bytes 3145736 | tf_op jit(solution)/shard_map/ppermute | solution.py:31
  89.2 0.7 broadcast_dynamic-update-slice_fusion.2
  89.9 2.2 %collective-permute-start.6 = (f32[1024,256]{1,0:T(8,128)}, f32[1024,256]{1,0:T(8,128)}, u32[]{:S(2)}, u32[]{:S(2)}) collective-permute-start(f32[1024,256]{1,0:T(8,128)} %collective-permute-done.2), channel_id=1, source_target_pairs={{0,1},{1,0},{2,3},{3,2},{4,5},{5,4},{6,7},{7,6},{16,17},{17,16},{1... | collective-permute-start | bytes 3145736 | tf_op jit(solution)/shard_map/ppermute | solution.py:31
  92.1 0.7 broadcast_dynamic-update-slice_fusion.1
  92.8 1.2 maximum_add_fusion
  94.0 18.8 %collective-permute-done.4 = f32[1024,256]{1,0:T(8,128)} collective-permute-done((f32[1024,256]{1,0:T(8,128)S(1)}, f32[1024,256]{1,0:T(8,128)}, u32[]{:S(2)}, u32[]{:S(2)}) %collective-permute-start.4) | collective-permute-done | bytes 1048608 | tf_op jit(solution)/shard_map/ppermute | solution.py:31
  112.8 1.4 collective-permute-done.5
  114.3 2.5 %fusion.20 = f32[256,256]{1,0:T(8,128)S(1)} fusion(f32[1024,256]{1,0:T(8,128)} %collective-permute-done.4, f32[1024,256]{1,0:T(8,128)} %collective-permute-done.5), kind=kOutput, calls=%fused_computation.58 | convolution fusion | flops 402653184 | bytes 2359296 | tf_op jit(solution)/shard_map/dot_general | solution.py:158
  116.8 0.2 collective-permute-done.6
  117.1 2.5 %fusion = f32[256,256]{1,0:T(8,128)S(1)} fusion(f32[1024,256]{1,0:T(8,128)} %collective-permute-done.4, f32[1024,256]{1,0:T(8,128)} %collective-permute-done.6, f32[1024,256]{1,0:T(8,128)} %collective-permute-done.2, pred[]{:T(512)S(6)} %lt.15), kind=kOutput, calls=%fused_computation | convolution fusion | flops 402915328 | bytes 3407873 | tf_op jit(solution)/shard_map/dot_general | solution.py:158
  119.6 2.2 %fusion.19 = f32[256,256]{1,0:T(8,128)S(1)} fusion(f32[1024,256]{1,0:T(8,128)S(1)} %collective-permute-done.1, f32[1024,256]{1,0:T(8,128)} %collective-permute-done.5), kind=kOutput, calls=%fused_computation.57 | convolution fusion | flops 402653184 | bytes 2359296 | tf_op jit(solution)/shard_map/dot_general | solution.py:158
  121.9 2.2 %fusion.2 = f32[256,256]{1,0:T(8,128)S(1)} fusion(f32[1024,256]{1,0:T(8,128)} %collective-permute-done.4, f32[1024,256]{1,0:T(8,128)S(1)} %collective-permute-done, f32[1024,256]{1,0:T(8,128)S(1)} %copy-done, pred[]{:T(512)S(6)} %lt.15), kind=kOutput, calls=%fused_computation.2 | convolution fusion | flops 402915328 | bytes 3407873 | tf_op jit(solution)/shard_map/dot_general | solution.py:158
  124.2 0.1 collective-permute-start.7
  124.4 1.8 collective-permute-done.7
  126.2 0.1 maximum_add_fusion.1
  126.3 0.7 fusion.10
  126.9 0.7 fusion.9
  127.6 0.7 fusion.8
  128.3 0.7 fusion.7
  128.9 0.7 fusion.6
  129.6 23.4 %all_to_all.15 = f32[8,128,256]{2,1,0:T(8,128)S(1)} all-to-all(f32[8,128,256]{2,1,0:T(8,128)S(1)} %get-tuple-element.6), channel_id=1, replica_groups=mesh['xh'=2,'y'=4,'core'=2,'z'=8,'xl'=2] {'xh','y'}, dimensions={0} | all-to-all | bytes 2097152 | tf_op jit(solution)/shard_map/all_to_all | solution.py:168
  153.0 6.4 %all-to-all-start.2 = ((f32[8,128,256]{2,1,0:T(8,128)}), f32[8,128,256]{2,1,0:T(8,128)S(1)}, u32[]{:S(2)}, u32[]{:S(2)}) async-start(f32[8,128,256]{2,1,0:T(8,128)} %get-tuple-element.5), calls=%async_computation.2 | async-start | bytes 2097152 | tf_op jit(solution)/shard_map/all_to_all | solution.py:168
  159.4 0.1 reduce_sum.18
  159.5 13.1 %all-to-all-done.2 = f32[8,128,256]{2,1,0:T(8,128)S(1)} async-done(((f32[8,128,256]{2,1,0:T(8,128)}), f32[8,128,256]{2,1,0:T(8,128)S(1)}, u32[]{:S(2)}, u32[]{:S(2)}) %all-to-all-start.2) | async-done | bytes 1048608 | tf_op jit(solution)/shard_map/all_to_all | solution.py:168
  172.6 0.1 collective-permute-start.8
  172.7 1.3 collective-permute-done.8
  174.1 2.8 %collective-permute-start.9 = (f32[256,256]{1,0:T(8,128)S(1)}, f32[256,256]{1,0:T(8,128)S(1)}, u32[]{:S(2)}, u32[]{:S(2)}) collective-permute-start(f32[256,256]{1,0:T(8,128)S(1)} %pad_maximum_fusion.2), channel_id=1, source_target_pairs={{0,32},{1,49},{2,66},{3,83},{4,100},{5,117},{6,134},{7,151},{8,168... | collective-permute-start | bytes 786440 | tf_op jit(solution)/shard_map/ppermute | solution.py:31
  176.9 0.6 dynamic_slice.3
  178.1 12.0 %collective-permute-done.9 = f32[256,256]{1,0:T(8,128)S(1)} collective-permute-done((f32[256,256]{1,0:T(8,128)S(1)}, f32[256,256]{1,0:T(8,128)S(1)}, u32[]{:S(2)}, u32[]{:S(2)}) %collective-permute-start.9) | collective-permute-done | bytes 262176 | tf_op jit(solution)/shard_map/ppermute | solution.py:31
  190.2 0.1 copy.6
  190.3 0.7 bitcast_select_fusion
  (24 shorter events, 0.4 us)
Async XLA Ops:
  5.8 36.6 %all-to-all-start = ((f32[16,136,256]{2,1,0:T(8,128)}), f32[16,136,256]{2,1,0:T(8,128)S(1)}, u32[]{:S(2)}, u32[]{:S(2)}) async-start(f32[16,136,256]{2,1,0:T(8,128)} %mix_slices.1), calls=%async_computation | async-start | bytes 4456448 | tf_op jit(solution)/shard_map/all_to_all | solution.py:178
  42.5 1.4 copy-start.1
  47.8 28.4 %collective-permute-start.1 = (f32[1024,256]{1,0:T(8,128)}, f32[1024,256]{1,0:T(8,128)S(1)}, u32[]{:S(2)}, u32[]{:S(2)}) collective-permute-start(f32[1024,256]{1,0:T(8,128)} %sample.1), channel_id=1, source_target_pairs={{0,14},{1,15},{2,0},{3,1},{4,2},{5,3},{6,4},{7,5},{8,6},{9,7},{10,... | collective-permute-start | bytes 3145736 | tf_op jit(solution)/shard_map/ppermute | solution.py:31
  53.7 26.0 %collective-permute-start.2 = (f32[1024,256]{1,0:T(8,128)}, f32[1024,256]{1,0:T(8,128)}, u32[]{:S(2)}, u32[]{:S(2)}) collective-permute-start(f32[1024,256]{1,0:T(8,128)} %sample.1), channel_id=1, source_target_pairs={{0,2},{1,3},{2,4},{3,5},{4,6},{5,7},{6,8},{7,9},{8,10},{9,11},{10,... | collective-permute-start | bytes 3145736 | tf_op jit(solution)/shard_map/ppermute | solution.py:31
  53.7 28.2 %collective-permute-start = (f32[1024,256]{1,0:T(8,128)}, f32[1024,256]{1,0:T(8,128)S(1)}, u32[]{:S(2)}, u32[]{:S(2)}) collective-permute-start(f32[1024,256]{1,0:T(8,128)} %sample.1), channel_id=1, source_target_pairs={{0,1},{1,0},{2,3},{3,2},{4,5},{5,4},{6,7},{7,6},{8,9},{9,8},{10,11... | collective-permute-start | bytes 3145736 | tf_op jit(solution)/shard_map/ppermute | solution.py:31
  81.9 1.7 copy-start
  87.2 5.6 %collective-permute-start.3 = (f32[640,256]{1,0:T(8,128)}, f32[640,256]{1,0:T(8,128)}, u32[]{:S(2)}, u32[]{:S(2)}) collective-permute-start(f32[640,256]{1,0:T(8,128)} %pad_maximum_fusion), channel_id=1, source_target_pairs={{0,16},{1,17},{2,18},{3,19},{4,20},{5,21},{6,22},{7,23},{8,24},{9,... | collective-permute-start | bytes 1966088 | tf_op jit(solution)/shard_map/ppermute | solution.py:31
  87.2 25.7 %collective-permute-start.4 = (f32[1024,256]{1,0:T(8,128)S(1)}, f32[1024,256]{1,0:T(8,128)}, u32[]{:S(2)}, u32[]{:S(2)}) collective-permute-start(f32[1024,256]{1,0:T(8,128)S(1)} %collective-permute-done.1), channel_id=1, source_target_pairs={{0,15},{1,14},{2,0},{3,1},{4,2},{5,3},{6,4},{7,5},{8,6},{9,7},{10,... | collective-permute-start | bytes 3145736 | tf_op jit(solution)/shard_map/ppermute | solution.py:31
  87.2 27.1 %collective-permute-start.5 = (f32[1024,256]{1,0:T(8,128)}, f32[1024,256]{1,0:T(8,128)}, u32[]{:S(2)}, u32[]{:S(2)}) collective-permute-start(f32[1024,256]{1,0:T(8,128)} %collective-permute-done.2), channel_id=1, source_target_pairs={{0,2},{1,3},{2,4},{3,5},{4,6},{5,7},{6,8},{7,9},{8,10},{9,11},{10,... | collective-permute-start | bytes 3145736 | tf_op jit(solution)/shard_map/ppermute | solution.py:31
  89.9 27.2 %collective-permute-start.6 = (f32[1024,256]{1,0:T(8,128)}, f32[1024,256]{1,0:T(8,128)}, u32[]{:S(2)}, u32[]{:S(2)}) collective-permute-start(f32[1024,256]{1,0:T(8,128)} %collective-permute-done.2), channel_id=1, source_target_pairs={{0,1},{1,0},{2,3},{3,2},{4,5},{5,4},{6,7},{7,6},{16,17},{17,16},{1... | collective-permute-start | bytes 3145736 | tf_op jit(solution)/shard_map/ppermute | solution.py:31
  124.2 2.0 %collective-permute-start.7 = (f32[512,256]{1,0:T(8,128)S(1)}, f32[512,256]{1,0:T(8,128)S(1)}, u32[]{:S(2)}, u32[]{:S(2)}) collective-permute-start(f32[512,256]{1,0:T(8,128)S(1)} %pad_maximum_fusion.1), channel_id=1, source_target_pairs={{0,16},{1,17},{2,18},{3,19},{4,20},{5,21},{6,22},{7,23},{8,24},{9,... | collective-permute-start | bytes 1572872 | tf_op jit(solution)/shard_map/ppermute | solution.py:31
  153.0 19.5 %all-to-all-start.2 = ((f32[8,128,256]{2,1,0:T(8,128)}), f32[8,128,256]{2,1,0:T(8,128)S(1)}, u32[]{:S(2)}, u32[]{:S(2)}) async-start(f32[8,128,256]{2,1,0:T(8,128)} %get-tuple-element.5), calls=%async_computation.2 | async-start | bytes 2097152 | tf_op jit(solution)/shard_map/all_to_all | solution.py:168
  159.4 17.5 %copy-start.2 = (s32[256]{0:T(256)S(1)}, s32[256]{0:T(256)}, u32[]{:S(2)}) copy-start(s32[256]{0:T(256)} %constant.50.clone) | copy-start | bytes 3076
  172.6 1.4 collective-permute-start.8
  174.1 16.1 %collective-permute-start.9 = (f32[256,256]{1,0:T(8,128)S(1)}, f32[256,256]{1,0:T(8,128)S(1)}, u32[]{:S(2)}, u32[]{:S(2)}) collective-permute-start(f32[256,256]{1,0:T(8,128)S(1)} %pad_maximum_fusion.2), channel_id=1, source_target_pairs={{0,32},{1,49},{2,66},{3,83},{4,100},{5,117},{6,134},{7,151},{8,168... | collective-permute-start | bytes 786440 | tf_op jit(solution)/shard_map/ppermute | solution.py:31

commit v2 on v1

v2 whole, which is shorter than its diff:
```python
import itertools

import jax
import jax.numpy as jnp
import numpy as np
from jax import lax
from jax.experimental import pallas as pl
from jax.experimental.pallas import tpu as pltpu
from jax.sharding import Mesh
from jax.sharding import PartitionSpec as P

NAMES = ("xh", "y", "core", "z", "xl")
SIZES = (2, 4, 2, 8, 2)
ROW = ("xh", "y", "core")
COL = ("z", "xl")
CHIPS = ("xh", "y")
SLICES = 16
SPAN = 128
F32 = jnp.float32
BF16 = jnp.bfloat16


def permute(block, route):
    pairs = []
    for here in itertools.product(*[range(s) for s in SIZES]):
        there = route(*here)
        if there is None:
            continue
        there = tuple(v % s for v, s in zip(there, SIZES))
        pairs.append((int(np.ravel_multi_index(here, SIZES)), int(np.ravel_multi_index(there, SIZES))))
    return lax.ppermute(block, NAMES, pairs)


def hadamard(vals):
    step = 1
    vals = list(vals)
    while step < len(vals):
        for i in range(len(vals)):
            if not i & step:
                a, b = vals[i], vals[i | step]
                vals[i], vals[i | step] = a + b, a - b
        step *= 2
    return vals


def mix_kernel(signs_ref, picked_ref, x_ref, o_ref, sign_ref, x_buf, o_buf, in_sem, out_sem):
    steps, rows = 4, SPAN // 4

    def part(ref, k):
        return ref.at[:, pl.ds(k * rows, rows), :]

    loads = [pltpu.make_async_copy(part(x_ref, k), part(x_buf, k), in_sem.at[k]) for k in range(steps)]
    for load in loads:
        load.start()
    sign_ref[...] = signs_ref[...].astype(F32).T
    for s in range(SLICES):
        row = picked_ref[s // 2 : s // 2 + 1, :].astype(F32)
        o_buf[s, SPAN:, :] = jnp.broadcast_to(jnp.concatenate([row, row], axis=1), (8, 256))
    picks = pl.ds(SPAN, 8)
    stores = [pltpu.make_async_copy(o_buf.at[:, picks, :], o_ref.at[:, picks, :], out_sem.at[steps])]
    stores[0].start()
    for k in range(steps):
        loads[k].wait()

        def chunk(i, carry):
            at = pl.ds(pl.multiple_of(k * rows + i * 8, 8), 8)
            sign = sign_ref[at, :]
            sign = [jnp.broadcast_to(sign[:, a : a + 1], (8, 128)) for a in range(SLICES)]
            for first in (0, 128):
                cols = pl.ds(first, 128)
                vals = hadamard([x_buf[a, at, cols] * sign[a] for a in range(SLICES)])
                for s in range(SLICES):
                    o_buf[s, at, cols] = vals[s]
            return carry

        lax.fori_loop(0, rows // 8, chunk, 0)
        stores.append(pltpu.make_async_copy(part(o_buf, k), part(o_ref, k), out_sem.at[k]))
        stores[-1].start()
    for store in stores:
        store.wait()


def mix_slices(matrix, signs, picked):
    rows, cols = matrix.shape
    vmem = pl.BlockSpec(memory_space=pltpu.VMEM)
    shape = (SLICES, SPAN + 8, cols)
    return pl.pallas_call(
        mix_kernel,
        out_shape=pltpu.HBM(shape, F32),
        in_specs=[vmem, vmem, pl.BlockSpec(memory_space=pltpu.HBM)],
        out_specs=pl.BlockSpec(memory_space=pltpu.HBM),
        scratch_shapes=[
            pltpu.VMEM((SPAN, SLICES), F32),
            pltpu.VMEM((SLICES, SPAN, cols), F32),
            pltpu.VMEM(shape, F32),
            pltpu.SemaphoreType.DMA((4,)),
            pltpu.SemaphoreType.DMA((5,)),
        ],
        name="mix_slices",
    )(
        signs.reshape(SLICES, SPAN),
        picked.reshape(8, 128),
        pltpu.with_memory_space_constraint(matrix.reshape(SLICES, SPAN, cols), pltpu.HBM),
    )


def sample_kernel(scale, half_ref, y_ref, o_ref, mixed_ref, where_ref):
    picks = jnp.concatenate([y_ref[q, SPAN : SPAN + 1, :128] for q in range(SLICES)], axis=0)
    where_ref[...] = picks.T.astype(jnp.int32)

    def chunk(i, carry):
        rows = pl.ds(pl.multiple_of(i * 8, 8), 8)
        vals = hadamard([y_ref[p, rows, :] for p in range(SLICES)])
        for q in range(SLICES):
            mixed_ref[q, rows, :] = vals[q] * scale
        return carry

    lax.fori_loop(0, SPAN // 8, chunk, 0)
    mine = pl.ds(pl.multiple_of(half_ref[0] * 64, 64), 64)
    lane = lax.broadcasted_iota(jnp.int32, (64, SPAN), 1)
    for q in range(SLICES):
        both = where_ref[mine, q : q + 1] & lane
        both = both ^ (both >> 4)
        both = both ^ (both >> 2)
        both = both ^ (both >> 1)
        signs = (1 - 2 * (both & 1)).astype(F32).astype(BF16)
        vals = mixed_ref[q]
        high = vals.astype(BF16)
        rest = vals - high.astype(F32)
        mid = rest.astype(BF16)
        low = (rest - mid.astype(F32)).astype(BF16)
        out = jnp.dot(signs, low, preferred_element_type=F32)
        out += jnp.dot(signs, mid, preferred_element_type=F32)
        out += jnp.dot(signs, high, preferred_element_type=F32)
        o_ref[q * 64 : (q + 1) * 64, :] = out


def sample(slices, scale):
    cols = slices.shape[2]
    half = lax.axis_index("core").reshape(1)
    return pl.pallas_call(
        lambda *refs: sample_kernel(scale, *refs),
        out_shape=jax.ShapeDtypeStruct((SLICES * 64, cols), F32),
        in_specs=[pl.BlockSpec(memory_space=pltpu.SMEM), pl.BlockSpec(memory_space=pltpu.VMEM)],
        out_specs=pl.BlockSpec(memory_space=pltpu.VMEM),
        scratch_shapes=[pltpu.VMEM((SLICES, SPAN, cols), F32), pltpu.VMEM((SPAN, SLICES), jnp.int32)],
        compiler_params=pltpu.CompilerParams(vmem_limit_bytes=12 << 20),
        name="sample",
    )(half, slices)


def early_pairs(core):
    return [((1, 0), (0, 0)), ((1, 0), (0, 1)), ((1, 0), (-1, 0)), ((0, core), (0, 0))]


def late_pairs(z):
    if z < 4:
        return [((2, 0), (0, 1)), ((1, 0), (-2, 0)), ((2, 0), (-1, 1)), ((2, 0), (-2, 0))]
    return [((2, 1), (0, 0)), ((1, 0), (-2, 0)), ((2, 1), (-1, 0)), ((2, 1), (-2, 0))]


def home(late, xh, y, core, z, xl):
    unit = (xh * 4 + y) // 2
    (rz, rx), (cz, cx) = late_pairs(z)[unit] if late else early_pairs(core)[unit]
    mirror = core == 1 and (late or unit < 3)
    row, col = ((z + rz) % 8, xl ^ rx), ((z + cz) % 8, xl ^ cx)
    if mirror:
        row, col = col, row
    return (row[0] // 4, row[0] % 4, row[1], col[0], col[1]), mirror


def mirrored():
    table = np.zeros(SIZES, bool)
    for here in itertools.product(*[range(s) for s in SIZES]):
        for late in (False, True):
            there, mirror = home(late, *here)
            table[there] = mirror
    return table.reshape(-1)


def halves(ref):
    vals = ref[...]
    high = vals.astype(BF16)
    return high, (vals - high.astype(F32)).astype(BF16)


def turned(parts):
    return tuple(v.T for v in parts)


def block(a, b):
    out = jnp.dot(a[0], b[1], preferred_element_type=F32)
    out += jnp.dot(a[1], b[0], preferred_element_type=F32)
    return out + jnp.dot(a[0], b[0], preferred_element_type=F32)


def put_block(core, out, unit, keep_ref, send_ref):
    for half in range(2):
        for owner in range(2):
            rows = out[half * 128 + owner * 64 : half * 128 + owner * 64 + 64]

            @pl.when(core == owner)
            def _():
                keep_ref[2 * unit + half, :64, :] = rows

            @pl.when(core != owner)
            def _():
                send_ref[2 * unit + half, :64, :] = rows


def early_kernel(core_ref, own_ref, beside_ref, up_ref, down_ref, keep_ref, send_ref):
    core = core_ref[0]
    own, beside = halves(own_ref), halves(beside_ref)
    for owner, left in ((0, own), (1, beside)):
        out = block(turned(left), own)
        for half in range(2):
            rows = out[half * 128 : half * 128 + 128]

            @pl.when(core == owner)
            def _():
                keep_ref[6 + half] = rows

            @pl.when(core != owner)
            def _():
                send_ref[6 + half] = rows

    up = turned(halves(up_ref))
    for unit, right in enumerate((own, beside, halves(down_ref))):
        put_block(core, block(up, right), unit, keep_ref, send_ref)
    for unit in range(6):
        keep_ref[unit, 64:, :] = jnp.zeros((64, 256), F32)
        send_ref[unit, 64:, :] = jnp.zeros((64, 256), F32)


def late_kernel(
    flags_ref, own_ref, beside_ref, up_ref, down_ref, down_beside_ref, up2_ref, down2_ref, keep_ref, send_ref, pick_ref
):
    core, low = flags_ref[0], flags_ref[1]

    def pick(a_ref, b_ref):
        @pl.when(low == 1)
        def _():
            pick_ref[...] = a_ref[...]

        @pl.when(low == 0)
        def _():
            pick_ref[...] = b_ref[...]

        return halves(pick_ref)

    up2, down2 = turned(halves(up2_ref)), halves(down2_ref)
    put_block(core, block(up2, pick(beside_ref, own_ref)), 0, keep_ref, send_ref)
    put_block(core, block(turned(halves(up_ref)), down2), 1, keep_ref, send_ref)
    put_block(core, block(up2, pick(down_beside_ref, down_ref)), 2, keep_ref, send_ref)
    put_block(core, block(up2, down2), 3, keep_ref, send_ref)


def call_blocks(kernel, rows, flags, operands, scratch, cost, name):
    vmem = pl.BlockSpec(memory_space=pltpu.VMEM)
    return pl.pallas_call(
        kernel,
        out_shape=[jax.ShapeDtypeStruct((8, rows, 256), F32)] * 2,
        in_specs=[pl.BlockSpec(memory_space=pltpu.SMEM)] + [vmem] * len(operands),
        out_specs=[vmem] * 2,
        scratch_shapes=scratch,
        compiler_params=pltpu.CompilerParams(vmem_limit_bytes=20 << 20),
        cost_estimate=pl.CostEstimate(flops=cost, bytes_accessed=cost // 400, transcendentals=0),
        name=name,
    )(flags, *operands)


def other_core(v):
    return permute(v, lambda xh, y, c, z, x: (xh, y, c + 1, z, x))


def shards(matrix, signs, picked):
    core = lax.axis_index("core")
    z = lax.axis_index("z")
    chip = lax.axis_index("xh") * 4 + lax.axis_index("y")
    samples = picked.shape[0] * 16
    slices = mix_slices(matrix, signs, picked)
    slices = lax.all_to_all(slices, ROW, 0, 0, tiled=True)
    own = sample(slices, 1.0 / samples**0.5)

    up = permute(own, lambda xh, y, c, z, x: (xh, y, c, z - 1, x))
    down = permute(own, lambda xh, y, c, z, x: (xh, y, c, z + 1, x))
    beside = permute(own, lambda xh, y, c, z, x: (xh, y, c, z, x + 1))
    up2 = permute(up, lambda xh, y, c, z, x: (xh, y, c, z - 1, x if (z - 1) % 8 < 4 else x + 1))
    down2 = permute(down, lambda xh, y, c, z, x: (xh, y, c, z + 1, x))
    down_beside = permute(down, lambda xh, y, c, z, x: (xh, y, c, z, x + 1) if z < 4 else None)

    core_flag = core.reshape(1)
    keep, send = call_blocks(early_kernel, 128, core_flag, (own, beside, up, down), [], 1000, "early_blocks")
    early = keep + jnp.concatenate([other_core(send[2 * i : 2 * i + 2]) for i in range(4)])
    early = early.reshape(2, 4, 128, 256)
    row = lax.axis_index("y")
    total = lax.dynamic_index_in_dim(early, row, 1, keepdims=False)
    for step in range(1, 4):
        part = lax.dynamic_index_in_dim(early, (row + step) % 4, 1, keepdims=False)
        total += permute(part, lambda xh, y, c, z, x: (xh, y + step, c, z, x))

    def by_core(mine):
        got = other_core(mine)
        return jnp.concatenate([jnp.where(core == 0, mine, got), jnp.where(core == 0, got, mine)])

    def deliver(piece, late):
        def route(half):
            return lambda *here: home(late, *here)[0] if here[1] % 2 == half else None

        return permute(piece, route(0)), permute(piece, route(1))

    flags = jnp.stack([core, (z < 4).astype(jnp.int32)])
    keep, send = call_blocks(
        late_kernel,
        64,
        flags,
        (own, beside, up, down, down_beside, up2, down2),
        [pltpu.VMEM(own.shape, F32)],
        40_000_000_000,
        "late_blocks",
    )
    slots = lax.all_to_all(keep + other_core(send), CHIPS, 0, 0, tiled=True)
    plane = lax.axis_index("xh")
    early = jnp.where(plane == 0, total[0], total[1]) + permute(
        jnp.where(plane == 0, total[1], total[0]), lambda xh, y, c, z, x: (xh + 1, y, c, z, x)
    )
    early = deliver(jnp.where(chip >= 6, early, by_core(early[:64])), False)
    late = jnp.sum(slots, axis=0)
    late = deliver(by_core(late), True)
    whole = jnp.concatenate([a + b for a, b in zip(early, late)])
    return jnp.where(jnp.asarray(mirrored())[lax.axis_index(NAMES)], whole.T, whole)


def solution(mesh):
    mesh = Mesh(mesh.devices.reshape(SIZES), NAMES)
    return jax.shard_map(
        shards, mesh=mesh, in_specs=(P(ROW, COL), P(ROW), P(ROW)), out_specs=P(ROW, COL), check_vma=False
    )
```

time: 192 us -> 154 us (0.80)
  starting transfers between devices: 27.1 us -> 54.4 us
  waiting for transfers between devices: 101 us -> 75.2 us
  blocking collectives: 23.4 us -> 0 us
  matrix products: 17.2 us -> 0 us
  Pallas kernels: 9.8 us -> 17.1 us
  local copies, waits for them, and re-layouts: 6.87 us -> 1.95 us
    ppermute x10 -> x21, starting transfers between devices: 13.2 us -> 40.9 us  [permute(): return lax.ppermute(block, NAMES, pairs)]
    all_to_all x1 -> x0, blocking collectives: 23.4 us -> none  [reduce_chips(): got = lax.all_to_all(jnp.stack(slots), CHIPS, 0, 0, tiled=True)]
    ppermute x10 -> x21, waiting for transfers between devices: 58.8 us -> 38.6 us  [permute(): return lax.ppermute(block, NAMES, pairs)]
    dot_general x9 -> x0, matrix products: 17.2 us -> none  [block(): lax.dot_general(a, b, (((0,), (0,)), ((), ())), precision=lax.Precision.H...]
    pallas_call x1 -> x3, Pallas kernels: 5.84 us -> 15.8 us  [the longest x2 11.4 us: call_blocks(): pl.pallas_call(kernel, out_shape=[jax.ShapeDtypeStruct((8, rows, 256), F3...]
    all_to_all x1, waiting for transfers between devices: 13.1 us -> 7.43 us  [shards(): slots = lax.all_to_all(keep + other_core(send), CHIPS, 0, 0, tiled=True)]
    unnamed x16 -> x8, local copies, waits for them, and re-layouts: 5.48 us -> 0.23 us
    pallas_call x1, Pallas kernels: 3.95 us -> 1.33 us  [sample(): pl.pallas_call(lambda *refs: sample_kernel(scale, *refs), out_shape=jax.S...]
  transfers between devices with their start and end apart: 12 -> 23, of which waited for: 10 -> 10; matrix products, arithmetic and copies ran while one was open for 6% -> 3% of each run, Pallas kernels for 0% -> 7%
where the time goes in v2:
time: 154 us; the launch traced here: 153 us
  waiting for transfers between devices  75.2 us (49%)
  starting transfers between devices  54.4 us (35%)
  Pallas kernels  17.1 us (11%)
  other arithmetic  4.17 us (3%)
  local copies, waits for them, and re-layouts  1.95 us (1%)
    ppermute x21, starting transfers between devices, permute(): return lax.ppermute(block, NAMES, pairs)  40.9 us
    ppermute x21, waiting for transfers between devices, permute(): return lax.ppermute(block, NAMES, pairs)  38.6 us
    all_to_all x1, waiting for transfers between devices, shards(): slices = lax.all_to_all(slices, ROW, 0, 0, tiled=True)  29.2 us
    pallas_call x2, Pallas kernels, call_blocks(): pl.pallas_call(kernel, out_shape=[jax.ShapeDtypeStruct((8, rows, 256), F3...  11.4 us
    all_to_all x1, starting transfers between devices, shards(): slices = lax.all_to_all(slices, ROW, 0, 0, tiled=True)  7.46 us
    all_to_all x1, waiting for transfers between devices, shards(): slots = lax.all_to_all(keep + other_core(send), CHIPS, 0, 0, tiled=True)  7.43 us
    all_to_all x1, starting transfers between devices, shards(): slots = lax.all_to_all(keep + other_core(send), CHIPS, 0, 0, tiled=True)  6.03 us
    pallas_call x1, Pallas kernels, mix_slices(): pl.pallas_call(mix_kernel, out_shape=pltpu.HBM(shape, F32), in_specs=[vme...  4.38 us
  transfers between devices with their start and end apart: 23, of which 10 were waited for; matrix products, arithmetic and copies ran while one was open for 3% of the time, Pallas kernels for 7%

profile of v2, /device:TPU:6, one launch (start us, length us, event | category | flops | bytes accessed | tf_op | source)
XLA Modules:
  0.0 153.1 jit_solution(11096590439548770997)
XLA Ops:
  0.0 4.4 %mix_slices.1 = f32[16,136,256]{2,1,0:T(8,128)} custom-call(s32[16,128]{1,0:T(8,128)} %bitcast.28, s32[8,128]{1,0:T(8,128)} %bitcast.29, f32[16,128,256]{2,1,0:T(8,128)} %bitcast.27), custom_call_target="tpu_custom_call" | custom-call | tf_op jit(solution)/shard_map/mix_slices/pallas_call | solution.py:87
  4.4 7.5 %all-to-all-start = ((f32[16,136,256]{2,1,0:T(8,128)}), f32[16,136,256]{2,1,0:T(8,128)S(1)}, u32[]{:S(2)}, u32[]{:S(2)}) async-start(f32[16,136,256]{2,1,0:T(8,128)} %mix_slices.1), calls=%async_computation | async-start | bytes 4456448 | tf_op jit(solution)/shard_map/all_to_all | solution.py:282
  11.8 29.2 %all-to-all-done.refs_1_ = f32[16,136,256]{2,1,0:T(8,128)S(1)} async-done(((f32[16,136,256]{2,1,0:T(8,128)}), f32[16,136,256]{2,1,0:T(8,128)S(1)}, u32[]{:S(2)}, u32[]{:S(2)}) %all-to-all-start) | async-done | bytes 2228256 | tf_op jit(solution)/shard_map/all_to_all | solution.py:282
  41.0 1.3 sample.1.own_ref
  42.4 2.0 %collective-permute-start.2 = (f32[1024,256]{1,0:T(8,128)S(1)}, f32[1024,256]{1,0:T(8,128)S(1)}, u32[]{:S(2)}, u32[]{:S(2)}) collective-permute-start(f32[1024,256]{1,0:T(8,128)S(1)} %sample.1.own_ref), channel_id=1, source_target_pairs={{0,2},{1,3},{2,4},{3,5},{4,6},{5,7},{6,8},{7,9},{8,10},{9,11},{10,... | collective-permute-start | bytes 3145736 | tf_op jit(solution)/shard_map/ppermute | solution.py:31
  44.4 4.0 %collective-permute-start.1 = (f32[1024,256]{1,0:T(8,128)S(1)}, f32[1024,256]{1,0:T(8,128)S(1)}, u32[]{:S(2)}, u32[]{:S(2)}) collective-permute-start(f32[1024,256]{1,0:T(8,128)S(1)} %sample.1.own_ref), channel_id=1, source_target_pairs={{0,14},{1,15},{2,0},{3,1},{4,2},{5,3},{6,4},{7,5},{8,6},{9,7},{10,... | collective-permute-start | bytes 3145736 | tf_op jit(solution)/shard_map/ppermute | solution.py:31
  48.4 0.2 collective-permute-start
  48.6 22.7 %collective-permute-done.2.down_ref = f32[1024,256]{1,0:T(8,128)S(1)} collective-permute-done((f32[1024,256]{1,0:T(8,128)S(1)}, f32[1024,256]{1,0:T(8,128)S(1)}, u32[]{:S(2)}, u32[]{:S(2)}) %collective-permute-start.2) | collective-permute-done | bytes 1048608 | tf_op jit(solution)/shard_map/ppermute | solution.py:31
  71.3 2.0 %collective-permute-start.13 = (f32[1024,256]{1,0:T(8,128)S(1)}, f32[1024,256]{1,0:T(8,128)}, u32[]{:S(2)}, u32[]{:S(2)}) collective-permute-start(f32[1024,256]{1,0:T(8,128)S(1)} %collective-permute-done.2.down_ref), channel_id=1, source_target_pairs={{0,1},{1,0},{2,3},{3,2},{4,5},{5,4},{6,7},{7,6},{16,17},{17,16},{1... | collective-permute-start | bytes 3145736 | tf_op jit(solution)/shard_map/ppermute | solution.py:31
  73.3 0.1 collective-permute-start.15
  73.4 4.5 %collective-permute-start.14 = (f32[1024,256]{1,0:T(8,128)S(1)}, f32[1024,256]{1,0:T(8,128)}, u32[]{:S(2)}, u32[]{:S(2)}) collective-permute-start(f32[1024,256]{1,0:T(8,128)S(1)} %collective-permute-done.1.up_ref), channel_id=1, source_target_pairs={{0,15},{1,14},{2,0},{3,1},{4,2},{5,3},{6,4},{7,5},{8,6},{9,7},{10,... | collective-permute-start | bytes 3145736 | tf_op jit(solution)/shard_map/ppermute | solution.py:31
  78.0 5.0 %early_blocks.1 = (f32[8,128,256]{2,1,0:T(8,128)S(1)}, f32[8,128,256]{2,1,0:T(8,128)S(1)}) custom-call(s32[1]{0:T(128)} %bitcast.1.refs_0_.core_ref, f32[1024,256]{1,0:T(8,128)S(1)} %sample.1.own_ref, f32[1024,256]{1,0:T(8,128)S(1)} %collective-permute-done.beside_ref, f32[1024,256]{1,0:T(8,128)S(1)} %collective-permute-done.1.up_ref, ...), custom_call_target="tpu_custom_call" | custom-call | flops 1000 | bytes 2 | tf_op jit(solution)/shard_map/early_blocks/pallas_call | solution.py:260
  83.0 0.9 fusion.4
  84.0 0.2 copy-done.2
  84.2 0.0 collective-permute-start.3
  84.2 0.5 collective-permute-start.4
  84.7 1.4 collective-permute-done.3
  86.0 0.1 collective-permute-start.5
  86.2 0.0 collective-permute-done.4
  86.2 0.4 collective-permute-start.6
  86.6 0.1 pad_add_fusion.flags_ref
  86.6 1.3 collective-permute-done.5
  87.9 0.4 collective-permute-done.6
  88.3 1.6 %maximum_add_fusion = f32[8,128,256]{2,1,0:T(8,128)S(1)} fusion(f32[8,128,256]{2,1,0:T(8,128)} %copy-done.2, f32[2,128,256]{2,1,0:T(8,128)} %collective-permute-done.6, f32[2,128,256]{2,1,0:T(8,128)} %collective-permute-done.5, f32[2,128,256]{2,1,0:T(8,128)} %collective-permute-done.4, f32[2,128,256]{2,1,0:T(8,128)S(1)} %collective-permute-done.3), kind=kLoop, calls=%fused_computation | loop fusion | flops 1048576 | bytes 3145728 | tf_op jit(solution)/shard_map/add | solution.py:294
  90.0 0.1 dynamic-slice_bitcast_fusion.2
  90.0 2.5 %collective-permute-start.7 = (f32[2,128,256]{2,1,0:T(8,128)S(1)}, f32[2,128,256]{2,1,0:T(8,128)S(1)}, u32[]{:S(2)}, u32[]{:S(2)}) collective-permute-start(f32[2,128,256]{2,1,0:T(8,128)S(1)} %get-tuple-element.13), channel_id=1, source_target_pairs={{0,32},{1,33},{2,34},{3,35},{4,36},{5,37},{6,38},{7,39},{8,40},{9,... | collective-permute-start | bytes 786440 | tf_op jit(solution)/shard_map/ppermute | solution.py:31
  92.5 2.8 %collective-permute-start.8 = (f32[2,128,256]{2,1,0:T(8,128)S(1)}, f32[2,128,256]{2,1,0:T(8,128)S(1)}, u32[]{:S(2)}, u32[]{:S(2)}) collective-permute-start(f32[2,128,256]{2,1,0:T(8,128)S(1)} %get-tuple-element.15), channel_id=1, source_target_pairs={{0,64},{1,65},{2,66},{3,67},{4,68},{5,69},{6,70},{7,71},{8,72},{9,... | collective-permute-start | bytes 786440 | tf_op jit(solution)/shard_map/ppermute | solution.py:31
  95.3 2.1 %collective-permute-done.13.down_beside_ref = f32[1024,256]{1,0:T(8,128)} collective-permute-done((f32[1024,256]{1,0:T(8,128)S(1)}, f32[1024,256]{1,0:T(8,128)}, u32[]{:S(2)}, u32[]{:S(2)}) %collective-permute-start.13) | collective-permute-done | bytes 1048608 | tf_op jit(solution)/shard_map/ppermute | solution.py:31
  97.4 4.7 %collective-permute-start.9 = (f32[2,128,256]{2,1,0:T(8,128)S(1)}, f32[2,128,256]{2,1,0:T(8,128)S(1)}, u32[]{:S(2)}, u32[]{:S(2)}) collective-permute-start(f32[2,128,256]{2,1,0:T(8,128)S(1)} %get-tuple-element.14), channel_id=1, source_target_pairs={{0,96},{1,97},{2,98},{3,99},{4,100},{5,101},{6,102},{7,103},{8,104... | collective-permute-start | bytes 786440 | tf_op jit(solution)/shard_map/ppermute | solution.py:31
  102.1 6.4 %late_blocks.1 = (f32[8,64,256]{2,1,0:T(8,128)S(1)}, f32[8,64,256]{2,1,0:T(8,128)S(1)}) custom-call(s32[2]{0:T(128)S(1)} %pad_add_fusion.flags_ref, f32[1024,256]{1,0:T(8,128)S(1)} %sample.1.own_ref, f32[1024,256]{1,0:T(8,128)S(1)} %copy-done.1, f32[1024,256]{1,0:T(8,128)S(1)} %collective-permute-done.1.up_ref, ...), custom_call_target="tpu_custom_call" | custom-call | flops 40000000000 | bytes 100000000 | tf_op jit(solution)/shard_map/late_blocks/pallas_call | solution.py:260
  108.5 0.1 collective-permute-start.16
  108.7 0.1 fusion.1
  108.8 3.8 %collective-permute-start.10 = (f32[128,256]{1,0:T(8,128)S(1)}, f32[128,256]{1,0:T(8,128)S(1)}, u32[]{:S(2)}, u32[]{:S(2)}) collective-permute-start(f32[128,256]{1,0:T(8,128)S(1)} %select_bitcast_fusion), channel_id=1, source_target_pairs={{0,128},{1,129},{2,130},{3,131},{4,132},{5,133},{6,134},{7,135},{8... | collective-permute-start | bytes 393224 | tf_op jit(solution)/shard_map/ppermute | solution.py:31
  112.6 0.9 add.95
  113.5 6.0 %all-to-all-start.1 = ((f32[8,64,256]{2,1,0:T(8,128)}), f32[8,64,256]{2,1,0:T(8,128)S(1)}, u32[]{:S(2)}, u32[]{:S(2)}) async-start(f32[8,64,256]{2,1,0:T(8,128)} %add.95), calls=%async_computation.1 | async-start | bytes 1048576 | tf_op jit(solution)/shard_map/all_to_all | solution.py:322
  119.5 0.1 collective-permute-start.11
  119.6 1.2 collective-permute-done.11
  120.9 7.4 %all-to-all-done.1 = f32[8,64,256]{2,1,0:T(8,128)S(1)} async-done(((f32[8,64,256]{2,1,0:T(8,128)}), f32[8,64,256]{2,1,0:T(8,128)S(1)}, u32[]{:S(2)}, u32[]{:S(2)}) %all-to-all-start.1) | async-done | bytes 524320 | tf_op jit(solution)/shard_map/all_to_all | solution.py:322
  128.4 0.1 collective-permute-start.17
  128.5 6.8 %collective-permute-start.12 = (f32[128,256]{1,0:T(8,128)S(1)}, f32[128,256]{1,0:T(8,128)S(1)}, u32[]{:S(2)}, u32[]{:S(2)}) collective-permute-start(f32[128,256]{1,0:T(8,128)S(1)} %maximum_select_fusion), channel_id=1, source_target_pairs={{0,32},{1,49},{2,66},{3,83},{4,100},{5,117},{6,134},{7,151},{8,168... | collective-permute-start | bytes 393224 | tf_op jit(solution)/shard_map/ppermute | solution.py:31
  135.3 4.2 %collective-permute-start.18 = (f32[128,256]{1,0:T(8,128)S(1)}, f32[128,256]{1,0:T(8,128)S(1)}, u32[]{:S(2)}, u32[]{:S(2)}) collective-permute-start(f32[128,256]{1,0:T(8,128)S(1)} %pad_maximum_fusion.1), channel_id=1, source_target_pairs={{0,65},{1,80},{2,99},{3,114},{4,133},{5,148},{6,167},{7,182},{8,21... | collective-permute-start | bytes 393224 | tf_op jit(solution)/shard_map/ppermute | solution.py:31
  139.6 0.7 collective-permute-start.19
  140.2 1.3 collective-permute-start.20
  141.6 0.6 dynamic_slice.16
  142.2 4.9 %collective-permute-done.18 = f32[128,256]{1,0:T(8,128)S(1)} collective-permute-done((f32[128,256]{1,0:T(8,128)S(1)}, f32[128,256]{1,0:T(8,128)S(1)}, u32[]{:S(2)}, u32[]{:S(2)}) %collective-permute-start.18) | collective-permute-done | bytes 131104 | tf_op jit(solution)/shard_map/ppermute | solution.py:31
  147.0 4.6 %collective-permute-done.20 = f32[128,256]{1,0:T(8,128)S(1)} collective-permute-done((f32[128,256]{1,0:T(8,128)S(1)}, f32[128,256]{1,0:T(8,128)S(1)}, u32[]{:S(2)}, u32[]{:S(2)}) %collective-permute-start.20) | collective-permute-done | bytes 131104 | tf_op jit(solution)/shard_map/ppermute | solution.py:31
  151.7 0.1 copy.5
  151.8 1.3 fusion.2
  (30 shorter events, 0.2 us)
Async XLA Ops:
  4.4 36.7 %all-to-all-start = ((f32[16,136,256]{2,1,0:T(8,128)}), f32[16,136,256]{2,1,0:T(8,128)S(1)}, u32[]{:S(2)}, u32[]{:S(2)}) async-start(f32[16,136,256]{2,1,0:T(8,128)} %mix_slices.1), calls=%async_computation | async-start | bytes 4456448 | tf_op jit(solution)/shard_map/all_to_all | solution.py:282
  42.4 28.9 %collective-permute-start.2 = (f32[1024,256]{1,0:T(8,128)S(1)}, f32[1024,256]{1,0:T(8,128)S(1)}, u32[]{:S(2)}, u32[]{:S(2)}) collective-permute-start(f32[1024,256]{1,0:T(8,128)S(1)} %sample.1.own_ref), channel_id=1, source_target_pairs={{0,2},{1,3},{2,4},{3,5},{4,6},{5,7},{6,8},{7,9},{8,10},{9,11},{10,... | collective-permute-start | bytes 3145736 | tf_op jit(solution)/shard_map/ppermute | solution.py:31
  44.4 29.0 %collective-permute-start.1 = (f32[1024,256]{1,0:T(8,128)S(1)}, f32[1024,256]{1,0:T(8,128)S(1)}, u32[]{:S(2)}, u32[]{:S(2)}) collective-permute-start(f32[1024,256]{1,0:T(8,128)S(1)} %sample.1.own_ref), channel_id=1, source_target_pairs={{0,14},{1,15},{2,0},{3,1},{4,2},{5,3},{6,4},{7,5},{8,6},{9,7},{10,... | collective-permute-start | bytes 3145736 | tf_op jit(solution)/shard_map/ppermute | solution.py:31
  48.4 29.6 %collective-permute-start = (f32[1024,256]{1,0:T(8,128)S(1)}, f32[1024,256]{1,0:T(8,128)S(1)}, u32[]{:S(2)}, u32[]{:S(2)}) collective-permute-start(f32[1024,256]{1,0:T(8,128)S(1)} %sample.1.own_ref), channel_id=1, source_target_pairs={{0,1},{1,0},{2,3},{3,2},{4,5},{5,4},{6,7},{7,6},{8,9},{9,8},{10,11... | collective-permute-start | bytes 3145736 | tf_op jit(solution)/shard_map/ppermute | solution.py:31
  71.3 26.1 %collective-permute-start.13 = (f32[1024,256]{1,0:T(8,128)S(1)}, f32[1024,256]{1,0:T(8,128)}, u32[]{:S(2)}, u32[]{:S(2)}) collective-permute-start(f32[1024,256]{1,0:T(8,128)S(1)} %collective-permute-done.2.down_ref), channel_id=1, source_target_pairs={{0,1},{1,0},{2,3},{3,2},{4,5},{5,4},{6,7},{7,6},{16,17},{17,16},{1... | collective-permute-start | bytes 3145736 | tf_op jit(solution)/shard_map/ppermute | solution.py:31
  73.3 28.8 %collective-permute-start.15 = (f32[1024,256]{1,0:T(8,128)S(1)}, f32[1024,256]{1,0:T(8,128)}, u32[]{:S(2)}, u32[]{:S(2)}) collective-permute-start(f32[1024,256]{1,0:T(8,128)S(1)} %collective-permute-done.2.down_ref), channel_id=1, source_target_pairs={{0,2},{1,3},{2,4},{3,5},{4,6},{5,7},{6,8},{7,9},{8,10},{9,11},{10,... | collective-permute-start | bytes 3145736 | tf_op jit(solution)/shard_map/ppermute | solution.py:31
  73.4 28.7 %collective-permute-start.14 = (f32[1024,256]{1,0:T(8,128)S(1)}, f32[1024,256]{1,0:T(8,128)}, u32[]{:S(2)}, u32[]{:S(2)}) collective-permute-start(f32[1024,256]{1,0:T(8,128)S(1)} %collective-permute-done.1.up_ref), channel_id=1, source_target_pairs={{0,15},{1,14},{2,0},{3,1},{4,2},{5,3},{6,4},{7,5},{8,6},{9,7},{10,... | collective-permute-start | bytes 3145736 | tf_op jit(solution)/shard_map/ppermute | solution.py:31
  78.0 6.0 %copy-start = (f32[1024,256]{1,0:T(8,128)}, f32[1024,256]{1,0:T(8,128)S(1)}, u32[]{:S(2)}) copy-start(f32[1024,256]{1,0:T(8,128)S(1)} %collective-permute-done.beside_ref) | copy-start | bytes 3145732
  83.0 1.2 copy-start.2
  84.2 1.9 %collective-permute-start.3 = (f32[2,128,256]{2,1,0:T(8,128)S(1)}, f32[2,128,256]{2,1,0:T(8,128)S(1)}, u32[]{:S(2)}, u32[]{:S(2)}) collective-permute-start(f32[2,128,256]{2,1,0:T(8,128)S(1)} %get-tuple-element.16), channel_id=1, source_target_pairs={{0,16},{1,17},{2,18},{3,19},{4,20},{5,21},{6,22},{7,23},{8,24},{9,... | collective-permute-start | bytes 786440 | tf_op jit(solution)/shard_map/ppermute | solution.py:31
  84.2 2.0 %collective-permute-start.4 = (f32[2,128,256]{2,1,0:T(8,128)S(1)}, f32[2,128,256]{2,1,0:T(8,128)}, u32[]{:S(2)}, u32[]{:S(2)}) collective-permute-start(f32[2,128,256]{2,1,0:T(8,128)S(1)} %get-tuple-element.19), channel_id=1, source_target_pairs={{0,16},{1,17},{2,18},{3,19},{4,20},{5,21},{6,22},{7,23},{8,24},{9,... | collective-permute-start | bytes 786440 | tf_op jit(solution)/shard_map/ppermute | solution.py:31
  86.0 1.9 %collective-permute-start.5 = (f32[2,128,256]{2,1,0:T(8,128)}, f32[2,128,256]{2,1,0:T(8,128)}, u32[]{:S(2)}, u32[]{:S(2)}) collective-permute-start(f32[2,128,256]{2,1,0:T(8,128)} %get-tuple-element.18), channel_id=1, source_target_pairs={{0,16},{1,17},{2,18},{3,19},{4,20},{5,21},{6,22},{7,23},{8,24},{9,... | collective-permute-start | bytes 786440 | tf_op jit(solution)/shard_map/ppermute | solution.py:31
  86.2 2.1 %collective-permute-start.6 = (f32[2,128,256]{2,1,0:T(8,128)}, f32[2,128,256]{2,1,0:T(8,128)}, u32[]{:S(2)}, u32[]{:S(2)}) collective-permute-start(f32[2,128,256]{2,1,0:T(8,128)} %get-tuple-element.17), channel_id=1, source_target_pairs={{0,16},{1,17},{2,18},{3,19},{4,20},{5,21},{6,22},{7,23},{8,24},{9,... | collective-permute-start | bytes 786440 | tf_op jit(solution)/shard_map/ppermute | solution.py:31
  88.3 13.8 %copy-start.1 = (f32[1024,256]{1,0:T(8,128)S(1)}, f32[1024,256]{1,0:T(8,128)}, u32[]{:S(2)}) copy-start(f32[1024,256]{1,0:T(8,128)} %copy-done) | copy-start | bytes 3145732
  90.0 18.6 %collective-permute-start.7 = (f32[2,128,256]{2,1,0:T(8,128)S(1)}, f32[2,128,256]{2,1,0:T(8,128)S(1)}, u32[]{:S(2)}, u32[]{:S(2)}) collective-permute-start(f32[2,128,256]{2,1,0:T(8,128)S(1)} %get-tuple-element.13), channel_id=1, source_target_pairs={{0,32},{1,33},{2,34},{3,35},{4,36},{5,37},{6,38},{7,39},{8,40},{9,... | collective-permute-start | bytes 786440 | tf_op jit(solution)/shard_map/ppermute | solution.py:31
  92.5 16.2 %collective-permute-start.8 = (f32[2,128,256]{2,1,0:T(8,128)S(1)}, f32[2,128,256]{2,1,0:T(8,128)S(1)}, u32[]{:S(2)}, u32[]{:S(2)}) collective-permute-start(f32[2,128,256]{2,1,0:T(8,128)S(1)} %get-tuple-element.15), channel_id=1, source_target_pairs={{0,64},{1,65},{2,66},{3,67},{4,68},{5,69},{6,70},{7,71},{8,72},{9,... | collective-permute-start | bytes 786440 | tf_op jit(solution)/shard_map/ppermute | solution.py:31
  97.4 11.3 %collective-permute-start.9 = (f32[2,128,256]{2,1,0:T(8,128)S(1)}, f32[2,128,256]{2,1,0:T(8,128)S(1)}, u32[]{:S(2)}, u32[]{:S(2)}) collective-permute-start(f32[2,128,256]{2,1,0:T(8,128)S(1)} %get-tuple-element.14), channel_id=1, source_target_pairs={{0,96},{1,97},{2,98},{3,99},{4,100},{5,101},{6,102},{7,103},{8,104... | collective-permute-start | bytes 786440 | tf_op jit(solution)/shard_map/ppermute | solution.py:31
  108.5 4.0 %collective-permute-start.16 = (f32[8,64,256]{2,1,0:T(8,128)S(1)}, f32[8,64,256]{2,1,0:T(8,128)S(1)}, u32[]{:S(2)}, u32[]{:S(2)}) collective-permute-start(f32[8,64,256]{2,1,0:T(8,128)S(1)} %get-tuple-element.12), channel_id=1, source_target_pairs={{0,16},{1,17},{2,18},{3,19},{4,20},{5,21},{6,22},{7,23},{8,24},{9,... | collective-permute-start | bytes 1572872 | tf_op jit(solution)/shard_map/ppermute | solution.py:31
  108.8 10.7 %collective-permute-start.10 = (f32[128,256]{1,0:T(8,128)S(1)}, f32[128,256]{1,0:T(8,128)S(1)}, u32[]{:S(2)}, u32[]{:S(2)}) collective-permute-start(f32[128,256]{1,0:T(8,128)S(1)} %select_bitcast_fusion), channel_id=1, source_target_pairs={{0,128},{1,129},{2,130},{3,131},{4,132},{5,133},{6,134},{7,135},{8... | collective-permute-start | bytes 393224 | tf_op jit(solution)/shard_map/ppermute | solution.py:31
  112.6 29.0 %copy-start.3 = (pred[256]{0:T(512)(128)(4,1)S(1)}, pred[256]{0:T(512)(128)(4,1)}, u32[]{:S(2)}) copy-start(pred[256]{0:T(512)(128)(4,1)} %constant.72.clone) | copy-start | bytes 772
  113.5 14.9 %all-to-all-start.1 = ((f32[8,64,256]{2,1,0:T(8,128)}), f32[8,64,256]{2,1,0:T(8,128)S(1)}, u32[]{:S(2)}, u32[]{:S(2)}) async-start(f32[8,64,256]{2,1,0:T(8,128)} %add.95), calls=%async_computation.1 | async-start | bytes 1048576 | tf_op jit(solution)/shard_map/all_to_all | solution.py:322
  119.5 1.3 collective-permute-start.11
  128.4 6.9 %collective-permute-start.17 = (f32[64,256]{1,0:T(8,128)S(1)}, f32[64,256]{1,0:T(8,128)S(1)}, u32[]{:S(2)}, u32[]{:S(2)}) collective-permute-start(f32[64,256]{1,0:T(8,128)S(1)} %reduce_sum.9), channel_id=1, source_target_pairs={{0,16},{1,17},{2,18},{3,19},{4,20},{5,21},{6,22},{7,23},{8,24},{9,... | collective-permute-start | bytes 196616 | tf_op jit(solution)/shard_map/ppermute | solution.py:31
  128.5 13.7 %collective-permute-start.12 = (f32[128,256]{1,0:T(8,128)S(1)}, f32[128,256]{1,0:T(8,128)S(1)}, u32[]{:S(2)}, u32[]{:S(2)}) collective-permute-start(f32[128,256]{1,0:T(8,128)S(1)} %maximum_select_fusion), channel_id=1, source_target_pairs={{0,32},{1,49},{2,66},{3,83},{4,100},{5,117},{6,134},{7,151},{8,168... | collective-permute-start | bytes 393224 | tf_op jit(solution)/shard_map/ppermute | solution.py:31
  135.3 11.7 %collective-permute-start.18 = (f32[128,256]{1,0:T(8,128)S(1)}, f32[128,256]{1,0:T(8,128)S(1)}, u32[]{:S(2)}, u32[]{:S(2)}) collective-permute-start(f32[128,256]{1,0:T(8,128)S(1)} %pad_maximum_fusion.1), channel_id=1, source_target_pairs={{0,65},{1,80},{2,99},{3,114},{4,133},{5,148},{6,167},{7,182},{8,21... | collective-permute-start | bytes 393224 | tf_op jit(solution)/shard_map/ppermute | solution.py:31
  139.6 7.5 %collective-permute-start.19 = (f32[128,256]{1,0:T(8,128)S(1)}, f32[128,256]{1,0:T(8,128)S(1)}, u32[]{:S(2)}, u32[]{:S(2)}) collective-permute-start(f32[128,256]{1,0:T(8,128)S(1)} %maximum_select_fusion), channel_id=1, source_target_pairs={{32,32},{33,49},{34,66},{35,83},{36,100},{37,117},{38,134},{39,151... | collective-permute-start | bytes 393224 | tf_op jit(solution)/shard_map/ppermute | solution.py:31
  140.2 11.4 %collective-permute-start.20 = (f32[128,256]{1,0:T(8,128)S(1)}, f32[128,256]{1,0:T(8,128)S(1)}, u32[]{:S(2)}, u32[]{:S(2)}) collective-permute-start(f32[128,256]{1,0:T(8,128)S(1)} %pad_maximum_fusion.1), channel_id=1, source_target_pairs={{32,65},{33,80},{34,99},{35,114},{36,133},{37,148},{38,167},{39,18... | collective-permute-start | bytes 393224 | tf_op jit(solution)/shard_map/ppermute | solution.py:31

commit v3 on v2

--- a/solution.py
+++ b/solution.py
@@ -169,12 +169,12 @@
     return (row[0] // 4, row[0] % 4, row[1], col[0], col[1]), mirror
 
 
-def mirrored():
-    table = np.zeros(SIZES, bool)
+def arrivals():
+    table = np.zeros(SIZES, np.int32)
     for here in itertools.product(*[range(s) for s in SIZES]):
         for late in (False, True):
             there, mirror = home(late, *here)
-            table[there] = mirror
+            table[there] = 2 * late + mirror
     return table.reshape(-1)
 
 
@@ -232,35 +232,44 @@
         send_ref[unit, 64:, :] = jnp.zeros((64, 256), F32)
 
 
-def late_kernel(
-    flags_ref, own_ref, beside_ref, up_ref, down_ref, down_beside_ref, up2_ref, down2_ref, keep_ref, send_ref, pick_ref
-):
+def late_kernel(flags_ref, own_ref, beside_ref, up_ref, down_ref, down_beside_ref, up2_ref, down2_ref, keep_ref, send_ref, buf, sem):
     core, low = flags_ref[0], flags_ref[1]
 
-    def pick(a_ref, b_ref):
-        @pl.when(low == 1)
-        def _():
-            pick_ref[...] = a_ref[...]
-
-        @pl.when(low == 0)
-        def _():
-            pick_ref[...] = b_ref[...]
-
-        return halves(pick_ref)
-
-    up2, down2 = turned(halves(up2_ref)), halves(down2_ref)
-    put_block(core, block(up2, pick(beside_ref, own_ref)), 0, keep_ref, send_ref)
-    put_block(core, block(turned(halves(up_ref)), down2), 1, keep_ref, send_ref)
-    put_block(core, block(up2, pick(down_beside_ref, down_ref)), 2, keep_ref, send_ref)
+    def load(k, ref):
+        return pltpu.make_async_copy(ref, buf.at[k], sem.at[k])
+
+    for k, ref in enumerate((up2_ref, down2_ref, up_ref)):
+        load(k, ref).start()
+
+    @pl.when(low == 1)
+    def _():
+        load(3, down_beside_ref).start()
+        load(4, beside_ref).start()
+
+    @pl.when(low == 0)
+    def _():
+        load(3, down_ref).start()
+        load(4, own_ref).start()
+
+    load(0, up2_ref).wait()
+    up2 = turned(halves(buf.at[0]))
+    load(1, down2_ref).wait()
+    down2 = halves(buf.at[1])
     put_block(core, block(up2, down2), 3, keep_ref, send_ref)
-
-
-def call_blocks(kernel, rows, flags, operands, scratch, cost, name):
+    load(2, up_ref).wait()
+    put_block(core, block(turned(halves(buf.at[2])), down2), 1, keep_ref, send_ref)
+    load(3, down_ref).wait()
+    put_block(core, block(up2, halves(buf.at[3])), 2, keep_ref, send_ref)
+    load(4, own_ref).wait()
+    put_block(core, block(up2, halves(buf.at[4])), 0, keep_ref, send_ref)
+
+
+def call_blocks(kernel, rows, flags, operands, space, scratch, cost, name):
     vmem = pl.BlockSpec(memory_space=pltpu.VMEM)
     return pl.pallas_call(
         kernel,
         out_shape=[jax.ShapeDtypeStruct((8, rows, 256), F32)] * 2,
-        in_specs=[pl.BlockSpec(memory_space=pltpu.SMEM)] + [vmem] * len(operands),
+        in_specs=[pl.BlockSpec(memory_space=pltpu.SMEM)] + [pl.BlockSpec(memory_space=space)] * len(operands),
         out_specs=[vmem] * 2,
         scratch_shapes=scratch,
         compiler_params=pltpu.CompilerParams(vmem_limit_bytes=20 << 20),
@@ -290,7 +299,7 @@
     down_beside = permute(down, lambda xh, y, c, z, x: (xh, y, c, z, x + 1) if z < 4 else None)
 
     core_flag = core.reshape(1)
-    keep, send = call_blocks(early_kernel, 128, core_flag, (own, beside, up, down), [], 1000, "early_blocks")
+    keep, send = call_blocks(early_kernel, 128, core_flag, (own, beside, up, down), pltpu.VMEM, [], 1000, "early_blocks")
     early = keep + jnp.concatenate([other_core(send[2 * i : 2 * i + 2]) for i in range(4)])
     early = early.reshape(2, 4, 128, 256)
     row = lax.axis_index("y")
@@ -303,19 +312,14 @@
         got = other_core(mine)
         return jnp.concatenate([jnp.where(core == 0, mine, got), jnp.where(core == 0, got, mine)])
 
-    def deliver(piece, late):
-        def route(half):
-            return lambda *here: home(late, *here)[0] if here[1] % 2 == half else None
-
-        return permute(piece, route(0)), permute(piece, route(1))
-
     flags = jnp.stack([core, (z < 4).astype(jnp.int32)])
     keep, send = call_blocks(
         late_kernel,
         64,
         flags,
         (own, beside, up, down, down_beside, up2, down2),
-        [pltpu.VMEM(own.shape, F32)],
+        pl.ANY,
+        [pltpu.VMEM((5, *own.shape), F32), pltpu.SemaphoreType.DMA((5,))],
         40_000_000_000,
         "late_blocks",
     )
@@ -324,11 +328,21 @@
     early = jnp.where(plane == 0, total[0], total[1]) + permute(
         jnp.where(plane == 0, total[1], total[0]), lambda xh, y, c, z, x: (xh + 1, y, c, z, x)
     )
-    early = deliver(jnp.where(chip >= 6, early, by_core(early[:64])), False)
-    late = jnp.sum(slots, axis=0)
-    late = deliver(by_core(late), True)
-    whole = jnp.concatenate([a + b for a, b in zip(early, late)])
-    return jnp.where(jnp.asarray(mirrored())[lax.axis_index(NAMES)], whole.T, whole)
+    got, rest = [], early[:64]
+    for part in range(2):
+        got.append(other_core(rest[part * 32 : part * 32 + 32]))
+        got[-1], rest = lax.optimization_barrier((got[-1], rest))
+    got, rest = jnp.concatenate(got), early[:64]
+    both = jnp.concatenate([jnp.where(core == 0, rest, got), jnp.where(core == 0, got, rest)])
+    early = jnp.where(chip >= 6, early, both)
+    late = by_core(jnp.sum(slots, axis=0))
+    even = chip % 2 == 0
+    first = permute(jnp.where(even, early, late), lambda *here: home(here[1] % 2 == 1, *here)[0])
+    second = permute(jnp.where(even, late, early), lambda *here: home(here[1] % 2 == 0, *here)[0])
+    kind = jnp.asarray(arrivals())[lax.axis_index(NAMES)]
+    swap = kind >= 2
+    whole = jnp.concatenate([jnp.where(swap, second, first), jnp.where(swap, first, second)])
+    return jnp.where(kind % 2 == 1, whole.T, whole)
 
 
 def solution(mesh):

time: 154 us -> 151 us (0.981)
  starting transfers between devices: 54.4 us -> 48 us
  between operations: 0.31 us -> 2.89 us
  waiting for transfers between devices: 75.2 us -> 76.9 us
    ppermute x21 -> x20, starting transfers between devices: 40.9 us -> 35.4 us  [permute(): return lax.ppermute(block, NAMES, pairs)]
    ppermute x21 -> x20, waiting for transfers between devices: 38.6 us -> 41.2 us  [permute(): return lax.ppermute(block, NAMES, pairs)]
  transfers between devices with their start and end apart: 23 -> 22, of which waited for: 10 -> 12; matrix products, arithmetic and copies ran while one was open for 3% -> 3% of each run, Pallas kernels for 7% -> 7%
where the time goes in v3:
time: 151 us; the launch traced here: 150 us
  waiting for transfers between devices  76.9 us (51%)
  starting transfers between devices  48 us (32%)
  Pallas kernels  16.9 us (11%)
  other arithmetic  3.56 us (2%)
  between operations  2.89 us (2%)
  local copies, waits for them, and re-layouts  1.99 us (1%)
    ppermute x20, waiting for transfers between devices, permute(): return lax.ppermute(block, NAMES, pairs)  41.2 us
    ppermute x20, starting transfers between devices, permute(): return lax.ppermute(block, NAMES, pairs)  35.4 us
    all_to_all x1, waiting for transfers between devices, shards(): slices = lax.all_to_all(slices, ROW, 0, 0, tiled=True)  29.2 us
    pallas_call x2, Pallas kernels, call_blocks(): pl.pallas_call(kernel, out_shape=[jax.ShapeDtypeStruct((8, rows, 256), F3...  11.1 us
    all_to_all x1, starting transfers between devices, shards(): slices = lax.all_to_all(slices, ROW, 0, 0, tiled=True)  7.46 us
    all_to_all x1, waiting for transfers between devices, shards(): slots = lax.all_to_all(keep + other_core(send), CHIPS, 0, 0, tiled=True)  6.43 us
    all_to_all x1, starting transfers between devices, shards(): slots = lax.all_to_all(keep + other_core(send), CHIPS, 0, 0, tiled=True)  5.08 us
    pallas_call x1, Pallas kernels, mix_slices(): pl.pallas_call(mix_kernel, out_shape=pltpu.HBM(shape, F32), in_specs=[vme...  4.46 us
  transfers between devices with their start and end apart: 22, of which 12 were waited for; matrix products, arithmetic and copies ran while one was open for 3% of the time, Pallas kernels for 7%

profile of v3, /device:TPU:6, one launch (start us, length us, event | category | flops | bytes accessed | tf_op | source)
XLA Modules:
  0.0 150.1 jit_solution(17406167248140673586)
XLA Ops:
  0.0 4.5 %mix_slices.1 = f32[16,136,256]{2,1,0:T(8,128)} custom-call(s32[16,128]{1,0:T(8,128)} %bitcast.28, s32[8,128]{1,0:T(8,128)} %bitcast.29, f32[16,128,256]{2,1,0:T(8,128)} %bitcast.27), custom_call_target="tpu_custom_call" | custom-call | tf_op jit(solution)/shard_map/mix_slices/pallas_call | solution.py:87
  4.5 7.5 %all-to-all-start = ((f32[16,136,256]{2,1,0:T(8,128)}), f32[16,136,256]{2,1,0:T(8,128)S(1)}, u32[]{:S(2)}, u32[]{:S(2)}) async-start(f32[16,136,256]{2,1,0:T(8,128)} %mix_slices.1), calls=%async_computation | async-start | bytes 4456448 | tf_op jit(solution)/shard_map/all_to_all | solution.py:291
  11.9 29.2 %all-to-all-done.refs_1_ = f32[16,136,256]{2,1,0:T(8,128)S(1)} async-done(((f32[16,136,256]{2,1,0:T(8,128)}), f32[16,136,256]{2,1,0:T(8,128)S(1)}, u32[]{:S(2)}, u32[]{:S(2)}) %all-to-all-start) | async-done | bytes 2228256 | tf_op jit(solution)/shard_map/all_to_all | solution.py:291
  41.1 1.3 sample.1.own_ref
  42.5 2.0 %collective-permute-start.2 = (f32[1024,256]{1,0:T(8,128)S(1)}, f32[1024,256]{1,0:T(8,128)S(1)}, u32[]{:S(2)}, u32[]{:S(2)}) collective-permute-start(f32[1024,256]{1,0:T(8,128)S(1)} %sample.1.own_ref), channel_id=1, source_target_pairs={{0,2},{1,3},{2,4},{3,5},{4,6},{5,7},{6,8},{7,9},{8,10},{9,11},{10,... | collective-permute-start | bytes 3145736 | tf_op jit(solution)/shard_map/ppermute | solution.py:31
  44.5 4.0 %collective-permute-start.1 = (f32[1024,256]{1,0:T(8,128)S(1)}, f32[1024,256]{1,0:T(8,128)S(1)}, u32[]{:S(2)}, u32[]{:S(2)}) collective-permute-start(f32[1024,256]{1,0:T(8,128)S(1)} %sample.1.own_ref), channel_id=1, source_target_pairs={{0,14},{1,15},{2,0},{3,1},{4,2},{5,3},{6,4},{7,5},{8,6},{9,7},{10,... | collective-permute-start | bytes 3145736 | tf_op jit(solution)/shard_map/ppermute | solution.py:31
  48.5 0.2 collective-permute-start
  48.7 22.7 %collective-permute-done.2.down_ref = f32[1024,256]{1,0:T(8,128)S(1)} collective-permute-done((f32[1024,256]{1,0:T(8,128)S(1)}, f32[1024,256]{1,0:T(8,128)S(1)}, u32[]{:S(2)}, u32[]{:S(2)}) %collective-permute-start.2) | collective-permute-done | bytes 1048608 | tf_op jit(solution)/shard_map/ppermute | solution.py:31
  71.4 2.0 %collective-permute-start.3 = (f32[1024,256]{1,0:T(8,128)S(1)}, f32[1024,256]{1,0:T(8,128)}, u32[]{:S(2)}, u32[]{:S(2)}) collective-permute-start(f32[1024,256]{1,0:T(8,128)S(1)} %collective-permute-done.2.down_ref), channel_id=1, source_target_pairs={{0,1},{1,0},{2,3},{3,2},{4,5},{5,4},{6,7},{7,6},{16,17},{17,16},{1... | collective-permute-start | bytes 3145736 | tf_op jit(solution)/shard_map/ppermute | solution.py:31
  73.4 0.1 collective-permute-start.5
  73.5 4.5 %collective-permute-start.4 = (f32[1024,256]{1,0:T(8,128)S(1)}, f32[1024,256]{1,0:T(8,128)}, u32[]{:S(2)}, u32[]{:S(2)}) collective-permute-start(f32[1024,256]{1,0:T(8,128)S(1)} %collective-permute-done.1.up_ref), channel_id=1, source_target_pairs={{0,15},{1,14},{2,0},{3,1},{4,2},{5,3},{6,4},{7,5},{8,6},{9,7},{10,... | collective-permute-start | bytes 3145736 | tf_op jit(solution)/shard_map/ppermute | solution.py:31
  78.1 5.0 %early_blocks.1 = (f32[8,128,256]{2,1,0:T(8,128)S(1)}, f32[8,128,256]{2,1,0:T(8,128)S(1)}) custom-call(s32[1]{0:T(128)} %bitcast.1.refs_0_.core_ref, f32[1024,256]{1,0:T(8,128)S(1)} %sample.1.own_ref, f32[1024,256]{1,0:T(8,128)S(1)} %collective-permute-done.beside_ref, f32[1024,256]{1,0:T(8,128)S(1)} %collective-permute-done.1.up_ref, ...), custom_call_target="tpu_custom_call" | custom-call | flops 1000 | bytes 2 | tf_op jit(solution)/shard_map/early_blocks/pallas_call | solution.py:269
  83.1 1.0 fusion.6
  84.0 0.2 copy-done.2
  84.2 0.5 collective-permute-start.10
  84.7 1.4 collective-permute-done.11
  86.1 0.1 collective-permute-start.9
  86.3 0.0 collective-permute-done.10
  86.3 0.4 collective-permute-start.8
  86.6 0.1 pad_add_fusion.flags_ref
  86.7 1.3 collective-permute-done.9
  88.0 0.4 collective-permute-done.8
  88.4 1.6 %maximum_add_fusion = f32[8,128,256]{2,1,0:T(8,128)S(1)} fusion(f32[8,128,256]{2,1,0:T(8,128)} %copy-done.2, f32[2,128,256]{2,1,0:T(8,128)S(1)} %collective-permute-done.11, f32[2,128,256]{2,1,0:T(8,128)} %collective-permute-done.10, f32[2,128,256]{2,1,0:T(8,128)} %collective-permute-done.9, f32[2,128,256]{2,1,0:T(8,128)} %collective-permute-done.8), kind=kLoop, calls=%fused_computation | loop fusion | flops 1048576 | bytes 3145728 | tf_op jit(solution)/shard_map/add | solution.py:303
  90.0 0.1 dynamic-slice_bitcast_fusion.2
  90.1 3.8 %collective-permute-start.14 = (f32[2,128,256]{2,1,0:T(8,128)S(1)}, f32[2,128,256]{2,1,0:T(8,128)S(1)}, u32[]{:S(2)}, u32[]{:S(2)}) collective-permute-start(f32[2,128,256]{2,1,0:T(8,128)S(1)} %get-tuple-element.20), channel_id=1, source_target_pairs={{0,96},{1,97},{2,98},{3,99},{4,100},{5,101},{6,102},{7,103},{8,104... | collective-permute-start | bytes 786440 | tf_op jit(solution)/shard_map/ppermute | solution.py:31
  93.9 0.7 collective-permute-start.13
  94.6 2.8 %collective-permute-done.3.down_beside_ref = f32[1024,256]{1,0:T(8,128)} collective-permute-done((f32[1024,256]{1,0:T(8,128)S(1)}, f32[1024,256]{1,0:T(8,128)}, u32[]{:S(2)}, u32[]{:S(2)}) %collective-permute-start.3) | collective-permute-done | bytes 1048608 | tf_op jit(solution)/shard_map/ppermute | solution.py:31
  97.5 2.4 %collective-permute-start.12 = (f32[2,128,256]{2,1,0:T(8,128)S(1)}, f32[2,128,256]{2,1,0:T(8,128)S(1)}, u32[]{:S(2)}, u32[]{:S(2)}) collective-permute-start(f32[2,128,256]{2,1,0:T(8,128)S(1)} %get-tuple-element.19), channel_id=1, source_target_pairs={{0,32},{1,33},{2,34},{3,35},{4,36},{5,37},{6,38},{7,39},{8,40},{9,... | collective-permute-start | bytes 786440 | tf_op jit(solution)/shard_map/ppermute | solution.py:31
  99.9 6.1 %late_blocks.1 = (f32[8,64,256]{2,1,0:T(8,128)S(1)}, f32[8,64,256]{2,1,0:T(8,128)S(1)}) custom-call(s32[2]{0:T(128)S(1)} %pad_add_fusion.flags_ref, f32[1024,256]{1,0:T(8,128)S(1)} %sample.1.own_ref, f32[1024,256]{1,0:T(8,128)S(1)} %copy-done.1, f32[1024,256]{1,0:T(8,128)S(1)} %collective-permute-done.1.up_ref, ...), custom_call_target="tpu_custom_call" | custom-call | flops 40000000000 | bytes 100000000 | tf_op jit(solution)/shard_map/late_blocks/pallas_call | solution.py:269
  105.9 0.1 collective-permute-start.6
  106.1 3.0 %collective-permute-done.12 = f32[2,128,256]{2,1,0:T(8,128)S(1)} collective-permute-done((f32[2,128,256]{2,1,0:T(8,128)S(1)}, f32[2,128,256]{2,1,0:T(8,128)S(1)}, u32[]{:S(2)}, u32[]{:S(2)}) %collective-permute-start.12) | collective-permute-done | bytes 262176 | tf_op jit(solution)/shard_map/ppermute | solution.py:31
  109.1 0.1 fusion.1
  109.2 4.1 %collective-permute-start.15 = (f32[128,256]{1,0:T(8,128)S(1)}, f32[128,256]{1,0:T(8,128)S(1)}, u32[]{:S(2)}, u32[]{:S(2)}) collective-permute-start(f32[128,256]{1,0:T(8,128)S(1)} %select_bitcast_fusion), channel_id=1, source_target_pairs={{0,128},{1,129},{2,130},{3,131},{4,132},{5,133},{6,134},{7,135},{8... | collective-permute-start | bytes 393224 | tf_op jit(solution)/shard_map/ppermute | solution.py:31
  113.2 0.9 add.82
  114.1 5.1 %all-to-all-start.1 = ((f32[8,64,256]{2,1,0:T(8,128)}), f32[8,64,256]{2,1,0:T(8,128)S(1)}, u32[]{:S(2)}, u32[]{:S(2)}) async-start(f32[8,64,256]{2,1,0:T(8,128)} %add.82), calls=%async_computation.1 | async-start | bytes 1048576 | tf_op jit(solution)/shard_map/all_to_all | solution.py:326
  119.2 0.1 collective-permute-start.16
  119.4 1.2 collective-permute-done.16
  120.5 0.2 collective-permute-start.17
  120.7 1.0 collective-permute-done.17
  121.7 6.4 %all-to-all-done.1 = f32[8,64,256]{2,1,0:T(8,128)S(1)} async-done(((f32[8,64,256]{2,1,0:T(8,128)}), f32[8,64,256]{2,1,0:T(8,128)S(1)}, u32[]{:S(2)}, u32[]{:S(2)}) %all-to-all-start.1) | async-done | bytes 524320 | tf_op jit(solution)/shard_map/all_to_all | solution.py:326
  128.2 0.1 collective-permute-start.7
  128.3 1.2 collective-permute-done.7
  129.6 8.2 %collective-permute-start.18 = (f32[128,256]{1,0:T(8,128)S(1)}, f32[128,256]{1,0:T(8,128)S(1)}, u32[]{:S(2)}, u32[]{:S(2)}) collective-permute-start(f32[128,256]{1,0:T(8,128)S(1)} %get-tuple-element.26), channel_id=1, source_target_pairs={{0,65},{1,80},{2,99},{3,114},{4,133},{5,148},{6,167},{7,182},{8,21... | collective-permute-start | bytes 393224 | tf_op jit(solution)/shard_map/ppermute | solution.py:31
  137.8 2.0 %collective-permute-start.19 = (f32[128,256]{1,0:T(8,128)S(1)}, f32[128,256]{1,0:T(8,128)S(1)}, u32[]{:S(2)}, u32[]{:S(2)}) collective-permute-start(f32[128,256]{1,0:T(8,128)S(1)} %get-tuple-element.27), channel_id=1, source_target_pairs={{0,32},{1,49},{2,66},{3,83},{4,100},{5,117},{6,134},{7,151},{8,168... | collective-permute-start | bytes 393224 | tf_op jit(solution)/shard_map/ppermute | solution.py:31
  139.8 0.6 dynamic_slice.16
  143.0 6.2 %collective-permute-done.19 = f32[128,256]{1,0:T(8,128)S(1)} collective-permute-done((f32[128,256]{1,0:T(8,128)S(1)}, f32[128,256]{1,0:T(8,128)S(1)}, u32[]{:S(2)}, u32[]{:S(2)}) %collective-permute-start.19) | collective-permute-done | bytes 131104 | tf_op jit(solution)/shard_map/ppermute | solution.py:31
  149.2 0.1 copy.5
  149.4 0.7 fusion.2
  (30 shorter events, 0.2 us)
Async XLA Ops:
  4.5 36.7 %all-to-all-start = ((f32[16,136,256]{2,1,0:T(8,128)}), f32[16,136,256]{2,1,0:T(8,128)S(1)}, u32[]{:S(2)}, u32[]{:S(2)}) async-start(f32[16,136,256]{2,1,0:T(8,128)} %mix_slices.1), calls=%async_computation | async-start | bytes 4456448 | tf_op jit(solution)/shard_map/all_to_all | solution.py:291
  42.5 28.9 %collective-permute-start.2 = (f32[1024,256]{1,0:T(8,128)S(1)}, f32[1024,256]{1,0:T(8,128)S(1)}, u32[]{:S(2)}, u32[]{:S(2)}) collective-permute-start(f32[1024,256]{1,0:T(8,128)S(1)} %sample.1.own_ref), channel_id=1, source_target_pairs={{0,2},{1,3},{2,4},{3,5},{4,6},{5,7},{6,8},{7,9},{8,10},{9,11},{10,... | collective-permute-start | bytes 3145736 | tf_op jit(solution)/shard_map/ppermute | solution.py:31
  44.5 29.0 %collective-permute-start.1 = (f32[1024,256]{1,0:T(8,128)S(1)}, f32[1024,256]{1,0:T(8,128)S(1)}, u32[]{:S(2)}, u32[]{:S(2)}) collective-permute-start(f32[1024,256]{1,0:T(8,128)S(1)} %sample.1.own_ref), channel_id=1, source_target_pairs={{0,14},{1,15},{2,0},{3,1},{4,2},{5,3},{6,4},{7,5},{8,6},{9,7},{10,... | collective-permute-start | bytes 3145736 | tf_op jit(solution)/shard_map/ppermute | solution.py:31
  48.5 29.6 %collective-permute-start = (f32[1024,256]{1,0:T(8,128)S(1)}, f32[1024,256]{1,0:T(8,128)S(1)}, u32[]{:S(2)}, u32[]{:S(2)}) collective-permute-start(f32[1024,256]{1,0:T(8,128)S(1)} %sample.1.own_ref), channel_id=1, source_target_pairs={{0,1},{1,0},{2,3},{3,2},{4,5},{5,4},{6,7},{7,6},{8,9},{9,8},{10,11... | collective-permute-start | bytes 3145736 | tf_op jit(solution)/shard_map/ppermute | solution.py:31
  71.4 26.1 %collective-permute-start.3 = (f32[1024,256]{1,0:T(8,128)S(1)}, f32[1024,256]{1,0:T(8,128)}, u32[]{:S(2)}, u32[]{:S(2)}) collective-permute-start(f32[1024,256]{1,0:T(8,128)S(1)} %collective-permute-done.2.down_ref), channel_id=1, source_target_pairs={{0,1},{1,0},{2,3},{3,2},{4,5},{5,4},{6,7},{7,6},{16,17},{17,16},{1... | collective-permute-start | bytes 3145736 | tf_op jit(solution)/shard_map/ppermute | solution.py:31
  73.4 26.5 %collective-permute-start.5 = (f32[1024,256]{1,0:T(8,128)S(1)}, f32[1024,256]{1,0:T(8,128)}, u32[]{:S(2)}, u32[]{:S(2)}) collective-permute-start(f32[1024,256]{1,0:T(8,128)S(1)} %collective-permute-done.2.down_ref), channel_id=1, source_target_pairs={{0,2},{1,3},{2,4},{3,5},{4,6},{5,7},{6,8},{7,9},{8,10},{9,11},{10,... | collective-permute-start | bytes 3145736 | tf_op jit(solution)/shard_map/ppermute | solution.py:31
  73.5 26.3 %collective-permute-start.4 = (f32[1024,256]{1,0:T(8,128)S(1)}, f32[1024,256]{1,0:T(8,128)}, u32[]{:S(2)}, u32[]{:S(2)}) collective-permute-start(f32[1024,256]{1,0:T(8,128)S(1)} %collective-permute-done.1.up_ref), channel_id=1, source_target_pairs={{0,15},{1,14},{2,0},{3,1},{4,2},{5,3},{6,4},{7,5},{8,6},{9,7},{10,... | collective-permute-start | bytes 3145736 | tf_op jit(solution)/shard_map/ppermute | solution.py:31
  78.1 6.0 %copy-start = (f32[1024,256]{1,0:T(8,128)}, f32[1024,256]{1,0:T(8,128)S(1)}, u32[]{:S(2)}) copy-start(f32[1024,256]{1,0:T(8,128)S(1)} %collective-permute-done.beside_ref) | copy-start | bytes 3145732
  83.1 1.2 copy-start.2
  84.2 1.9 %collective-permute-start.11 = (f32[2,128,256]{2,1,0:T(8,128)S(1)}, f32[2,128,256]{2,1,0:T(8,128)S(1)}, u32[]{:S(2)}, u32[]{:S(2)}) collective-permute-start(f32[2,128,256]{2,1,0:T(8,128)S(1)} %get-tuple-element.23), channel_id=1, source_target_pairs={{0,16},{1,17},{2,18},{3,19},{4,20},{5,21},{6,22},{7,23},{8,24},{9,... | collective-permute-start | bytes 786440 | tf_op jit(solution)/shard_map/ppermute | solution.py:31
  84.2 2.0 %collective-permute-start.10 = (f32[2,128,256]{2,1,0:T(8,128)S(1)}, f32[2,128,256]{2,1,0:T(8,128)}, u32[]{:S(2)}, u32[]{:S(2)}) collective-permute-start(f32[2,128,256]{2,1,0:T(8,128)S(1)} %get-tuple-element.24), channel_id=1, source_target_pairs={{0,16},{1,17},{2,18},{3,19},{4,20},{5,21},{6,22},{7,23},{8,24},{9,... | collective-permute-start | bytes 786440 | tf_op jit(solution)/shard_map/ppermute | solution.py:31
  86.1 1.9 %collective-permute-start.9 = (f32[2,128,256]{2,1,0:T(8,128)}, f32[2,128,256]{2,1,0:T(8,128)}, u32[]{:S(2)}, u32[]{:S(2)}) collective-permute-start(f32[2,128,256]{2,1,0:T(8,128)} %get-tuple-element.25), channel_id=1, source_target_pairs={{0,16},{1,17},{2,18},{3,19},{4,20},{5,21},{6,22},{7,23},{8,24},{9,... | collective-permute-start | bytes 786440 | tf_op jit(solution)/shard_map/ppermute | solution.py:31
  86.3 2.1 %collective-permute-start.8 = (f32[2,128,256]{2,1,0:T(8,128)}, f32[2,128,256]{2,1,0:T(8,128)}, u32[]{:S(2)}, u32[]{:S(2)}) collective-permute-start(f32[2,128,256]{2,1,0:T(8,128)} %get-tuple-element.22), channel_id=1, source_target_pairs={{0,16},{1,17},{2,18},{3,19},{4,20},{5,21},{6,22},{7,23},{8,24},{9,... | collective-permute-start | bytes 786440 | tf_op jit(solution)/shard_map/ppermute | solution.py:31
  88.4 11.5 %copy-start.1 = (f32[1024,256]{1,0:T(8,128)S(1)}, f32[1024,256]{1,0:T(8,128)}, u32[]{:S(2)}) copy-start(f32[1024,256]{1,0:T(8,128)} %copy-done) | copy-start | bytes 3145732
  90.1 15.9 %collective-permute-start.14 = (f32[2,128,256]{2,1,0:T(8,128)S(1)}, f32[2,128,256]{2,1,0:T(8,128)S(1)}, u32[]{:S(2)}, u32[]{:S(2)}) collective-permute-start(f32[2,128,256]{2,1,0:T(8,128)S(1)} %get-tuple-element.20), channel_id=1, source_target_pairs={{0,96},{1,97},{2,98},{3,99},{4,100},{5,101},{6,102},{7,103},{8,104... | collective-permute-start | bytes 786440 | tf_op jit(solution)/shard_map/ppermute | solution.py:31
  93.9 12.2 %collective-permute-start.13 = (f32[2,128,256]{2,1,0:T(8,128)S(1)}, f32[2,128,256]{2,1,0:T(8,128)S(1)}, u32[]{:S(2)}, u32[]{:S(2)}) collective-permute-start(f32[2,128,256]{2,1,0:T(8,128)S(1)} %get-tuple-element.21), channel_id=1, source_target_pairs={{0,64},{1,65},{2,66},{3,67},{4,68},{5,69},{6,70},{7,71},{8,72},{9,... | collective-permute-start | bytes 786440 | tf_op jit(solution)/shard_map/ppermute | solution.py:31
  97.5 11.6 %collective-permute-start.12 = (f32[2,128,256]{2,1,0:T(8,128)S(1)}, f32[2,128,256]{2,1,0:T(8,128)S(1)}, u32[]{:S(2)}, u32[]{:S(2)}) collective-permute-start(f32[2,128,256]{2,1,0:T(8,128)S(1)} %get-tuple-element.19), channel_id=1, source_target_pairs={{0,32},{1,33},{2,34},{3,35},{4,36},{5,37},{6,38},{7,39},{8,40},{9,... | collective-permute-start | bytes 786440 | tf_op jit(solution)/shard_map/ppermute | solution.py:31
  105.9 7.3 %collective-permute-start.6 = (f32[8,64,256]{2,1,0:T(8,128)S(1)}, f32[8,64,256]{2,1,0:T(8,128)S(1)}, u32[]{:S(2)}, u32[]{:S(2)}) collective-permute-start(f32[8,64,256]{2,1,0:T(8,128)S(1)} %get-tuple-element.13), channel_id=1, source_target_pairs={{0,16},{1,17},{2,18},{3,19},{4,20},{5,21},{6,22},{7,23},{8,24},{9,... | collective-permute-start | bytes 1572872 | tf_op jit(solution)/shard_map/ppermute | solution.py:31
  109.2 10.0 %collective-permute-start.15 = (f32[128,256]{1,0:T(8,128)S(1)}, f32[128,256]{1,0:T(8,128)S(1)}, u32[]{:S(2)}, u32[]{:S(2)}) collective-permute-start(f32[128,256]{1,0:T(8,128)S(1)} %select_bitcast_fusion), channel_id=1, source_target_pairs={{0,128},{1,129},{2,130},{3,131},{4,132},{5,133},{6,134},{7,135},{8... | collective-permute-start | bytes 393224 | tf_op jit(solution)/shard_map/ppermute | solution.py:31
  114.1 25.7 %copy-start.3 = (s32[256]{0:T(256)S(1)}, s32[256]{0:T(256)}, u32[]{:S(2)}) copy-start(s32[256]{0:T(256)} %constant.83.clone) | copy-start | bytes 3076
  114.1 14.1 %all-to-all-start.1 = ((f32[8,64,256]{2,1,0:T(8,128)}), f32[8,64,256]{2,1,0:T(8,128)S(1)}, u32[]{:S(2)}, u32[]{:S(2)}) async-start(f32[8,64,256]{2,1,0:T(8,128)} %add.82), calls=%async_computation.1 | async-start | bytes 1048576 | tf_op jit(solution)/shard_map/all_to_all | solution.py:326
  119.2 1.3 collective-permute-start.16
  120.5 1.2 collective-permute-start.17
  128.2 1.3 collective-permute-start.7
  129.6 13.4 %collective-permute-start.18 = (f32[128,256]{1,0:T(8,128)S(1)}, f32[128,256]{1,0:T(8,128)S(1)}, u32[]{:S(2)}, u32[]{:S(2)}) collective-permute-start(f32[128,256]{1,0:T(8,128)S(1)} %get-tuple-element.26), channel_id=1, source_target_pairs={{0,65},{1,80},{2,99},{3,114},{4,133},{5,148},{6,167},{7,182},{8,21... | collective-permute-start | bytes 393224 | tf_op jit(solution)/shard_map/ppermute | solution.py:31
  137.8 11.4 %collective-permute-start.19 = (f32[128,256]{1,0:T(8,128)S(1)}, f32[128,256]{1,0:T(8,128)S(1)}, u32[]{:S(2)}, u32[]{:S(2)}) collective-permute-start(f32[128,256]{1,0:T(8,128)S(1)} %get-tuple-element.27), channel_id=1, source_target_pairs={{0,32},{1,49},{2,66},{3,83},{4,100},{5,117},{6,134},{7,151},{8,168... | collective-permute-start | bytes 393224 | tf_op jit(solution)/shard_map/ppermute | solution.py:31

commit v4 on v3

--- a/solution.py
+++ b/solution.py
@@ -55,9 +55,9 @@
     sign_ref[...] = signs_ref[...].astype(F32).T
     for s in range(SLICES):
         row = picked_ref[s // 2 : s // 2 + 1, :].astype(F32)
-        o_buf[s, SPAN:, :] = jnp.broadcast_to(jnp.concatenate([row, row], axis=1), (8, 256))
-    picks = pl.ds(SPAN, 8)
-    stores = [pltpu.make_async_copy(o_buf.at[:, picks, :], o_ref.at[:, picks, :], out_sem.at[steps])]
+        o_buf[s, 2 * SPAN :, :] = jnp.broadcast_to(row, (8, 128))
+    picks = pl.ds(2 * SPAN, 8)
+    stores = [pltpu.make_async_copy(o_buf.at[:, picks, :], o_ref.at[:, picks, :], out_sem.at[0, steps])]
     stores[0].start()
     for k in range(steps):
         loads[k].wait()
@@ -66,16 +66,18 @@
             at = pl.ds(pl.multiple_of(k * rows + i * 8, 8), 8)
             sign = sign_ref[at, :]
             sign = [jnp.broadcast_to(sign[:, a : a + 1], (8, 128)) for a in range(SLICES)]
-            for first in (0, 128):
-                cols = pl.ds(first, 128)
-                vals = hadamard([x_buf[a, at, cols] * sign[a] for a in range(SLICES)])
+            for half in range(2):
+                vals = hadamard([x_buf[a, at, half * 128 : half * 128 + 128] * sign[a] for a in range(SLICES)])
+                to = pl.ds(pl.multiple_of(half * SPAN + k * rows + i * 8, 8), 8)
                 for s in range(SLICES):
-                    o_buf[s, at, cols] = vals[s]
+                    o_buf[s, to, :] = vals[s]
             return carry
 
-        lax.fori_loop(0, rows // 8, chunk, 0)
-        stores.append(pltpu.make_async_copy(part(o_buf, k), part(o_ref, k), out_sem.at[k]))
-        stores[-1].start()
+        lax.fori_loop(0, rows // 8, chunk, 0, unroll=True)
+        for half in range(2):
+            done = pl.ds(half * SPAN + k * rows, rows)
+            stores.append(pltpu.make_async_copy(o_buf.at[:, done, :], o_ref.at[:, done, :], out_sem.at[half, k]))
+            stores[-1].start()
     for store in stores:
         store.wait()
 
@@ -83,7 +85,7 @@
 def mix_slices(matrix, signs, picked):
     rows, cols = matrix.shape
     vmem = pl.BlockSpec(memory_space=pltpu.VMEM)
-    shape = (SLICES, SPAN + 8, cols)
+    shape = (SLICES, 2 * SPAN + 8, 128)
     return pl.pallas_call(
         mix_kernel,
         out_shape=pltpu.HBM(shape, F32),
@@ -94,7 +96,7 @@
             pltpu.VMEM((SLICES, SPAN, cols), F32),
             pltpu.VMEM(shape, F32),
             pltpu.SemaphoreType.DMA((4,)),
-            pltpu.SemaphoreType.DMA((5,)),
+            pltpu.SemaphoreType.DMA((2, 5)),
         ],
         name="mix_slices",
     )(
@@ -105,14 +107,16 @@
 
 
 def sample_kernel(scale, half_ref, y_ref, o_ref, mixed_ref, where_ref):
-    picks = jnp.concatenate([y_ref[q, SPAN : SPAN + 1, :128] for q in range(SLICES)], axis=0)
+    picks = jnp.concatenate([y_ref[q, 2 * SPAN : 2 * SPAN + 1, :] for q in range(SLICES)], axis=0)
     where_ref[...] = picks.T.astype(jnp.int32)
 
     def chunk(i, carry):
         rows = pl.ds(pl.multiple_of(i * 8, 8), 8)
-        vals = hadamard([y_ref[p, rows, :] for p in range(SLICES)])
-        for q in range(SLICES):
-            mixed_ref[q, rows, :] = vals[q] * scale
+        for half in range(2):
+            at = pl.ds(pl.multiple_of(half * SPAN + i * 8, 8), 8)
+            vals = hadamard([y_ref[p, at, :] for p in range(SLICES)])
+            for q in range(SLICES):
+                mixed_ref[q, rows, half * 128 : half * 128 + 128] = vals[q] * scale
         return carry
 
     lax.fori_loop(0, SPAN // 8, chunk, 0)
@@ -136,7 +140,7 @@
 
 
 def sample(slices, scale):
-    cols = slices.shape[2]
+    cols = 2 * slices.shape[2]
     half = lax.axis_index("core").reshape(1)
     return pl.pallas_call(
         lambda *refs: sample_kernel(scale, *refs),
@@ -150,7 +154,7 @@
 
 
 def early_pairs(core):
-    return [((1, 0), (0, 0)), ((1, 0), (0, 1)), ((1, 0), (-1, 0)), ((0, core), (0, 0))]
+    return [((1, 0), (0, 0)), ((1, 0), (0, 1)), ((1, 0), (-1, 0)), ((0, 0), (0, core))]
 
 
 def late_pairs(z):
@@ -194,81 +198,67 @@
     return out + jnp.dot(a[0], b[0], preferred_element_type=F32)
 
 
-def put_block(core, out, unit, keep_ref, send_ref):
+def split_block(core, out, out_ref, unit, keep_ref, send_ref, places):
+    out_ref[unit] = out
     for half in range(2):
-        for owner in range(2):
-            rows = out[half * 128 + owner * 64 : half * 128 + owner * 64 + 64]
-
-            @pl.when(core == owner)
-            def _():
-                keep_ref[2 * unit + half, :64, :] = rows
-
-            @pl.when(core != owner)
-            def _():
-                send_ref[2 * unit + half, :64, :] = rows
-
-
-def early_kernel(core_ref, own_ref, beside_ref, up_ref, down_ref, keep_ref, send_ref):
+        for ref, owner in ((keep_ref, core), (send_ref, 1 - core)):
+            rows = pl.ds(pl.multiple_of(half * 128 + owner * 64, 64), 64)
+            ref[places[half]] = out_ref[unit, rows, :]
+
+
+def early_kernel(core_ref, own_ref, beside_ref, up_ref, down_ref, keep_ref, send_ref, out_ref):
     core = core_ref[0]
-    own, beside = halves(own_ref), halves(beside_ref)
-    for owner, left in ((0, own), (1, beside)):
-        out = block(turned(left), own)
-        for half in range(2):
-            rows = out[half * 128 : half * 128 + 128]
-
-            @pl.when(core == owner)
-            def _():
-                keep_ref[6 + half] = rows
-
-            @pl.when(core != owner)
-            def _():
-                send_ref[6 + half] = rows
-
-    up = turned(halves(up_ref))
-    for unit, right in enumerate((own, beside, halves(down_ref))):
-        put_block(core, block(up, right), unit, keep_ref, send_ref)
-    for unit in range(6):
-        keep_ref[unit, 64:, :] = jnp.zeros((64, 256), F32)
-        send_ref[unit, 64:, :] = jnp.zeros((64, 256), F32)
-
-
-def late_kernel(flags_ref, own_ref, beside_ref, up_ref, down_ref, down_beside_ref, up2_ref, down2_ref, keep_ref, send_ref, buf, sem):
+
+    def places(unit):
+        chips = (2 * unit, 2 * unit + 1)
+        return [(chip % 4, slice(0, 64) if chip < 4 else slice(64, 128)) for chip in chips]
+
+    own, beside, down = halves(own_ref), halves(beside_ref), halves(down_ref)
+    up, turn = turned(halves(up_ref)), turned(own)
+    for unit, right in enumerate((own, beside, down)):
+        split_block(core, block(up, right), out_ref, unit, keep_ref, send_ref, places(unit))
+    out_ref[3] = block(turn, own)
+    out_ref[4] = block(turn, beside)
+    for half in range(2):
+        rows = slice(half * 128, half * 128 + 128)
+        keep_ref[2 + half, 64:, :] = out_ref[3 + core, rows, :]
+        send_ref[2 + half, 64:, :] = out_ref[4 - core, rows, :]
+        for ref in (keep_ref, send_ref):
+            ref[half, 128:, :] = jnp.zeros((64, 256), F32)
+
+
+def late_kernel(
+    flags_ref, own_ref, beside_ref, up_ref, down_ref, down_beside_ref, up2_ref, down2_ref, keep_ref, send_ref, out_ref, high_ref, low_ref
+):
     core, low = flags_ref[0], flags_ref[1]
 
-    def load(k, ref):
-        return pltpu.make_async_copy(ref, buf.at[k], sem.at[k])
-
-    for k, ref in enumerate((up2_ref, down2_ref, up_ref)):
-        load(k, ref).start()
-
-    @pl.when(low == 1)
-    def _():
-        load(3, down_beside_ref).start()
-        load(4, beside_ref).start()
-
-    @pl.when(low == 0)
-    def _():
-        load(3, down_ref).start()
-        load(4, own_ref).start()
-
-    load(0, up2_ref).wait()
-    up2 = turned(halves(buf.at[0]))
-    load(1, down2_ref).wait()
-    down2 = halves(buf.at[1])
-    put_block(core, block(up2, down2), 3, keep_ref, send_ref)
-    load(2, up_ref).wait()
-    put_block(core, block(turned(halves(buf.at[2])), down2), 1, keep_ref, send_ref)
-    load(3, down_ref).wait()
-    put_block(core, block(up2, halves(buf.at[3])), 2, keep_ref, send_ref)
-    load(4, own_ref).wait()
-    put_block(core, block(up2, halves(buf.at[4])), 0, keep_ref, send_ref)
-
-
-def call_blocks(kernel, rows, flags, operands, space, scratch, cost, name):
+    def pick(k, a_ref, b_ref):
+        @pl.when(low == 1)
+        def _():
+            high_ref[k], low_ref[k] = halves(a_ref)
+
+        @pl.when(low == 0)
+        def _():
+            high_ref[k], low_ref[k] = halves(b_ref)
+
+    pick(0, beside_ref, own_ref)
+    pick(1, down_beside_ref, down_ref)
+    up2, down2 = turned(halves(up2_ref)), halves(down2_ref)
+    blocks = [
+        (up2, (high_ref[0], low_ref[0])),
+        (turned(halves(up_ref)), down2),
+        (up2, (high_ref[1], low_ref[1])),
+        (up2, down2),
+    ]
+    for unit, pair in enumerate(blocks):
+        split_block(core, block(*pair), out_ref, unit, keep_ref, send_ref, (2 * unit, 2 * unit + 1))
+
+
+def call_blocks(kernel, shape, flags, operands, space, scratch, cost, name):
     vmem = pl.BlockSpec(memory_space=pltpu.VMEM)
     return pl.pallas_call(
         kernel,
-        out_shape=[jax.ShapeDtypeStruct((8, rows, 256), F32)] * 2,
+        out_shape=[jax.ShapeDtypeStruct((*shape, 256), F32)] * 2,
         in_specs=[pl.BlockSpec(memory_space=pltpu.SMEM)] + [pl.BlockSpec(memory_space=space)] * len(operands),
         out_specs=[vmem] * 2,
         scratch_shapes=scratch,
@@ -299,13 +289,12 @@
     down_beside = permute(down, lambda xh, y, c, z, x: (xh, y, c, z, x + 1) if z < 4 else None)
 
     core_flag = core.reshape(1)
-    keep, send = call_blocks(early_kernel, 128, core_flag, (own, beside, up, down), pltpu.VMEM, [], 1000, "early_blocks")
-    early = keep + jnp.concatenate([other_core(send[2 * i : 2 * i + 2]) for i in range(4)])
-    early = early.reshape(2, 4, 128, 256)
+    keep, send = call_blocks(early_kernel, (4, 192), core_flag, (own, beside, up, down), pltpu.VMEM, [pltpu.VMEM((5, 256, 256), F32)], 1000, "early_blocks")
+    early = keep + jnp.concatenate([other_core(send[i : i + 1]) for i in range(4)])
     row = lax.axis_index("y")
-    total = lax.dynamic_index_in_dim(early, row, 1, keepdims=False)
+    total = lax.dynamic_index_in_dim(early, row, 0, keepdims=False)
     for step in range(1, 4):
-        part = lax.dynamic_index_in_dim(early, (row + step) % 4, 1, keepdims=False)
+        part = lax.dynamic_index_in_dim(early, (row + step) % 4, 0, keepdims=False)
         total += permute(part, lambda xh, y, c, z, x: (xh, y + step, c, z, x))
 
     def by_core(mine):
@@ -315,18 +304,18 @@
     flags = jnp.stack([core, (z < 4).astype(jnp.int32)])
     keep, send = call_blocks(
         late_kernel,
-        64,
+        (8, 64),
         flags,
         (own, beside, up, down, down_beside, up2, down2),
-        pl.ANY,
-        [pltpu.VMEM((5, *own.shape), F32), pltpu.SemaphoreType.DMA((5,))],
+        pltpu.VMEM,
+        [pltpu.VMEM((4, 256, 256), F32)] + [pltpu.VMEM((2, *own.shape), BF16)] * 2,
         40_000_000_000,
         "late_blocks",
     )
     slots = lax.all_to_all(keep + other_core(send), CHIPS, 0, 0, tiled=True)
     plane = lax.axis_index("xh")
-    early = jnp.where(plane == 0, total[0], total[1]) + permute(
-        jnp.where(plane == 0, total[1], total[0]), lambda xh, y, c, z, x: (xh + 1, y, c, z, x)
+    early = jnp.where(plane == 0, total[:128], total[64:]) + permute(
+        jnp.where(plane == 0, total[64:], total[:128]), lambda xh, y, c, z, x: (xh + 1, y, c, z, x)
     )
     got, rest = [], early[:64]
     for part in range(2):

time: 151 us -> 144 us (0.954)
  Pallas kernels: 16.9 us -> 11.3 us
    pallas_call x2, Pallas kernels: 11.1 us -> 6.4 us  [call_blocks(): pl.pallas_call(kernel, out_shape=[jax.ShapeDtypeStruct((*shape, 256), F32...]
    ppermute x20, starting transfers between devices: 35.4 us -> 33.2 us  [permute(): return lax.ppermute(block, NAMES, pairs)]
  transfers between devices with their start and end apart: 22 -> 22, of which waited for: 12 -> 14; matrix products, arithmetic and copies ran while one was open for 3% -> 3% of each run, Pallas kernels for 7% -> 4%
where the time goes in v4:
time: 144 us; the launch traced here: 143 us
  waiting for transfers between devices  76.2 us (53%)
  starting transfers between devices  46.8 us (32%)
  Pallas kernels  11.3 us (8%)
  other arithmetic  3.33 us (2%)
  between operations  2.87 us (2%)
  local copies, waits for them, and re-layouts  2.45 us (2%)
    ppermute x20, waiting for transfers between devices, permute(): return lax.ppermute(block, NAMES, pairs)  41.4 us
    ppermute x20, starting transfers between devices, permute(): return lax.ppermute(block, NAMES, pairs)  33.2 us
    all_to_all x1, waiting for transfers between devices, shards(): slices = lax.all_to_all(slices, ROW, 0, 0, tiled=True)  28.4 us
    all_to_all x1, starting transfers between devices, shards(): slices = lax.all_to_all(slices, ROW, 0, 0, tiled=True)  7.46 us
    pallas_call x2, Pallas kernels, call_blocks(): pl.pallas_call(kernel, out_shape=[jax.ShapeDtypeStruct((*shape, 256), F32...  6.4 us
    all_to_all x1, waiting for transfers between devices, shards(): slots = lax.all_to_all(keep + other_core(send), CHIPS, 0, 0, tiled=True)  6.37 us
    all_to_all x1, starting transfers between devices, shards(): slots = lax.all_to_all(keep + other_core(send), CHIPS, 0, 0, tiled=True)  6.13 us
    pallas_call x1, Pallas kernels, mix_slices(): pl.pallas_call(mix_kernel, out_shape=pltpu.HBM(shape, F32), in_specs=[vme...  3.51 us
  transfers between devices with their start and end apart: 22, of which 14 were waited for; matrix products, arithmetic and copies ran while one was open for 3% of the time, Pallas kernels for 4%

profile of v4, /device:TPU:6, one launch (start us, length us, event | category | flops | bytes accessed | tf_op | source)
XLA Modules:
  0.0 142.9 jit_solution(17824373468115131497)
XLA Ops:
  0.0 3.5 %mix_slices.1 = f32[16,264,128]{2,1,0:T(8,128)} custom-call(s32[16,128]{1,0:T(8,128)} %bitcast.21, s32[8,128]{1,0:T(8,128)} %bitcast.22, f32[16,128,256]{2,1,0:T(8,128)} %bitcast.20), custom_call_target="tpu_custom_call" | custom-call | tf_op jit(solution)/shard_map/mix_slices/pallas_call | solution.py:89
  3.5 7.5 %all-to-all-start = ((f32[16,264,128]{2,1,0:T(8,128)}), f32[16,264,128]{2,1,0:T(8,128)S(1)}, u32[]{:S(2)}, u32[]{:S(2)}) async-start(f32[16,264,128]{2,1,0:T(8,128)} %mix_slices.1), calls=%async_computation | async-start | bytes 4325376 | tf_op jit(solution)/shard_map/all_to_all | solution.py:281
  11.0 28.4 %all-to-all-done.refs_1_ = f32[16,264,128]{2,1,0:T(8,128)S(1)} async-done(((f32[16,264,128]{2,1,0:T(8,128)}), f32[16,264,128]{2,1,0:T(8,128)S(1)}, u32[]{:S(2)}, u32[]{:S(2)}) %all-to-all-start) | async-done | bytes 2162720 | tf_op jit(solution)/shard_map/all_to_all | solution.py:281
  39.4 1.4 sample.1.own_ref
  40.8 2.0 %collective-permute-start.2 = (f32[1024,256]{1,0:T(8,128)S(1)}, f32[1024,256]{1,0:T(8,128)S(1)}, u32[]{:S(2)}, u32[]{:S(2)}) collective-permute-start(f32[1024,256]{1,0:T(8,128)S(1)} %sample.1.own_ref), channel_id=1, source_target_pairs={{0,2},{1,3},{2,4},{3,5},{4,6},{5,7},{6,8},{7,9},{8,10},{9,11},{10,... | collective-permute-start | bytes 3145736 | tf_op jit(solution)/shard_map/ppermute | solution.py:31
  42.8 4.0 %collective-permute-start.1 = (f32[1024,256]{1,0:T(8,128)S(1)}, f32[1024,256]{1,0:T(8,128)S(1)}, u32[]{:S(2)}, u32[]{:S(2)}) collective-permute-start(f32[1024,256]{1,0:T(8,128)S(1)} %sample.1.own_ref), channel_id=1, source_target_pairs={{0,14},{1,15},{2,0},{3,1},{4,2},{5,3},{6,4},{7,5},{8,6},{9,7},{10,... | collective-permute-start | bytes 3145736 | tf_op jit(solution)/shard_map/ppermute | solution.py:31
  46.8 0.3 collective-permute-start
  47.0 22.6 %collective-permute-done.2.down_ref = f32[1024,256]{1,0:T(8,128)S(1)} collective-permute-done((f32[1024,256]{1,0:T(8,128)S(1)}, f32[1024,256]{1,0:T(8,128)S(1)}, u32[]{:S(2)}, u32[]{:S(2)}) %collective-permute-start.2) | collective-permute-done | bytes 1048608 | tf_op jit(solution)/shard_map/ppermute | solution.py:31
  69.7 2.1 %collective-permute-start.3 = (f32[1024,256]{1,0:T(8,128)S(1)}, f32[1024,256]{1,0:T(8,128)}, u32[]{:S(2)}, u32[]{:S(2)}) collective-permute-start(f32[1024,256]{1,0:T(8,128)S(1)} %collective-permute-done.2.down_ref), channel_id=1, source_target_pairs={{0,1},{1,0},{2,3},{3,2},{4,5},{5,4},{6,7},{7,6},{16,17},{17,16},{1... | collective-permute-start | bytes 3145736 | tf_op jit(solution)/shard_map/ppermute | solution.py:31
  71.8 0.9 collective-permute-start.4
  72.7 1.2 collective-permute-start.5
  73.9 2.3 %early_blocks.1 = (f32[4,192,256]{2,1,0:T(8,128)S(1)}, f32[4,192,256]{2,1,0:T(8,128)S(1)}) custom-call(s32[1]{0:T(128)} %bitcast.1.refs_0_.core_ref, f32[1024,256]{1,0:T(8,128)S(1)} %sample.1.own_ref, f32[1024,256]{1,0:T(8,128)S(1)} %collective-permute-done.beside_ref, f32[1024,256]{1,0:T(8,128)S(1)} %collective-permute-done.1.up_ref, ...), custom_call_target="tpu_custom_call" | custom-call | flops 1000 | bytes 2 | tf_op jit(solution)/shard_map/early_blocks/pallas_call | solution.py:259
  76.2 0.8 fusion.6
  77.1 0.1 copy-done.2
  77.2 0.5 collective-permute-start.10
  77.7 0.9 collective-permute-done.11
  78.6 0.1 collective-permute-start.9
  78.8 0.1 collective-permute-done.10
  78.9 0.7 copy-done.3
  79.6 0.2 collective-permute-start.8
  79.8 0.1 pad_add_fusion.flags_ref
  79.9 0.5 collective-permute-done.9
  80.4 0.8 collective-permute-done.8
  81.2 1.4 maximum_add_fusion
  82.7 5.4 %collective-permute-start.14 = (f32[192,256]{1,0:T(8,128)S(1)}, f32[192,256]{1,0:T(8,128)S(1)}, u32[]{:S(2)}, u32[]{:S(2)}) collective-permute-start(f32[192,256]{1,0:T(8,128)S(1)} %get-tuple-element.20), channel_id=1, source_target_pairs={{0,96},{1,97},{2,98},{3,99},{4,100},{5,101},{6,102},{7,103},{8,104... | collective-permute-start | bytes 589832 | tf_op jit(solution)/shard_map/ppermute | solution.py:31
  88.1 7.7 %collective-permute-done.3.down_beside_ref = f32[1024,256]{1,0:T(8,128)} collective-permute-done((f32[1024,256]{1,0:T(8,128)S(1)}, f32[1024,256]{1,0:T(8,128)}, u32[]{:S(2)}, u32[]{:S(2)}) %collective-permute-start.3) | collective-permute-done | bytes 1048608 | tf_op jit(solution)/shard_map/ppermute | solution.py:31
  95.8 2.4 %collective-permute-start.12 = (f32[192,256]{1,0:T(8,128)S(1)}, f32[192,256]{1,0:T(8,128)S(1)}, u32[]{:S(2)}, u32[]{:S(2)}) collective-permute-start(f32[192,256]{1,0:T(8,128)S(1)} %get-tuple-element.19), channel_id=1, source_target_pairs={{0,32},{1,33},{2,34},{3,35},{4,36},{5,37},{6,38},{7,39},{8,40},{9,... | collective-permute-start | bytes 589832 | tf_op jit(solution)/shard_map/ppermute | solution.py:31
  98.1 4.1 %late_blocks.1 = (f32[8,64,256]{2,1,0:T(8,128)S(1)}, f32[8,64,256]{2,1,0:T(8,128)S(1)}) custom-call(s32[2]{0:T(128)S(1)} %pad_add_fusion.flags_ref, f32[1024,256]{1,0:T(8,128)S(1)} %sample.1.own_ref, f32[1024,256]{1,0:T(8,128)S(1)} %copy-done.1, f32[1024,256]{1,0:T(8,128)S(1)} %collective-permute-done.1.up_ref, ...), custom_call_target="tpu_custom_call" | custom-call | flops 40000000000 | bytes 100000000 | tf_op jit(solution)/shard_map/late_blocks/pallas_call | solution.py:259
  102.2 0.1 collective-permute-start.6
  102.4 2.2 %collective-permute-done.12 = f32[192,256]{1,0:T(8,128)S(1)} collective-permute-done((f32[192,256]{1,0:T(8,128)S(1)}, f32[192,256]{1,0:T(8,128)S(1)}, u32[]{:S(2)}, u32[]{:S(2)}) %collective-permute-start.12) | collective-permute-done | bytes 196640 | tf_op jit(solution)/shard_map/ppermute | solution.py:31
  104.6 0.1 fusion.3
  104.7 3.5 %collective-permute-start.15 = (f32[128,256]{1,0:T(8,128)S(1)}, f32[128,256]{1,0:T(8,128)S(1)}, u32[]{:S(2)}, u32[]{:S(2)}) collective-permute-start(f32[128,256]{1,0:T(8,128)S(1)} %slice_select_fusion), channel_id=1, source_target_pairs={{0,128},{1,129},{2,130},{3,131},{4,132},{5,133},{6,134},{7,135},{8... | collective-permute-start | bytes 393224 | tf_op jit(solution)/shard_map/ppermute | solution.py:31
  108.2 0.9 add.82
  109.1 6.1 %all-to-all-start.1 = ((f32[8,64,256]{2,1,0:T(8,128)}), f32[8,64,256]{2,1,0:T(8,128)S(1)}, u32[]{:S(2)}, u32[]{:S(2)}) async-start(f32[8,64,256]{2,1,0:T(8,128)} %add.82), calls=%async_computation.1 | async-start | bytes 1048576 | tf_op jit(solution)/shard_map/all_to_all | solution.py:315
  115.3 0.1 collective-permute-start.16
  115.4 1.2 collective-permute-done.16
  116.6 0.2 collective-permute-start.17
  116.7 1.0 collective-permute-done.17
  117.8 6.4 %all-to-all-done.1 = f32[8,64,256]{2,1,0:T(8,128)S(1)} async-done(((f32[8,64,256]{2,1,0:T(8,128)}), f32[8,64,256]{2,1,0:T(8,128)S(1)}, u32[]{:S(2)}, u32[]{:S(2)}) %all-to-all-start.1) | async-done | bytes 524320 | tf_op jit(solution)/shard_map/all_to_all | solution.py:315
  124.2 0.1 collective-permute-start.7
  124.3 1.2 collective-permute-done.7
  125.6 4.9 %collective-permute-start.18 = (f32[128,256]{1,0:T(8,128)S(1)}, f32[128,256]{1,0:T(8,128)S(1)}, u32[]{:S(2)}, u32[]{:S(2)}) collective-permute-start(f32[128,256]{1,0:T(8,128)S(1)} %get-tuple-element.26), channel_id=1, source_target_pairs={{0,65},{1,80},{2,99},{3,114},{4,133},{5,148},{6,167},{7,182},{8,21... | collective-permute-start | bytes 393224 | tf_op jit(solution)/shard_map/ppermute | solution.py:31
  130.5 5.2 %collective-permute-start.19 = (f32[128,256]{1,0:T(8,128)S(1)}, f32[128,256]{1,0:T(8,128)S(1)}, u32[]{:S(2)}, u32[]{:S(2)}) collective-permute-start(f32[128,256]{1,0:T(8,128)S(1)} %get-tuple-element.27), channel_id=1, source_target_pairs={{0,32},{1,49},{2,66},{3,83},{4,100},{5,117},{6,134},{7,151},{8,168... | collective-permute-start | bytes 393224 | tf_op jit(solution)/shard_map/ppermute | solution.py:31
  135.7 0.6 dynamic_slice.16
  138.9 0.6 collective-permute-done.18
  139.5 2.5 %collective-permute-done.19 = f32[128,256]{1,0:T(8,128)S(1)} collective-permute-done((f32[128,256]{1,0:T(8,128)S(1)}, f32[128,256]{1,0:T(8,128)S(1)}, u32[]{:S(2)}, u32[]{:S(2)}) %collective-permute-start.19) | collective-permute-done | bytes 131104 | tf_op jit(solution)/shard_map/ppermute | solution.py:31
  142.1 0.1 copy.5
  142.2 0.7 fusion
  (32 shorter events, 0.3 us)
Async XLA Ops:
  3.5 35.9 %all-to-all-start = ((f32[16,264,128]{2,1,0:T(8,128)}), f32[16,264,128]{2,1,0:T(8,128)S(1)}, u32[]{:S(2)}, u32[]{:S(2)}) async-start(f32[16,264,128]{2,1,0:T(8,128)} %mix_slices.1), calls=%async_computation | async-start | bytes 4325376 | tf_op jit(solution)/shard_map/all_to_all | solution.py:281
  40.8 28.9 %collective-permute-start.2 = (f32[1024,256]{1,0:T(8,128)S(1)}, f32[1024,256]{1,0:T(8,128)S(1)}, u32[]{:S(2)}, u32[]{:S(2)}) collective-permute-start(f32[1024,256]{1,0:T(8,128)S(1)} %sample.1.own_ref), channel_id=1, source_target_pairs={{0,2},{1,3},{2,4},{3,5},{4,6},{5,7},{6,8},{7,9},{8,10},{9,11},{10,... | collective-permute-start | bytes 3145736 | tf_op jit(solution)/shard_map/ppermute | solution.py:31
  42.8 29.0 %collective-permute-start.1 = (f32[1024,256]{1,0:T(8,128)S(1)}, f32[1024,256]{1,0:T(8,128)S(1)}, u32[]{:S(2)}, u32[]{:S(2)}) collective-permute-start(f32[1024,256]{1,0:T(8,128)S(1)} %sample.1.own_ref), channel_id=1, source_target_pairs={{0,14},{1,15},{2,0},{3,1},{4,2},{5,3},{6,4},{7,5},{8,6},{9,7},{10,... | collective-permute-start | bytes 3145736 | tf_op jit(solution)/shard_map/ppermute | solution.py:31
  46.8 27.1 %collective-permute-start = (f32[1024,256]{1,0:T(8,128)S(1)}, f32[1024,256]{1,0:T(8,128)S(1)}, u32[]{:S(2)}, u32[]{:S(2)}) collective-permute-start(f32[1024,256]{1,0:T(8,128)S(1)} %sample.1.own_ref), channel_id=1, source_target_pairs={{0,1},{1,0},{2,3},{3,2},{4,5},{5,4},{6,7},{7,6},{8,9},{9,8},{10,11... | collective-permute-start | bytes 3145736 | tf_op jit(solution)/shard_map/ppermute | solution.py:31
  69.7 26.1 %collective-permute-start.3 = (f32[1024,256]{1,0:T(8,128)S(1)}, f32[1024,256]{1,0:T(8,128)}, u32[]{:S(2)}, u32[]{:S(2)}) collective-permute-start(f32[1024,256]{1,0:T(8,128)S(1)} %collective-permute-done.2.down_ref), channel_id=1, source_target_pairs={{0,1},{1,0},{2,3},{3,2},{4,5},{5,4},{6,7},{7,6},{16,17},{17,16},{1... | collective-permute-start | bytes 3145736 | tf_op jit(solution)/shard_map/ppermute | solution.py:31
  71.8 26.4 %collective-permute-start.4 = (f32[1024,256]{1,0:T(8,128)S(1)}, f32[1024,256]{1,0:T(8,128)}, u32[]{:S(2)}, u32[]{:S(2)}) collective-permute-start(f32[1024,256]{1,0:T(8,128)S(1)} %collective-permute-done.1.up_ref), channel_id=1, source_target_pairs={{0,15},{1,14},{2,0},{3,1},{4,2},{5,3},{6,4},{7,5},{8,6},{9,7},{10,... | collective-permute-start | bytes 3145736 | tf_op jit(solution)/shard_map/ppermute | solution.py:31
  72.7 25.5 %collective-permute-start.5 = (f32[1024,256]{1,0:T(8,128)S(1)}, f32[1024,256]{1,0:T(8,128)}, u32[]{:S(2)}, u32[]{:S(2)}) collective-permute-start(f32[1024,256]{1,0:T(8,128)S(1)} %collective-permute-done.2.down_ref), channel_id=1, source_target_pairs={{0,2},{1,3},{2,4},{3,5},{4,6},{5,7},{6,8},{7,9},{8,10},{9,11},{10,... | collective-permute-start | bytes 3145736 | tf_op jit(solution)/shard_map/ppermute | solution.py:31
  73.9 3.2 %copy-start = (f32[1024,256]{1,0:T(8,128)}, f32[1024,256]{1,0:T(8,128)S(1)}, u32[]{:S(2)}) copy-start(f32[1024,256]{1,0:T(8,128)S(1)} %collective-permute-done.beside_ref) | copy-start | bytes 3145732
  76.2 1.0 copy-start.2
  77.2 1.4 %collective-permute-start.11 = (f32[1,192,256]{2,1,0:T(8,128)S(1)}, f32[1,192,256]{2,1,0:T(8,128)S(1)}, u32[]{:S(2)}, u32[]{:S(2)}) collective-permute-start(f32[1,192,256]{2,1,0:T(8,128)S(1)} %get-tuple-element.23), channel_id=1, source_target_pairs={{0,16},{1,17},{2,18},{3,19},{4,20},{5,21},{6,22},{7,23},{8,24},{9,... | collective-permute-start | bytes 589832 | tf_op jit(solution)/shard_map/ppermute | solution.py:31
  77.2 1.7 %collective-permute-start.10 = (f32[1,192,256]{2,1,0:T(8,128)S(1)}, f32[1,192,256]{2,1,0:T(8,128)S(1)}, u32[]{:S(2)}, u32[]{:S(2)}) collective-permute-start(f32[1,192,256]{2,1,0:T(8,128)S(1)} %get-tuple-element.24), channel_id=1, source_target_pairs={{0,16},{1,17},{2,18},{3,19},{4,20},{5,21},{6,22},{7,23},{8,24},{9,... | collective-permute-start | bytes 589832 | tf_op jit(solution)/shard_map/ppermute | solution.py:31
  78.6 1.8 %collective-permute-start.9 = (f32[1,192,256]{2,1,0:T(8,128)}, f32[1,192,256]{2,1,0:T(8,128)}, u32[]{:S(2)}, u32[]{:S(2)}) collective-permute-start(f32[1,192,256]{2,1,0:T(8,128)} %get-tuple-element.25), channel_id=1, source_target_pairs={{0,16},{1,17},{2,18},{3,19},{4,20},{5,21},{6,22},{7,23},{8,24},{9,... | collective-permute-start | bytes 589832 | tf_op jit(solution)/shard_map/ppermute | solution.py:31
  78.9 0.7 copy-start.3
  79.6 1.6 %collective-permute-start.8 = (f32[1,192,256]{2,1,0:T(8,128)S(1)}, f32[1,192,256]{2,1,0:T(8,128)}, u32[]{:S(2)}, u32[]{:S(2)}) collective-permute-start(f32[1,192,256]{2,1,0:T(8,128)S(1)} %get-tuple-element.22), channel_id=1, source_target_pairs={{0,16},{1,17},{2,18},{3,19},{4,20},{5,21},{6,22},{7,23},{8,24},{9,... | collective-permute-start | bytes 589832 | tf_op jit(solution)/shard_map/ppermute | solution.py:31
  79.8 18.3 %copy-start.1 = (f32[1024,256]{1,0:T(8,128)S(1)}, f32[1024,256]{1,0:T(8,128)}, u32[]{:S(2)}) copy-start(f32[1024,256]{1,0:T(8,128)} %copy-done) | copy-start | bytes 3145732
  82.7 19.7 %collective-permute-start.14 = (f32[192,256]{1,0:T(8,128)S(1)}, f32[192,256]{1,0:T(8,128)S(1)}, u32[]{:S(2)}, u32[]{:S(2)}) collective-permute-start(f32[192,256]{1,0:T(8,128)S(1)} %get-tuple-element.20), channel_id=1, source_target_pairs={{0,96},{1,97},{2,98},{3,99},{4,100},{5,101},{6,102},{7,103},{8,104... | collective-permute-start | bytes 589832 | tf_op jit(solution)/shard_map/ppermute | solution.py:31
  88.0 14.3 %collective-permute-start.13 = (f32[192,256]{1,0:T(8,128)S(1)}, f32[192,256]{1,0:T(8,128)S(1)}, u32[]{:S(2)}, u32[]{:S(2)}) collective-permute-start(f32[192,256]{1,0:T(8,128)S(1)} %get-tuple-element.21), channel_id=1, source_target_pairs={{0,64},{1,65},{2,66},{3,67},{4,68},{5,69},{6,70},{7,71},{8,72},{9,... | collective-permute-start | bytes 589832 | tf_op jit(solution)/shard_map/ppermute | solution.py:31
  95.8 8.8 %collective-permute-start.12 = (f32[192,256]{1,0:T(8,128)S(1)}, f32[192,256]{1,0:T(8,128)S(1)}, u32[]{:S(2)}, u32[]{:S(2)}) collective-permute-start(f32[192,256]{1,0:T(8,128)S(1)} %get-tuple-element.19), channel_id=1, source_target_pairs={{0,32},{1,33},{2,34},{3,35},{4,36},{5,37},{6,38},{7,39},{8,40},{9,... | collective-permute-start | bytes 589832 | tf_op jit(solution)/shard_map/ppermute | solution.py:31
  102.2 6.0 %collective-permute-start.6 = (f32[8,64,256]{2,1,0:T(8,128)S(1)}, f32[8,64,256]{2,1,0:T(8,128)S(1)}, u32[]{:S(2)}, u32[]{:S(2)}) collective-permute-start(f32[8,64,256]{2,1,0:T(8,128)S(1)} %get-tuple-element.13), channel_id=1, source_target_pairs={{0,16},{1,17},{2,18},{3,19},{4,20},{5,21},{6,22},{7,23},{8,24},{9,... | collective-permute-start | bytes 1572872 | tf_op jit(solution)/shard_map/ppermute | solution.py:31
  104.7 10.5 %collective-permute-start.15 = (f32[128,256]{1,0:T(8,128)S(1)}, f32[128,256]{1,0:T(8,128)S(1)}, u32[]{:S(2)}, u32[]{:S(2)}) collective-permute-start(f32[128,256]{1,0:T(8,128)S(1)} %slice_select_fusion), channel_id=1, source_target_pairs={{0,128},{1,129},{2,130},{3,131},{4,132},{5,133},{6,134},{7,135},{8... | collective-permute-start | bytes 393224 | tf_op jit(solution)/shard_map/ppermute | solution.py:31
  109.1 26.7 %copy-start.4 = (s32[256]{0:T(256)S(1)}, s32[256]{0:T(256)}, u32[]{:S(2)}) copy-start(s32[256]{0:T(256)} %constant.83.clone) | copy-start | bytes 3076
  109.1 15.1 %all-to-all-start.1 = ((f32[8,64,256]{2,1,0:T(8,128)}), f32[8,64,256]{2,1,0:T(8,128)S(1)}, u32[]{:S(2)}, u32[]{:S(2)}) async-start(f32[8,64,256]{2,1,0:T(8,128)} %add.82), calls=%async_computation.1 | async-start | bytes 1048576 | tf_op jit(solution)/shard_map/all_to_all | solution.py:315
  115.3 1.3 collective-permute-start.16
  116.6 1.2 collective-permute-start.17
  124.2 1.3 collective-permute-start.7
  125.6 13.9 %collective-permute-start.18 = (f32[128,256]{1,0:T(8,128)S(1)}, f32[128,256]{1,0:T(8,128)S(1)}, u32[]{:S(2)}, u32[]{:S(2)}) collective-permute-start(f32[128,256]{1,0:T(8,128)S(1)} %get-tuple-element.26), channel_id=1, source_target_pairs={{0,65},{1,80},{2,99},{3,114},{4,133},{5,148},{6,167},{7,182},{8,21... | collective-permute-start | bytes 393224 | tf_op jit(solution)/shard_map/ppermute | solution.py:31
  130.5 11.5 %collective-permute-start.19 = (f32[128,256]{1,0:T(8,128)S(1)}, f32[128,256]{1,0:T(8,128)S(1)}, u32[]{:S(2)}, u32[]{:S(2)}) collective-permute-start(f32[128,256]{1,0:T(8,128)S(1)} %get-tuple-element.27), channel_id=1, source_target_pairs={{0,32},{1,49},{2,66},{3,83},{4,100},{5,117},{6,134},{7,151},{8,168... | collective-permute-start | bytes 393224 | tf_op jit(solution)/shard_map/ppermute | solution.py:31

commit v5 on v4

--- a/solution.py
+++ b/solution.py
@@ -13,9 +13,11 @@
 SIZES = (2, 4, 2, 8, 2)
 ROW = ("xh", "y", "core")
 COL = ("z", "xl")
+EXCHANGE = ("y", "core", "xh")
 CHIPS = ("xh", "y")
 SLICES = 16
 SPAN = 128
+PLACE = [(s // 2 % 4 * 2 + s % 2) * 2 + s // 8 for s in range(16)]
 F32 = jnp.float32
 BF16 = jnp.bfloat16
 
@@ -55,7 +57,7 @@
     sign_ref[...] = signs_ref[...].astype(F32).T
     for s in range(SLICES):
         row = picked_ref[s // 2 : s // 2 + 1, :].astype(F32)
-        o_buf[s, 2 * SPAN :, :] = jnp.broadcast_to(row, (8, 128))
+        o_buf[PLACE[s], 2 * SPAN :, :] = jnp.broadcast_to(row, (8, 128))
     picks = pl.ds(2 * SPAN, 8)
     stores = [pltpu.make_async_copy(o_buf.at[:, picks, :], o_ref.at[:, picks, :], out_sem.at[0, steps])]
     stores[0].start()
@@ -70,7 +72,7 @@
                 vals = hadamard([x_buf[a, at, half * 128 : half * 128 + 128] * sign[a] for a in range(SLICES)])
                 to = pl.ds(pl.multiple_of(half * SPAN + k * rows + i * 8, 8), 8)
                 for s in range(SLICES):
-                    o_buf[s, to, :] = vals[s]
+                    o_buf[PLACE[s], to, :] = vals[s]
             return carry
 
         lax.fori_loop(0, rows // 8, chunk, 0, unroll=True)
@@ -107,14 +109,14 @@
 
 
 def sample_kernel(scale, half_ref, y_ref, o_ref, mixed_ref, where_ref):
-    picks = jnp.concatenate([y_ref[q, 2 * SPAN : 2 * SPAN + 1, :] for q in range(SLICES)], axis=0)
+    picks = jnp.concatenate([y_ref[PLACE[q], 2 * SPAN : 2 * SPAN + 1, :] for q in range(SLICES)], axis=0)
     where_ref[...] = picks.T.astype(jnp.int32)
 
     def chunk(i, carry):
         rows = pl.ds(pl.multiple_of(i * 8, 8), 8)
         for half in range(2):
             at = pl.ds(pl.multiple_of(half * SPAN + i * 8, 8), 8)
-            vals = hadamard([y_ref[p, at, :] for p in range(SLICES)])
+            vals = hadamard([y_ref[PLACE[p], at, :] for p in range(SLICES)])
             for q in range(SLICES):
                 mixed_ref[q, rows, half * 128 : half * 128 + 128] = vals[q] * scale
         return carry
@@ -278,7 +280,7 @@
     chip = lax.axis_index("xh") * 4 + lax.axis_index("y")
     samples = picked.shape[0] * 16
     slices = mix_slices(matrix, signs, picked)
-    slices = lax.all_to_all(slices, ROW, 0, 0, tiled=True)
+    slices = lax.all_to_all(slices, EXCHANGE, 0, 0, tiled=True)
     own = sample(slices, 1.0 / samples**0.5)
 
     up = permute(own, lambda xh, y, c, z, x: (xh, y, c, z - 1, x))

time: 144 us -> 140 us (0.972)
  starting transfers between devices: 46.8 us -> 42.3 us
    ppermute x20, starting transfers between devices: 33.2 us -> 28.8 us  [permute(): return lax.ppermute(block, NAMES, pairs)]
    ppermute x20, waiting for transfers between devices: 41.4 us -> 45.3 us  [permute(): return lax.ppermute(block, NAMES, pairs)]
    all_to_all x1, waiting for transfers between devices: 28.4 us -> 25.3 us  [shards(): slices = lax.all_to_all(slices, EXCHANGE, 0, 0, tiled=True)]
  transfers between devices with their start and end apart: 22 -> 22, of which waited for: 14 -> 17; matrix products, arithmetic and copies ran while one was open for 3% -> 3% of each run, Pallas kernels for 4% -> 5%
where the time goes in v5:
time: 140 us; the launch traced here: 139 us
  waiting for transfers between devices  77 us (55%)
  starting transfers between devices  42.3 us (30%)
  Pallas kernels  11.3 us (8%)
  other arithmetic  3.33 us (2%)
  between operations  2.87 us (2%)
  local copies, waits for them, and re-layouts  2.45 us (2%)
    ppermute x20, waiting for transfers between devices, permute(): return lax.ppermute(block, NAMES, pairs)  45.3 us
    ppermute x20, starting transfers between devices, permute(): return lax.ppermute(block, NAMES, pairs)  28.8 us
    all_to_all x1, waiting for transfers between devices, shards(): slices = lax.all_to_all(slices, EXCHANGE, 0, 0, tiled=True)  25.3 us
    all_to_all x1, starting transfers between devices, shards(): slices = lax.all_to_all(slices, EXCHANGE, 0, 0, tiled=True)  7.46 us
    pallas_call x2, Pallas kernels, call_blocks(): pl.pallas_call(kernel, out_shape=[jax.ShapeDtypeStruct((*shape, 256), F32...  6.39 us
    all_to_all x1, waiting for transfers between devices, shards(): slots = lax.all_to_all(keep + other_core(send), CHIPS, 0, 0, tiled=True)  6.37 us
    all_to_all x1, starting transfers between devices, shards(): slots = lax.all_to_all(keep + other_core(send), CHIPS, 0, 0, tiled=True)  6.08 us
    pallas_call x1, Pallas kernels, mix_slices(): pl.pallas_call(mix_kernel, out_shape=pltpu.HBM(shape, F32), in_specs=[vme...  3.51 us
  transfers between devices with their start and end apart: 22, of which 17 were waited for; matrix products, arithmetic and copies ran while one was open for 3% of the time, Pallas kernels for 5%

profile of v5, /device:TPU:6, one launch (start us, length us, event | category | flops | bytes accessed | tf_op | source)
XLA Modules:
  0.0 139.2 jit_solution(5494457972570277914)
XLA Ops:
  0.0 3.5 %mix_slices.1 = f32[16,264,128]{2,1,0:T(8,128)} custom-call(s32[16,128]{1,0:T(8,128)} %bitcast.21, s32[8,128]{1,0:T(8,128)} %bitcast.22, f32[16,128,256]{2,1,0:T(8,128)} %bitcast.20), custom_call_target="tpu_custom_call" | custom-call | tf_op jit(solution)/shard_map/mix_slices/pallas_call | solution.py:91
  3.5 7.5 %all-to-all-start = ((f32[16,264,128]{2,1,0:T(8,128)}), f32[16,264,128]{2,1,0:T(8,128)S(1)}, u32[]{:S(2)}, u32[]{:S(2)}) async-start(f32[16,264,128]{2,1,0:T(8,128)} %mix_slices.1), calls=%async_computation | async-start | bytes 4325376 | tf_op jit(solution)/shard_map/all_to_all | solution.py:283
  11.0 25.3 %all-to-all-done.refs_1_ = f32[16,264,128]{2,1,0:T(8,128)S(1)} async-done(((f32[16,264,128]{2,1,0:T(8,128)}), f32[16,264,128]{2,1,0:T(8,128)S(1)}, u32[]{:S(2)}, u32[]{:S(2)}) %all-to-all-start) | async-done | bytes 2162720 | tf_op jit(solution)/shard_map/all_to_all | solution.py:283
  36.3 1.4 sample.1.own_ref
  37.7 2.0 %collective-permute-start.2 = (f32[1024,256]{1,0:T(8,128)S(1)}, f32[1024,256]{1,0:T(8,128)S(1)}, u32[]{:S(2)}, u32[]{:S(2)}) collective-permute-start(f32[1024,256]{1,0:T(8,128)S(1)} %sample.1.own_ref), channel_id=1, source_target_pairs={{0,2},{1,3},{2,4},{3,5},{4,6},{5,7},{6,8},{7,9},{8,10},{9,11},{10,... | collective-permute-start | bytes 3145736 | tf_op jit(solution)/shard_map/ppermute | solution.py:33
  39.7 4.0 %collective-permute-start.1 = (f32[1024,256]{1,0:T(8,128)S(1)}, f32[1024,256]{1,0:T(8,128)S(1)}, u32[]{:S(2)}, u32[]{:S(2)}) collective-permute-start(f32[1024,256]{1,0:T(8,128)S(1)} %sample.1.own_ref), channel_id=1, source_target_pairs={{0,14},{1,15},{2,0},{3,1},{4,2},{5,3},{6,4},{7,5},{8,6},{9,7},{10,... | collective-permute-start | bytes 3145736 | tf_op jit(solution)/shard_map/ppermute | solution.py:33
  43.7 1.2 collective-permute-start
  44.9 21.5 %collective-permute-done.2.down_ref = f32[1024,256]{1,0:T(8,128)S(1)} collective-permute-done((f32[1024,256]{1,0:T(8,128)S(1)}, f32[1024,256]{1,0:T(8,128)S(1)}, u32[]{:S(2)}, u32[]{:S(2)}) %collective-permute-start.2) | collective-permute-done | bytes 1048608 | tf_op jit(solution)/shard_map/ppermute | solution.py:33
  66.5 3.6 %collective-permute-start.3 = (f32[1024,256]{1,0:T(8,128)S(1)}, f32[1024,256]{1,0:T(8,128)}, u32[]{:S(2)}, u32[]{:S(2)}) collective-permute-start(f32[1024,256]{1,0:T(8,128)S(1)} %collective-permute-done.2.down_ref), channel_id=1, source_target_pairs={{0,1},{1,0},{2,3},{3,2},{4,5},{5,4},{6,7},{7,6},{16,17},{17,16},{1... | collective-permute-start | bytes 3145736 | tf_op jit(solution)/shard_map/ppermute | solution.py:33
  70.0 1.5 %collective-permute-start.4 = (f32[1024,256]{1,0:T(8,128)S(1)}, f32[1024,256]{1,0:T(8,128)}, u32[]{:S(2)}, u32[]{:S(2)}) collective-permute-start(f32[1024,256]{1,0:T(8,128)S(1)} %collective-permute-done.1.up_ref), channel_id=1, source_target_pairs={{0,15},{1,14},{2,0},{3,1},{4,2},{5,3},{6,4},{7,5},{8,6},{9,7},{10,... | collective-permute-start | bytes 3145736 | tf_op jit(solution)/shard_map/ppermute | solution.py:33
  71.6 0.6 collective-permute-start.5
  72.2 2.3 %early_blocks.1 = (f32[4,192,256]{2,1,0:T(8,128)S(1)}, f32[4,192,256]{2,1,0:T(8,128)S(1)}) custom-call(s32[1]{0:T(128)} %bitcast.1.refs_0_.core_ref, f32[1024,256]{1,0:T(8,128)S(1)} %sample.1.own_ref, f32[1024,256]{1,0:T(8,128)S(1)} %collective-permute-done.beside_ref, f32[1024,256]{1,0:T(8,128)S(1)} %collective-permute-done.1.up_ref, ...), custom_call_target="tpu_custom_call" | custom-call | flops 1000 | bytes 2 | tf_op jit(solution)/shard_map/early_blocks/pallas_call | solution.py:261
  74.5 0.8 fusion.6
  75.3 0.1 copy-done.2
  75.5 0.5 collective-permute-start.10
  76.0 0.9 collective-permute-done.11
  76.9 0.1 collective-permute-start.9
  77.0 0.1 collective-permute-done.10
  77.2 0.7 copy-done.3
  77.9 0.2 collective-permute-start.8
  78.2 0.5 collective-permute-done.9
  78.7 0.8 collective-permute-done.8
  79.5 1.4 %maximum_add_fusion = f32[4,192,256]{2,1,0:T(8,128)S(1)} fusion(f32[4,192,256]{2,1,0:T(8,128)} %copy-done.2, f32[1,192,256]{2,1,0:T(8,128)S(1)} %collective-permute-done.11, f32[1,192,256]{2,1,0:T(8,128)} %copy-done.3, f32[1,192,256]{2,1,0:T(8,128)} %collective-permute-done.9, f32[1,192,256]{2,1,0:T(8,128)} %collective-permute-done.8), kind=kLoop, calls=%fused_computation | loop fusion | flops 786432 | bytes 2359296 | tf_op jit(solution)/shard_map/add | solution.py:295
  80.9 2.2 %collective-permute-start.14 = (f32[192,256]{1,0:T(8,128)S(1)}, f32[192,256]{1,0:T(8,128)S(1)}, u32[]{:S(2)}, u32[]{:S(2)}) collective-permute-start(f32[192,256]{1,0:T(8,128)S(1)} %get-tuple-element.20), channel_id=1, source_target_pairs={{0,96},{1,97},{2,98},{3,99},{4,100},{5,101},{6,102},{7,103},{8,104... | collective-permute-start | bytes 589832 | tf_op jit(solution)/shard_map/ppermute | solution.py:33
  83.1 0.8 collective-permute-start.13
  83.9 10.6 %collective-permute-done.3.down_beside_ref = f32[1024,256]{1,0:T(8,128)} collective-permute-done((f32[1024,256]{1,0:T(8,128)S(1)}, f32[1024,256]{1,0:T(8,128)}, u32[]{:S(2)}, u32[]{:S(2)}) %collective-permute-start.3) | collective-permute-done | bytes 1048608 | tf_op jit(solution)/shard_map/ppermute | solution.py:33
  94.5 0.8 collective-permute-start.12
  95.3 0.3 collective-permute-done.4.up2_ref
  95.6 2.6 %collective-permute-done.5.down2_ref = f32[1024,256]{1,0:T(8,128)} collective-permute-done((f32[1024,256]{1,0:T(8,128)S(1)}, f32[1024,256]{1,0:T(8,128)}, u32[]{:S(2)}, u32[]{:S(2)}) %collective-permute-start.5) | collective-permute-done | bytes 1048608 | tf_op jit(solution)/shard_map/ppermute | solution.py:33
  98.2 4.1 %late_blocks.1 = (f32[8,64,256]{2,1,0:T(8,128)S(1)}, f32[8,64,256]{2,1,0:T(8,128)S(1)}) custom-call(s32[2]{0:T(128)S(1)} %pad_add_fusion.flags_ref, f32[1024,256]{1,0:T(8,128)S(1)} %sample.1.own_ref, f32[1024,256]{1,0:T(8,128)S(1)} %copy-done.1, f32[1024,256]{1,0:T(8,128)S(1)} %collective-permute-done.1.up_ref, ...), custom_call_target="tpu_custom_call" | custom-call | flops 40000000000 | bytes 100000000 | tf_op jit(solution)/shard_map/late_blocks/pallas_call | solution.py:261
  102.4 0.2 collective-permute-done.12
  102.7 0.6 collective-permute-start.15
  103.3 0.9 collective-permute-done.6
  104.2 0.9 add.82
  105.1 6.1 %all-to-all-start.1 = ((f32[8,64,256]{2,1,0:T(8,128)}), f32[8,64,256]{2,1,0:T(8,128)S(1)}, u32[]{:S(2)}, u32[]{:S(2)}) async-start(f32[8,64,256]{2,1,0:T(8,128)} %add.82), calls=%async_computation.1 | async-start | bytes 1048576 | tf_op jit(solution)/shard_map/all_to_all | solution.py:317
  111.4 1.2 collective-permute-done.16
  112.5 0.2 collective-permute-start.17
  112.7 1.0 collective-permute-done.17
  113.7 6.4 %all-to-all-done.1 = f32[8,64,256]{2,1,0:T(8,128)S(1)} async-done(((f32[8,64,256]{2,1,0:T(8,128)}), f32[8,64,256]{2,1,0:T(8,128)S(1)}, u32[]{:S(2)}, u32[]{:S(2)}) %all-to-all-start.1) | async-done | bytes 524320 | tf_op jit(solution)/shard_map/all_to_all | solution.py:317
  120.2 0.1 collective-permute-start.7
  120.3 1.2 collective-permute-done.7
  121.6 5.3 %collective-permute-start.18 = (f32[128,256]{1,0:T(8,128)S(1)}, f32[128,256]{1,0:T(8,128)S(1)}, u32[]{:S(2)}, u32[]{:S(2)}) collective-permute-start(f32[128,256]{1,0:T(8,128)S(1)} %get-tuple-element.26), channel_id=1, source_target_pairs={{0,65},{1,80},{2,99},{3,114},{4,133},{5,148},{6,167},{7,182},{8,21... | collective-permute-start | bytes 393224 | tf_op jit(solution)/shard_map/ppermute | solution.py:33
  126.8 4.9 %collective-permute-start.19 = (f32[128,256]{1,0:T(8,128)S(1)}, f32[128,256]{1,0:T(8,128)S(1)}, u32[]{:S(2)}, u32[]{:S(2)}) collective-permute-start(f32[128,256]{1,0:T(8,128)S(1)} %get-tuple-element.27), channel_id=1, source_target_pairs={{0,32},{1,49},{2,66},{3,83},{4,100},{5,117},{6,134},{7,151},{8,168... | collective-permute-start | bytes 393224 | tf_op jit(solution)/shard_map/ppermute | solution.py:33
  131.7 0.6 dynamic_slice.16
  134.9 0.6 collective-permute-done.18
  135.5 2.8 %collective-permute-done.19 = f32[128,256]{1,0:T(8,128)S(1)} collective-permute-done((f32[128,256]{1,0:T(8,128)S(1)}, f32[128,256]{1,0:T(8,128)S(1)}, u32[]{:S(2)}, u32[]{:S(2)}) %collective-permute-start.19) | collective-permute-done | bytes 131104 | tf_op jit(solution)/shard_map/ppermute | solution.py:33
  138.4 0.1 copy.5
  138.5 0.7 fusion
  (32 shorter events, 0.6 us)
Async XLA Ops:
  3.5 32.8 %all-to-all-start = ((f32[16,264,128]{2,1,0:T(8,128)}), f32[16,264,128]{2,1,0:T(8,128)S(1)}, u32[]{:S(2)}, u32[]{:S(2)}) async-start(f32[16,264,128]{2,1,0:T(8,128)} %mix_slices.1), calls=%async_computation | async-start | bytes 4325376 | tf_op jit(solution)/shard_map/all_to_all | solution.py:283
  37.7 28.8 %collective-permute-start.2 = (f32[1024,256]{1,0:T(8,128)S(1)}, f32[1024,256]{1,0:T(8,128)S(1)}, u32[]{:S(2)}, u32[]{:S(2)}) collective-permute-start(f32[1024,256]{1,0:T(8,128)S(1)} %sample.1.own_ref), channel_id=1, source_target_pairs={{0,2},{1,3},{2,4},{3,5},{4,6},{5,7},{6,8},{7,9},{8,10},{9,11},{10,... | collective-permute-start | bytes 3145736 | tf_op jit(solution)/shard_map/ppermute | solution.py:33
  39.7 30.4 %collective-permute-start.1 = (f32[1024,256]{1,0:T(8,128)S(1)}, f32[1024,256]{1,0:T(8,128)S(1)}, u32[]{:S(2)}, u32[]{:S(2)}) collective-permute-start(f32[1024,256]{1,0:T(8,128)S(1)} %sample.1.own_ref), channel_id=1, source_target_pairs={{0,14},{1,15},{2,0},{3,1},{4,2},{5,3},{6,4},{7,5},{8,6},{9,7},{10,... | collective-permute-start | bytes 3145736 | tf_op jit(solution)/shard_map/ppermute | solution.py:33
  43.7 28.5 %collective-permute-start = (f32[1024,256]{1,0:T(8,128)S(1)}, f32[1024,256]{1,0:T(8,128)S(1)}, u32[]{:S(2)}, u32[]{:S(2)}) collective-permute-start(f32[1024,256]{1,0:T(8,128)S(1)} %sample.1.own_ref), channel_id=1, source_target_pairs={{0,1},{1,0},{2,3},{3,2},{4,5},{5,4},{6,7},{7,6},{8,9},{9,8},{10,11... | collective-permute-start | bytes 3145736 | tf_op jit(solution)/shard_map/ppermute | solution.py:33
  66.5 28.0 %collective-permute-start.3 = (f32[1024,256]{1,0:T(8,128)S(1)}, f32[1024,256]{1,0:T(8,128)}, u32[]{:S(2)}, u32[]{:S(2)}) collective-permute-start(f32[1024,256]{1,0:T(8,128)S(1)} %collective-permute-done.2.down_ref), channel_id=1, source_target_pairs={{0,1},{1,0},{2,3},{3,2},{4,5},{5,4},{6,7},{7,6},{16,17},{17,16},{1... | collective-permute-start | bytes 3145736 | tf_op jit(solution)/shard_map/ppermute | solution.py:33
  70.0 25.5 %collective-permute-start.4 = (f32[1024,256]{1,0:T(8,128)S(1)}, f32[1024,256]{1,0:T(8,128)}, u32[]{:S(2)}, u32[]{:S(2)}) collective-permute-start(f32[1024,256]{1,0:T(8,128)S(1)} %collective-permute-done.1.up_ref), channel_id=1, source_target_pairs={{0,15},{1,14},{2,0},{3,1},{4,2},{5,3},{6,4},{7,5},{8,6},{9,7},{10,... | collective-permute-start | bytes 3145736 | tf_op jit(solution)/shard_map/ppermute | solution.py:33
  71.6 26.6 %collective-permute-start.5 = (f32[1024,256]{1,0:T(8,128)S(1)}, f32[1024,256]{1,0:T(8,128)}, u32[]{:S(2)}, u32[]{:S(2)}) collective-permute-start(f32[1024,256]{1,0:T(8,128)S(1)} %collective-permute-done.2.down_ref), channel_id=1, source_target_pairs={{0,2},{1,3},{2,4},{3,5},{4,6},{5,7},{6,8},{7,9},{8,10},{9,11},{10,... | collective-permute-start | bytes 3145736 | tf_op jit(solution)/shard_map/ppermute | solution.py:33
  72.2 3.2 %copy-start = (f32[1024,256]{1,0:T(8,128)}, f32[1024,256]{1,0:T(8,128)S(1)}, u32[]{:S(2)}) copy-start(f32[1024,256]{1,0:T(8,128)S(1)} %collective-permute-done.beside_ref) | copy-start | bytes 3145732
  74.5 1.0 copy-start.2
  75.4 1.4 %collective-permute-start.11 = (f32[1,192,256]{2,1,0:T(8,128)S(1)}, f32[1,192,256]{2,1,0:T(8,128)S(1)}, u32[]{:S(2)}, u32[]{:S(2)}) collective-permute-start(f32[1,192,256]{2,1,0:T(8,128)S(1)} %get-tuple-element.23), channel_id=1, source_target_pairs={{0,16},{1,17},{2,18},{3,19},{4,20},{5,21},{6,22},{7,23},{8,24},{9,... | collective-permute-start | bytes 589832 | tf_op jit(solution)/shard_map/ppermute | solution.py:33
  75.5 1.7 %collective-permute-start.10 = (f32[1,192,256]{2,1,0:T(8,128)S(1)}, f32[1,192,256]{2,1,0:T(8,128)S(1)}, u32[]{:S(2)}, u32[]{:S(2)}) collective-permute-start(f32[1,192,256]{2,1,0:T(8,128)S(1)} %get-tuple-element.24), channel_id=1, source_target_pairs={{0,16},{1,17},{2,18},{3,19},{4,20},{5,21},{6,22},{7,23},{8,24},{9,... | collective-permute-start | bytes 589832 | tf_op jit(solution)/shard_map/ppermute | solution.py:33
  76.9 1.8 %collective-permute-start.9 = (f32[1,192,256]{2,1,0:T(8,128)}, f32[1,192,256]{2,1,0:T(8,128)}, u32[]{:S(2)}, u32[]{:S(2)}) collective-permute-start(f32[1,192,256]{2,1,0:T(8,128)} %get-tuple-element.25), channel_id=1, source_target_pairs={{0,16},{1,17},{2,18},{3,19},{4,20},{5,21},{6,22},{7,23},{8,24},{9,... | collective-permute-start | bytes 589832 | tf_op jit(solution)/shard_map/ppermute | solution.py:33
  77.2 0.7 copy-start.3
  77.9 1.6 %collective-permute-start.8 = (f32[1,192,256]{2,1,0:T(8,128)S(1)}, f32[1,192,256]{2,1,0:T(8,128)}, u32[]{:S(2)}, u32[]{:S(2)}) collective-permute-start(f32[1,192,256]{2,1,0:T(8,128)S(1)} %get-tuple-element.22), channel_id=1, source_target_pairs={{0,16},{1,17},{2,18},{3,19},{4,20},{5,21},{6,22},{7,23},{8,24},{9,... | collective-permute-start | bytes 589832 | tf_op jit(solution)/shard_map/ppermute | solution.py:33
  78.1 20.1 %copy-start.1 = (f32[1024,256]{1,0:T(8,128)S(1)}, f32[1024,256]{1,0:T(8,128)}, u32[]{:S(2)}) copy-start(f32[1024,256]{1,0:T(8,128)} %copy-done) | copy-start | bytes 3145732
  80.9 21.4 %collective-permute-start.14 = (f32[192,256]{1,0:T(8,128)S(1)}, f32[192,256]{1,0:T(8,128)S(1)}, u32[]{:S(2)}, u32[]{:S(2)}) collective-permute-start(f32[192,256]{1,0:T(8,128)S(1)} %get-tuple-element.20), channel_id=1, source_target_pairs={{0,96},{1,97},{2,98},{3,99},{4,100},{5,101},{6,102},{7,103},{8,104... | collective-permute-start | bytes 589832 | tf_op jit(solution)/shard_map/ppermute | solution.py:33
  83.1 19.2 %collective-permute-start.13 = (f32[192,256]{1,0:T(8,128)S(1)}, f32[192,256]{1,0:T(8,128)S(1)}, u32[]{:S(2)}, u32[]{:S(2)}) collective-permute-start(f32[192,256]{1,0:T(8,128)S(1)} %get-tuple-element.21), channel_id=1, source_target_pairs={{0,64},{1,65},{2,66},{3,67},{4,68},{5,69},{6,70},{7,71},{8,72},{9,... | collective-permute-start | bytes 589832 | tf_op jit(solution)/shard_map/ppermute | solution.py:33
  94.5 8.2 %collective-permute-start.12 = (f32[192,256]{1,0:T(8,128)S(1)}, f32[192,256]{1,0:T(8,128)S(1)}, u32[]{:S(2)}, u32[]{:S(2)}) collective-permute-start(f32[192,256]{1,0:T(8,128)S(1)} %get-tuple-element.19), channel_id=1, source_target_pairs={{0,32},{1,33},{2,34},{3,35},{4,36},{5,37},{6,38},{7,39},{8,40},{9,... | collective-permute-start | bytes 589832 | tf_op jit(solution)/shard_map/ppermute | solution.py:33
  102.3 2.0 %collective-permute-start.6 = (f32[8,64,256]{2,1,0:T(8,128)S(1)}, f32[8,64,256]{2,1,0:T(8,128)S(1)}, u32[]{:S(2)}, u32[]{:S(2)}) collective-permute-start(f32[8,64,256]{2,1,0:T(8,128)S(1)} %get-tuple-element.13), channel_id=1, source_target_pairs={{0,16},{1,17},{2,18},{3,19},{4,20},{5,21},{6,22},{7,23},{8,24},{9,... | collective-permute-start | bytes 1572872 | tf_op jit(solution)/shard_map/ppermute | solution.py:33
  102.7 8.5 %collective-permute-start.15 = (f32[128,256]{1,0:T(8,128)S(1)}, f32[128,256]{1,0:T(8,128)S(1)}, u32[]{:S(2)}, u32[]{:S(2)}) collective-permute-start(f32[128,256]{1,0:T(8,128)S(1)} %slice_select_fusion), channel_id=1, source_target_pairs={{0,128},{1,129},{2,130},{3,131},{4,132},{5,133},{6,134},{7,135},{8... | collective-permute-start | bytes 393224 | tf_op jit(solution)/shard_map/ppermute | solution.py:33
  105.1 26.6 %copy-start.4 = (s32[256]{0:T(256)S(1)}, s32[256]{0:T(256)}, u32[]{:S(2)}) copy-start(s32[256]{0:T(256)} %constant.83.clone) | copy-start | bytes 3076
  105.1 15.0 %all-to-all-start.1 = ((f32[8,64,256]{2,1,0:T(8,128)}), f32[8,64,256]{2,1,0:T(8,128)S(1)}, u32[]{:S(2)}, u32[]{:S(2)}) async-start(f32[8,64,256]{2,1,0:T(8,128)} %add.82), calls=%async_computation.1 | async-start | bytes 1048576 | tf_op jit(solution)/shard_map/all_to_all | solution.py:317
  111.2 1.3 collective-permute-start.16
  112.5 1.2 collective-permute-start.17
  120.2 1.3 collective-permute-start.7
  121.6 14.0 %collective-permute-start.18 = (f32[128,256]{1,0:T(8,128)S(1)}, f32[128,256]{1,0:T(8,128)S(1)}, u32[]{:S(2)}, u32[]{:S(2)}) collective-permute-start(f32[128,256]{1,0:T(8,128)S(1)} %get-tuple-element.26), channel_id=1, source_target_pairs={{0,65},{1,80},{2,99},{3,114},{4,133},{5,148},{6,167},{7,182},{8,21... | collective-permute-start | bytes 393224 | tf_op jit(solution)/shard_map/ppermute | solution.py:33
  126.8 11.5 %collective-permute-start.19 = (f32[128,256]{1,0:T(8,128)S(1)}, f32[128,256]{1,0:T(8,128)S(1)}, u32[]{:S(2)}, u32[]{:S(2)}) collective-permute-start(f32[128,256]{1,0:T(8,128)S(1)} %get-tuple-element.27), channel_id=1, source_target_pairs={{0,32},{1,49},{2,66},{3,83},{4,100},{5,117},{6,134},{7,151},{8,168... | collective-permute-start | bytes 393224 | tf_op jit(solution)/shard_map/ppermute | solution.py:33

commit v6 on v5

--- a/solution.py
+++ b/solution.py
@@ -264,7 +264,7 @@
         in_specs=[pl.BlockSpec(memory_space=pltpu.SMEM)] + [pl.BlockSpec(memory_space=space)] * len(operands),
         out_specs=[vmem] * 2,
         scratch_shapes=scratch,
-        compiler_params=pltpu.CompilerParams(vmem_limit_bytes=20 << 20),
+        compiler_params=pltpu.CompilerParams(vmem_limit_bytes=14 << 20),
         cost_estimate=pl.CostEstimate(flops=cost, bytes_accessed=cost // 400, transcendentals=0),
         name=name,
     )(flags, *operands)

time: 140 us -> 140 us (level)
  no operation moved by 1% of the time
where the time goes in v6:
time: 140 us; the launch traced here: 139 us
  waiting for transfers between devices  77 us (55%)
  starting transfers between devices  42.3 us (30%)
  Pallas kernels  11.3 us (8%)
  other arithmetic  3.33 us (2%)
  between operations  2.87 us (2%)
  local copies, waits for them, and re-layouts  2.45 us (2%)
    ppermute x20, waiting for transfers between devices, permute(): return lax.ppermute(block, NAMES, pairs)  45.3 us
    ppermute x20, starting transfers between devices, permute(): return lax.ppermute(block, NAMES, pairs)  28.8 us
    all_to_all x1, waiting for transfers between devices, shards(): slices = lax.all_to_all(slices, EXCHANGE, 0, 0, tiled=True)  25.3 us
    all_to_all x1, starting transfers between devices, shards(): slices = lax.all_to_all(slices, EXCHANGE, 0, 0, tiled=True)  7.46 us
    pallas_call x2, Pallas kernels, call_blocks(): pl.pallas_call(kernel, out_shape=[jax.ShapeDtypeStruct((*shape, 256), F32...  6.39 us
    all_to_all x1, waiting for transfers between devices, shards(): slots = lax.all_to_all(keep + other_core(send), CHIPS, 0, 0, tiled=True)  6.37 us
    all_to_all x1, starting transfers between devices, shards(): slots = lax.all_to_all(keep + other_core(send), CHIPS, 0, 0, tiled=True)  6.08 us
    pallas_call x1, Pallas kernels, mix_slices(): pl.pallas_call(mix_kernel, out_shape=pltpu.HBM(shape, F32), in_specs=[vme...  3.51 us
  transfers between devices with their start and end apart: 22, of which 17 were waited for; matrix products, arithmetic and copies ran while one was open for 3% of the time, Pallas kernels for 5%

profile of v6, /device:TPU:6, one launch (start us, length us, event | category | flops | bytes accessed | tf_op | source)
XLA Modules:
  0.0 139.2 jit_solution(10197180864875800244)
XLA Ops:
  0.0 3.5 %mix_slices.1 = f32[16,264,128]{2,1,0:T(8,128)} custom-call(s32[16,128]{1,0:T(8,128)} %bitcast.21, s32[8,128]{1,0:T(8,128)} %bitcast.22, f32[16,128,256]{2,1,0:T(8,128)} %bitcast.20), custom_call_target="tpu_custom_call" | custom-call | tf_op jit(solution)/shard_map/mix_slices/pallas_call | solution.py:91
  3.5 7.5 %all-to-all-start = ((f32[16,264,128]{2,1,0:T(8,128)}), f32[16,264,128]{2,1,0:T(8,128)S(1)}, u32[]{:S(2)}, u32[]{:S(2)}) async-start(f32[16,264,128]{2,1,0:T(8,128)} %mix_slices.1), calls=%async_computation | async-start | bytes 4325376 | tf_op jit(solution)/shard_map/all_to_all | solution.py:283
  11.0 25.3 %all-to-all-done.refs_1_ = f32[16,264,128]{2,1,0:T(8,128)S(1)} async-done(((f32[16,264,128]{2,1,0:T(8,128)}), f32[16,264,128]{2,1,0:T(8,128)S(1)}, u32[]{:S(2)}, u32[]{:S(2)}) %all-to-all-start) | async-done | bytes 2162720 | tf_op jit(solution)/shard_map/all_to_all | solution.py:283
  36.3 1.4 sample.1.own_ref
  37.7 2.0 %collective-permute-start.2 = (f32[1024,256]{1,0:T(8,128)S(1)}, f32[1024,256]{1,0:T(8,128)S(1)}, u32[]{:S(2)}, u32[]{:S(2)}) collective-permute-start(f32[1024,256]{1,0:T(8,128)S(1)} %sample.1.own_ref), channel_id=1, source_target_pairs={{0,2},{1,3},{2,4},{3,5},{4,6},{5,7},{6,8},{7,9},{8,10},{9,11},{10,... | collective-permute-start | bytes 3145736 | tf_op jit(solution)/shard_map/ppermute | solution.py:33
  39.7 4.0 %collective-permute-start.1 = (f32[1024,256]{1,0:T(8,128)S(1)}, f32[1024,256]{1,0:T(8,128)S(1)}, u32[]{:S(2)}, u32[]{:S(2)}) collective-permute-start(f32[1024,256]{1,0:T(8,128)S(1)} %sample.1.own_ref), channel_id=1, source_target_pairs={{0,14},{1,15},{2,0},{3,1},{4,2},{5,3},{6,4},{7,5},{8,6},{9,7},{10,... | collective-permute-start | bytes 3145736 | tf_op jit(solution)/shard_map/ppermute | solution.py:33
  43.7 1.2 collective-permute-start
  44.9 21.5 %collective-permute-done.2.down_ref = f32[1024,256]{1,0:T(8,128)S(1)} collective-permute-done((f32[1024,256]{1,0:T(8,128)S(1)}, f32[1024,256]{1,0:T(8,128)S(1)}, u32[]{:S(2)}, u32[]{:S(2)}) %collective-permute-start.2) | collective-permute-done | bytes 1048608 | tf_op jit(solution)/shard_map/ppermute | solution.py:33
  66.5 3.6 %collective-permute-start.3 = (f32[1024,256]{1,0:T(8,128)S(1)}, f32[1024,256]{1,0:T(8,128)}, u32[]{:S(2)}, u32[]{:S(2)}) collective-permute-start(f32[1024,256]{1,0:T(8,128)S(1)} %collective-permute-done.2.down_ref), channel_id=1, source_target_pairs={{0,1},{1,0},{2,3},{3,2},{4,5},{5,4},{6,7},{7,6},{16,17},{17,16},{1... | collective-permute-start | bytes 3145736 | tf_op jit(solution)/shard_map/ppermute | solution.py:33
  70.0 1.5 %collective-permute-start.4 = (f32[1024,256]{1,0:T(8,128)S(1)}, f32[1024,256]{1,0:T(8,128)}, u32[]{:S(2)}, u32[]{:S(2)}) collective-permute-start(f32[1024,256]{1,0:T(8,128)S(1)} %collective-permute-done.1.up_ref), channel_id=1, source_target_pairs={{0,15},{1,14},{2,0},{3,1},{4,2},{5,3},{6,4},{7,5},{8,6},{9,7},{10,... | collective-permute-start | bytes 3145736 | tf_op jit(solution)/shard_map/ppermute | solution.py:33
  71.6 0.6 collective-permute-start.5
  72.2 2.3 %early_blocks.1 = (f32[4,192,256]{2,1,0:T(8,128)S(1)}, f32[4,192,256]{2,1,0:T(8,128)S(1)}) custom-call(s32[1]{0:T(128)} %bitcast.1.refs_0_.core_ref, f32[1024,256]{1,0:T(8,128)S(1)} %sample.1.own_ref, f32[1024,256]{1,0:T(8,128)S(1)} %collective-permute-done.beside_ref, f32[1024,256]{1,0:T(8,128)S(1)} %collective-permute-done.1.up_ref, ...), custom_call_target="tpu_custom_call" | custom-call | flops 1000 | bytes 2 | tf_op jit(solution)/shard_map/early_blocks/pallas_call | solution.py:261
  74.5 0.8 fusion.6
  75.3 0.1 copy-done.2
  75.5 0.5 collective-permute-start.10
  76.0 0.9 collective-permute-done.11
  76.9 0.1 collective-permute-start.9
  77.0 0.1 collective-permute-done.10
  77.2 0.7 copy-done.3
  77.9 0.2 collective-permute-start.8
  78.2 0.5 collective-permute-done.9
  78.7 0.8 collective-permute-done.8
  79.5 1.4 %maximum_add_fusion = f32[4,192,256]{2,1,0:T(8,128)S(1)} fusion(f32[4,192,256]{2,1,0:T(8,128)} %copy-done.2, f32[1,192,256]{2,1,0:T(8,128)S(1)} %collective-permute-done.11, f32[1,192,256]{2,1,0:T(8,128)} %copy-done.3, f32[1,192,256]{2,1,0:T(8,128)} %collective-permute-done.9, f32[1,192,256]{2,1,0:T(8,128)} %collective-permute-done.8), kind=kLoop, calls=%fused_computation | loop fusion | flops 786432 | bytes 2359296 | tf_op jit(solution)/shard_map/add | solution.py:295
  80.9 2.2 %collective-permute-start.14 = (f32[192,256]{1,0:T(8,128)S(1)}, f32[192,256]{1,0:T(8,128)S(1)}, u32[]{:S(2)}, u32[]{:S(2)}) collective-permute-start(f32[192,256]{1,0:T(8,128)S(1)} %get-tuple-element.20), channel_id=1, source_target_pairs={{0,96},{1,97},{2,98},{3,99},{4,100},{5,101},{6,102},{7,103},{8,104... | collective-permute-start | bytes 589832 | tf_op jit(solution)/shard_map/ppermute | solution.py:33
  83.1 0.8 collective-permute-start.13
  83.9 10.6 %collective-permute-done.3.down_beside_ref = f32[1024,256]{1,0:T(8,128)} collective-permute-done((f32[1024,256]{1,0:T(8,128)S(1)}, f32[1024,256]{1,0:T(8,128)}, u32[]{:S(2)}, u32[]{:S(2)}) %collective-permute-start.3) | collective-permute-done | bytes 1048608 | tf_op jit(solution)/shard_map/ppermute | solution.py:33
  94.5 0.8 collective-permute-start.12
  95.3 0.3 collective-permute-done.4.up2_ref
  95.6 2.6 %collective-permute-done.5.down2_ref = f32[1024,256]{1,0:T(8,128)} collective-permute-done((f32[1024,256]{1,0:T(8,128)S(1)}, f32[1024,256]{1,0:T(8,128)}, u32[]{:S(2)}, u32[]{:S(2)}) %collective-permute-start.5) | collective-permute-done | bytes 1048608 | tf_op jit(solution)/shard_map/ppermute | solution.py:33
  98.2 4.1 %late_blocks.1 = (f32[8,64,256]{2,1,0:T(8,128)S(1)}, f32[8,64,256]{2,1,0:T(8,128)S(1)}) custom-call(s32[2]{0:T(128)S(1)} %pad_add_fusion.flags_ref, f32[1024,256]{1,0:T(8,128)S(1)} %sample.1.own_ref, f32[1024,256]{1,0:T(8,128)S(1)} %copy-done.1, f32[1024,256]{1,0:T(8,128)S(1)} %collective-permute-done.1.up_ref, ...), custom_call_target="tpu_custom_call" | custom-call | flops 40000000000 | bytes 100000000 | tf_op jit(solution)/shard_map/late_blocks/pallas_call | solution.py:261
  102.4 0.2 collective-permute-done.12
  102.7 0.6 collective-permute-start.15
  103.3 0.9 collective-permute-done.6
  104.2 0.9 add.82
  105.1 6.1 %all-to-all-start.1 = ((f32[8,64,256]{2,1,0:T(8,128)}), f32[8,64,256]{2,1,0:T(8,128)S(1)}, u32[]{:S(2)}, u32[]{:S(2)}) async-start(f32[8,64,256]{2,1,0:T(8,128)} %add.82), calls=%async_computation.1 | async-start | bytes 1048576 | tf_op jit(solution)/shard_map/all_to_all | solution.py:317
  111.4 1.2 collective-permute-done.16
  112.5 0.2 collective-permute-start.17
  112.7 1.0 collective-permute-done.17
  113.7 6.4 %all-to-all-done.1 = f32[8,64,256]{2,1,0:T(8,128)S(1)} async-done(((f32[8,64,256]{2,1,0:T(8,128)}), f32[8,64,256]{2,1,0:T(8,128)S(1)}, u32[]{:S(2)}, u32[]{:S(2)}) %all-to-all-start.1) | async-done | bytes 524320 | tf_op jit(solution)/shard_map/all_to_all | solution.py:317
  120.2 0.1 collective-permute-start.7
  120.3 1.2 collective-permute-done.7
  121.6 5.3 %collective-permute-start.18 = (f32[128,256]{1,0:T(8,128)S(1)}, f32[128,256]{1,0:T(8,128)S(1)}, u32[]{:S(2)}, u32[]{:S(2)}) collective-permute-start(f32[128,256]{1,0:T(8,128)S(1)} %get-tuple-element.26), channel_id=1, source_target_pairs={{0,65},{1,80},{2,99},{3,114},{4,133},{5,148},{6,167},{7,182},{8,21... | collective-permute-start | bytes 393224 | tf_op jit(solution)/shard_map/ppermute | solution.py:33
  126.8 4.9 %collective-permute-start.19 = (f32[128,256]{1,0:T(8,128)S(1)}, f32[128,256]{1,0:T(8,128)S(1)}, u32[]{:S(2)}, u32[]{:S(2)}) collective-permute-start(f32[128,256]{1,0:T(8,128)S(1)} %get-tuple-element.27), channel_id=1, source_target_pairs={{0,32},{1,49},{2,66},{3,83},{4,100},{5,117},{6,134},{7,151},{8,168... | collective-permute-start | bytes 393224 | tf_op jit(solution)/shard_map/ppermute | solution.py:33
  131.7 0.6 dynamic_slice.16
  134.9 0.6 collective-permute-done.18
  135.5 2.8 %collective-permute-done.19 = f32[128,256]{1,0:T(8,128)S(1)} collective-permute-done((f32[128,256]{1,0:T(8,128)S(1)}, f32[128,256]{1,0:T(8,128)S(1)}, u32[]{:S(2)}, u32[]{:S(2)}) %collective-permute-start.19) | collective-permute-done | bytes 131104 | tf_op jit(solution)/shard_map/ppermute | solution.py:33
  138.4 0.1 copy.5
  138.5 0.7 fusion
  (32 shorter events, 0.6 us)
Async XLA Ops:
  3.5 32.8 %all-to-all-start = ((f32[16,264,128]{2,1,0:T(8,128)}), f32[16,264,128]{2,1,0:T(8,128)S(1)}, u32[]{:S(2)}, u32[]{:S(2)}) async-start(f32[16,264,128]{2,1,0:T(8,128)} %mix_slices.1), calls=%async_computation | async-start | bytes 4325376 | tf_op jit(solution)/shard_map/all_to_all | solution.py:283
  37.7 28.8 %collective-permute-start.2 = (f32[1024,256]{1,0:T(8,128)S(1)}, f32[1024,256]{1,0:T(8,128)S(1)}, u32[]{:S(2)}, u32[]{:S(2)}) collective-permute-start(f32[1024,256]{1,0:T(8,128)S(1)} %sample.1.own_ref), channel_id=1, source_target_pairs={{0,2},{1,3},{2,4},{3,5},{4,6},{5,7},{6,8},{7,9},{8,10},{9,11},{10,... | collective-permute-start | bytes 3145736 | tf_op jit(solution)/shard_map/ppermute | solution.py:33
  39.7 30.4 %collective-permute-start.1 = (f32[1024,256]{1,0:T(8,128)S(1)}, f32[1024,256]{1,0:T(8,128)S(1)}, u32[]{:S(2)}, u32[]{:S(2)}) collective-permute-start(f32[1024,256]{1,0:T(8,128)S(1)} %sample.1.own_ref), channel_id=1, source_target_pairs={{0,14},{1,15},{2,0},{3,1},{4,2},{5,3},{6,4},{7,5},{8,6},{9,7},{10,... | collective-permute-start | bytes 3145736 | tf_op jit(solution)/shard_map/ppermute | solution.py:33
  43.7 28.5 %collective-permute-start = (f32[1024,256]{1,0:T(8,128)S(1)}, f32[1024,256]{1,0:T(8,128)S(1)}, u32[]{:S(2)}, u32[]{:S(2)}) collective-permute-start(f32[1024,256]{1,0:T(8,128)S(1)} %sample.1.own_ref), channel_id=1, source_target_pairs={{0,1},{1,0},{2,3},{3,2},{4,5},{5,4},{6,7},{7,6},{8,9},{9,8},{10,11... | collective-permute-start | bytes 3145736 | tf_op jit(solution)/shard_map/ppermute | solution.py:33
  66.5 28.0 %collective-permute-start.3 = (f32[1024,256]{1,0:T(8,128)S(1)}, f32[1024,256]{1,0:T(8,128)}, u32[]{:S(2)}, u32[]{:S(2)}) collective-permute-start(f32[1024,256]{1,0:T(8,128)S(1)} %collective-permute-done.2.down_ref), channel_id=1, source_target_pairs={{0,1},{1,0},{2,3},{3,2},{4,5},{5,4},{6,7},{7,6},{16,17},{17,16},{1... | collective-permute-start | bytes 3145736 | tf_op jit(solution)/shard_map/ppermute | solution.py:33
  70.0 25.5 %collective-permute-start.4 = (f32[1024,256]{1,0:T(8,128)S(1)}, f32[1024,256]{1,0:T(8,128)}, u32[]{:S(2)}, u32[]{:S(2)}) collective-permute-start(f32[1024,256]{1,0:T(8,128)S(1)} %collective-permute-done.1.up_ref), channel_id=1, source_target_pairs={{0,15},{1,14},{2,0},{3,1},{4,2},{5,3},{6,4},{7,5},{8,6},{9,7},{10,... | collective-permute-start | bytes 3145736 | tf_op jit(solution)/shard_map/ppermute | solution.py:33
  71.6 26.6 %collective-permute-start.5 = (f32[1024,256]{1,0:T(8,128)S(1)}, f32[1024,256]{1,0:T(8,128)}, u32[]{:S(2)}, u32[]{:S(2)}) collective-permute-start(f32[1024,256]{1,0:T(8,128)S(1)} %collective-permute-done.2.down_ref), channel_id=1, source_target_pairs={{0,2},{1,3},{2,4},{3,5},{4,6},{5,7},{6,8},{7,9},{8,10},{9,11},{10,... | collective-permute-start | bytes 3145736 | tf_op jit(solution)/shard_map/ppermute | solution.py:33
  72.2 3.2 %copy-start = (f32[1024,256]{1,0:T(8,128)}, f32[1024,256]{1,0:T(8,128)S(1)}, u32[]{:S(2)}) copy-start(f32[1024,256]{1,0:T(8,128)S(1)} %collective-permute-done.beside_ref) | copy-start | bytes 3145732
  74.5 1.0 copy-start.2
  75.4 1.4 %collective-permute-start.11 = (f32[1,192,256]{2,1,0:T(8,128)S(1)}, f32[1,192,256]{2,1,0:T(8,128)S(1)}, u32[]{:S(2)}, u32[]{:S(2)}) collective-permute-start(f32[1,192,256]{2,1,0:T(8,128)S(1)} %get-tuple-element.23), channel_id=1, source_target_pairs={{0,16},{1,17},{2,18},{3,19},{4,20},{5,21},{6,22},{7,23},{8,24},{9,... | collective-permute-start | bytes 589832 | tf_op jit(solution)/shard_map/ppermute | solution.py:33
  75.5 1.7 %collective-permute-start.10 = (f32[1,192,256]{2,1,0:T(8,128)S(1)}, f32[1,192,256]{2,1,0:T(8,128)S(1)}, u32[]{:S(2)}, u32[]{:S(2)}) collective-permute-start(f32[1,192,256]{2,1,0:T(8,128)S(1)} %get-tuple-element.24), channel_id=1, source_target_pairs={{0,16},{1,17},{2,18},{3,19},{4,20},{5,21},{6,22},{7,23},{8,24},{9,... | collective-permute-start | bytes 589832 | tf_op jit(solution)/shard_map/ppermute | solution.py:33
  76.9 1.8 %collective-permute-start.9 = (f32[1,192,256]{2,1,0:T(8,128)}, f32[1,192,256]{2,1,0:T(8,128)}, u32[]{:S(2)}, u32[]{:S(2)}) collective-permute-start(f32[1,192,256]{2,1,0:T(8,128)} %get-tuple-element.25), channel_id=1, source_target_pairs={{0,16},{1,17},{2,18},{3,19},{4,20},{5,21},{6,22},{7,23},{8,24},{9,... | collective-permute-start | bytes 589832 | tf_op jit(solution)/shard_map/ppermute | solution.py:33
  77.2 0.7 copy-start.3
  77.9 1.6 %collective-permute-start.8 = (f32[1,192,256]{2,1,0:T(8,128)S(1)}, f32[1,192,256]{2,1,0:T(8,128)}, u32[]{:S(2)}, u32[]{:S(2)}) collective-permute-start(f32[1,192,256]{2,1,0:T(8,128)S(1)} %get-tuple-element.22), channel_id=1, source_target_pairs={{0,16},{1,17},{2,18},{3,19},{4,20},{5,21},{6,22},{7,23},{8,24},{9,... | collective-permute-start | bytes 589832 | tf_op jit(solution)/shard_map/ppermute | solution.py:33
  78.1 20.1 %copy-start.1 = (f32[1024,256]{1,0:T(8,128)S(1)}, f32[1024,256]{1,0:T(8,128)}, u32[]{:S(2)}) copy-start(f32[1024,256]{1,0:T(8,128)} %copy-done) | copy-start | bytes 3145732
  80.9 21.4 %collective-permute-start.14 = (f32[192,256]{1,0:T(8,128)S(1)}, f32[192,256]{1,0:T(8,128)S(1)}, u32[]{:S(2)}, u32[]{:S(2)}) collective-permute-start(f32[192,256]{1,0:T(8,128)S(1)} %get-tuple-element.20), channel_id=1, source_target_pairs={{0,96},{1,97},{2,98},{3,99},{4,100},{5,101},{6,102},{7,103},{8,104... | collective-permute-start | bytes 589832 | tf_op jit(solution)/shard_map/ppermute | solution.py:33
  83.1 19.2 %collective-permute-start.13 = (f32[192,256]{1,0:T(8,128)S(1)}, f32[192,256]{1,0:T(8,128)S(1)}, u32[]{:S(2)}, u32[]{:S(2)}) collective-permute-start(f32[192,256]{1,0:T(8,128)S(1)} %get-tuple-element.21), channel_id=1, source_target_pairs={{0,64},{1,65},{2,66},{3,67},{4,68},{5,69},{6,70},{7,71},{8,72},{9,... | collective-permute-start | bytes 589832 | tf_op jit(solution)/shard_map/ppermute | solution.py:33
  94.5 8.2 %collective-permute-start.12 = (f32[192,256]{1,0:T(8,128)S(1)}, f32[192,256]{1,0:T(8,128)S(1)}, u32[]{:S(2)}, u32[]{:S(2)}) collective-permute-start(f32[192,256]{1,0:T(8,128)S(1)} %get-tuple-element.19), channel_id=1, source_target_pairs={{0,32},{1,33},{2,34},{3,35},{4,36},{5,37},{6,38},{7,39},{8,40},{9,... | collective-permute-start | bytes 589832 | tf_op jit(solution)/shard_map/ppermute | solution.py:33
  102.3 2.0 %collective-permute-start.6 = (f32[8,64,256]{2,1,0:T(8,128)S(1)}, f32[8,64,256]{2,1,0:T(8,128)S(1)}, u32[]{:S(2)}, u32[]{:S(2)}) collective-permute-start(f32[8,64,256]{2,1,0:T(8,128)S(1)} %get-tuple-element.13), channel_id=1, source_target_pairs={{0,16},{1,17},{2,18},{3,19},{4,20},{5,21},{6,22},{7,23},{8,24},{9,... | collective-permute-start | bytes 1572872 | tf_op jit(solution)/shard_map/ppermute | solution.py:33
  102.7 8.5 %collective-permute-start.15 = (f32[128,256]{1,0:T(8,128)S(1)}, f32[128,256]{1,0:T(8,128)S(1)}, u32[]{:S(2)}, u32[]{:S(2)}) collective-permute-start(f32[128,256]{1,0:T(8,128)S(1)} %slice_select_fusion), channel_id=1, source_target_pairs={{0,128},{1,129},{2,130},{3,131},{4,132},{5,133},{6,134},{7,135},{8... | collective-permute-start | bytes 393224 | tf_op jit(solution)/shard_map/ppermute | solution.py:33
  105.1 26.6 %copy-start.4 = (s32[256]{0:T(256)S(1)}, s32[256]{0:T(256)}, u32[]{:S(2)}) copy-start(s32[256]{0:T(256)} %constant.83.clone) | copy-start | bytes 3076
  105.1 15.0 %all-to-all-start.1 = ((f32[8,64,256]{2,1,0:T(8,128)}), f32[8,64,256]{2,1,0:T(8,128)S(1)}, u32[]{:S(2)}, u32[]{:S(2)}) async-start(f32[8,64,256]{2,1,0:T(8,128)} %add.82), calls=%async_computation.1 | async-start | bytes 1048576 | tf_op jit(solution)/shard_map/all_to_all | solution.py:317
  111.2 1.3 collective-permute-start.16
  112.5 1.2 collective-permute-start.17
  120.2 1.3 collective-permute-start.7
  121.6 14.0 %collective-permute-start.18 = (f32[128,256]{1,0:T(8,128)S(1)}, f32[128,256]{1,0:T(8,128)S(1)}, u32[]{:S(2)}, u32[]{:S(2)}) collective-permute-start(f32[128,256]{1,0:T(8,128)S(1)} %get-tuple-element.26), channel_id=1, source_target_pairs={{0,65},{1,80},{2,99},{3,114},{4,133},{5,148},{6,167},{7,182},{8,21... | collective-permute-start | bytes 393224 | tf_op jit(solution)/shard_map/ppermute | solution.py:33
  126.8 11.5 %collective-permute-start.19 = (f32[128,256]{1,0:T(8,128)S(1)}, f32[128,256]{1,0:T(8,128)S(1)}, u32[]{:S(2)}, u32[]{:S(2)}) collective-permute-start(f32[128,256]{1,0:T(8,128)S(1)} %get-tuple-element.27), channel_id=1, source_target_pairs={{0,32},{1,49},{2,66},{3,83},{4,100},{5,117},{6,134},{7,151},{8,168... | collective-permute-start | bytes 393224 | tf_op jit(solution)/shard_map/ppermute | solution.py:33
